TPU v7x, 128 devices: a whole 4x4x4 slice. The times are simulated.
128 devices in a mesh: sky: 16 (over y, x), tm: 4 (over z), fov: 2 (over core).
Axes of the slice: x: 4, y: 4, z: 4, core: 2. Of those that a mesh axis runs over, the one named last changes fastest.
Arguments:
- src_partials: float32 [262144, 5, 128], P(('sky', 'tm', 'fov')), may hold values from -0.375 to 0.375
- att_partials: float32 [262144, 4, 128], P(('sky', 'tm', 'fov')), may hold values from -0.3 to 0.3
- cal_partials: float32 [262144, 128], P(('sky', 'tm', 'fov')), may hold values from -0.6 to 0.6
- obs_phase: float32 [262144, 128], P(('sky', 'tm', 'fov')), may hold values from 0 to 1
- obs_residual: float32 [262144, 128], P(('sky', 'tm', 'fov')), may hold values from -6 to 6
- block_source: int32 [262144], P(('sky', 'tm', 'fov')), may hold values from 0 to 4095
- block_segment: int32 [262144], P(('sky', 'tm', 'fov')), may hold values from 0 to 2047, as said below
- block_unit: int32 [262144], P(('sky', 'tm', 'fov')), may hold values from 0 to 524287, as said below
- live_blocks: int32 [128], P(('sky', 'tm', 'fov')), may hold values from 608 to 2048, as said below
Outputs:
- src_update: float32 [5, 65536], P(None, 'sky')
- att_update: float32 [4, 4, 2048], P(None, 'tm', 'sky')
- cal_update: float32 [524288], P(('sky', 'tm', 'fov'))
Inputs may be any that keep to these rules, and one draw needn't show every extreme that they name: `block_segment`: only live blocks' segments matter. Of one device's live blocks at most 128 have segments of one sky index (s * 128 to (s + 1) * 128 - 1); for every tm and fov index some sky index s has exactly 128 such live blocks from every device of that tm and fov index. A device's live blocks are its first live_blocks blocks. `block_unit`: units fall into 128 ranges of 524288 / 128 units each (range r is the units of output shard r). Of one device's blocks, live or not, at most 32 have units of one range; on every device some range has exactly 32.
All inputs are finite; a program needn't handle non-finite values.
Results may differ from a plain program's by a relative error of at most 0.00011.
Values sent between devices are 32-bit elements; how exact they have to be, the bound alone decides.
No kernel may reach another device: no remote copies, remote signals or barrier semaphores. Data moves between devices by JAX's collectives and lax.ppermute only.
A program may use at most 128 MiB of HBM per device.

v0:
```python
import jax
import jax.numpy as jnp
from jax import lax
from jax.experimental import pallas as pl
from jax.experimental.pallas import tpu as pltpu
from jax.sharding import PartitionSpec as P

BLK = 2048
NB = 256
STEPS = BLK // NB
OBS = 128
CAP = 32
RANGES = 128
SHARE = 4096
PIECES = 9
F32 = jnp.float32
BF16 = jnp.bfloat16
ALL = ("sky", "tm", "fov")

index_pairs = [(i, j) for i in range(5) for j in range(i, 5)]


def split_parts(x, count):
    parts = []
    for _ in range(count - 1):
        part = x.astype(BF16)
        parts.append(part)
        x = x - part.astype(F32)
    parts.append(x.astype(BF16))
    return parts


def dot_nt(a, b):
    return lax.dot_general(a, b, (((1,), (1,)), ((), ())), preferred_element_type=F32)


def dot_nn(a, b):
    return lax.dot_general(a, b, (((1,), (0,)), ((), ())), preferred_element_type=F32)


def rows_equal(count, row, dtype=F32):
    iota = lax.broadcasted_iota(jnp.int32, (count, row.shape[1]), 0)
    return jnp.where(iota == row, 1.0, 0.0).astype(dtype)


def accumulate(ref, product, step):
    @pl.when(step == 0)
    def _():
        ref[...] = product

    @pl.when(step > 0)
    def _():
        ref[...] += product


def live_row(info_ref, step):
    position = step * NB + lax.broadcasted_iota(jnp.int32, (1, NB), 1)
    return jnp.where(position < info_ref[0], 1.0, 0.0)


def column_sum(x):
    return jnp.sum(x, axis=0, keepdims=True)


def spline_basis(phase):
    rest = 1.0 - phase
    square = phase * phase
    cubed = square * phase
    half = 0.5 * cubed
    return (
        rest * rest * rest * (1.0 / 6.0),
        half - square + (2.0 / 3.0),
        0.5 * (square + phase) - half + (1.0 / 6.0),
        cubed * (1.0 / 6.0),
    )


def normals_kernel(info_ref, src_ref, res_ref, idx_ref, keep_ref, send_ref, srct_ref, acc_ref):
    step = pl.program_id(0)
    for i in range(5):
        srct_ref[i] = src_ref[i].T
    srct_ref[5] = res_ref[...].T
    idx = idx_ref[0] ^ (info_ref[1] * 2048)
    high = rows_equal(16, idx >> 8) * live_row(info_ref, step)
    low = rows_equal(256, idx & 255, BF16)
    halves = []
    for h in range(NB // 128):
        lanes = slice(h * 128, (h + 1) * 128)
        sums = [None] * 20
        for o in range(OBS // 8):
            rows = [srct_ref[i, o * 8 : o * 8 + 8, lanes] for i in range(6)]
            terms = [rows[i] * rows[j] for i, j in index_pairs] + [rows[i] * rows[5] for i in range(5)]
            sums = terms if o == 0 else [s + t for s, t in zip(sums, terms)]
        halves.append([column_sum(s) for s in sums])
    pieces = []
    for k in range(20):
        row = jnp.concatenate([half[k] for half in halves], axis=1)
        pieces.append(high * row)
    stacked = jnp.concatenate(pieces, axis=0)
    left = jnp.concatenate(split_parts(stacked, 3), axis=0)
    accumulate(acc_ref, dot_nt(left, low), step)

    @pl.when(step == STEPS - 1)
    def _():
        for k in range(20):
            total = (
                acc_ref[k * 16 : k * 16 + 16]
                + acc_ref[320 + k * 16 : 320 + k * 16 + 16]
                + acc_ref[640 + k * 16 : 640 + k * 16 + 16]
            )
            keep_ref[k] = total[:8]
            send_ref[k] = total[8:]


def shifted(rows, distance):
    if distance == 0:
        return rows
    moved = pltpu.roll(rows, distance, 1)
    below = pltpu.roll(moved, 1, 0)
    row = lax.broadcasted_iota(jnp.int32, rows.shape, 0)
    lane = lax.broadcasted_iota(jnp.int32, rows.shape, 1)
    return jnp.where(lane >= distance, moved, jnp.where(row > 0, below, 0.0))


def knots_of(acc_ref, c):
    total = None
    for j in range(4):
        start = (j * 4 + c) * 8
        part = acc_ref[start : start + 8] + acc_ref[128 + start : 128 + start + 8]
        part = shifted(part, j)
        total = part if total is None else total + part
    return total


def diag_kernel(
    info_ref, att_ref, pha_ref, cal_ref, seg_ref, unit_ref,
    extra_ref, rank_ref, knots_ref, slots_ref, acc_ref, slot_ref, carry_ref,
):
    step = pl.program_id(0)
    live = live_row(info_ref, step)
    for c in range(4):
        for h in range(NB // 128):
            rows = att_ref[pl.ds(h * 512 + c, 128, stride=4), :]
            extra_ref[c, :, h * 128 : (h + 1) * 128] = rows.T
    extra_ref[4] = pha_ref[...].T
    extra_ref[5] = cal_ref[...].T
    seg = seg_ref[0]
    seg_high = rows_equal(8, seg >> 8) * live
    seg_low = rows_equal(256, seg & 255, BF16)
    halves = []
    for h in range(NB // 128):
        lanes = slice(h * 128, (h + 1) * 128)
        sums = [None] * 17
        for o in range(OBS // 8):
            rows = [extra_ref[i, o * 8 : o * 8 + 8, lanes] for i in range(6)]
            basis = [b * b for b in spline_basis(rows[4])]
            squares = [rows[c] * rows[c] for c in range(4)]
            terms = [b * s for b in basis for s in squares] + [rows[5] * rows[5]]
            sums = terms if o == 0 else [s + t for s, t in zip(sums, terms)]
        halves.append([column_sum(s) for s in sums])
    sums = [jnp.concatenate([half[k] for half in halves], axis=1) for k in range(17)]
    stacked = jnp.concatenate([seg_high * sums[k] for k in range(16)], axis=0)
    accumulate(acc_ref, dot_nt(jnp.concatenate(split_parts(stacked, 2), axis=0), seg_low), step)

    unit = unit_ref[0]
    owner = rows_equal(RANGES, unit >> 12)
    owner_low = owner.astype(BF16)
    before = lax.broadcasted_iota(jnp.int32, (NB, NB), 0) < lax.broadcasted_iota(jnp.int32, (NB, NB), 1)
    before = jnp.where(before, 1.0, 0.0).astype(BF16)
    earlier = dot_nn(owner_low, before) + jnp.where(step > 0, carry_ref[...], 0.0)
    rank = column_sum(owner * earlier)
    accumulate(carry_ref, dot_nn(owner_low, jnp.ones((NB, NB), BF16)), step)
    rank = rank.astype(jnp.int32)
    rank_ref[0] = rank
    place = rows_equal(CAP, rank)
    inner = (unit & (SHARE - 1)).astype(F32)
    stacked = jnp.concatenate([place * (sums[16] * live), place * inner], axis=0)
    accumulate(slot_ref, dot_nt(jnp.concatenate(split_parts(stacked, 2), axis=0), owner_low), step)

    @pl.when(step == STEPS - 1)
    def _():
        for c in range(4):
            knots_ref[c] = knots_of(acc_ref, c)
        slots_ref[...] = slot_ref[:64] + slot_ref[64:]


def solve_kernel(a_ref, b_ref, c_ref, d_ref, out_ref):
    packed = [(a_ref[k] + c_ref[k]) + (b_ref[k] + d_ref[k]) for k in range(20)]
    matrix = {}
    for position, (i, j) in enumerate(index_pairs):
        matrix[i, j] = packed[position] + (1.0 if i == j else 0.0)
    factor = {}
    inverse = {}
    for i in range(5):
        for j in range(i + 1):
            running = matrix[j, i]
            for k in range(j):
                running = running - factor[i, k] * factor[j, k]
            if i == j:
                inverse[i] = 1.0 / jnp.sqrt(running)
            else:
                factor[i, j] = running * inverse[j]
    forward = []
    for i in range(5):
        running = packed[15 + i]
        for k in range(i):
            running = running - factor[i, k] * forward[k]
        forward.append(running * inverse[i])
    result = [None] * 5
    for i in reversed(range(5)):
        running = forward[i]
        for k in range(i + 1, 5):
            running = running - factor[k, i] * result[k]
        result[i] = running * inverse[i]
        out_ref[i] = result[i]


def apply_kernel(
    info_ref, srct_ref, extra_ref, idx_ref, seg_ref, unit_ref, rank_ref, mine_ref, other_ref,
    diag_ref, slots_ref, out_ref, update_ref, table_ref, acc_ref, slot_ref,
):
    step = pl.program_id(0)
    fov = info_ref[1]

    @pl.when(step == 0)
    def _():
        out_ref[...] = jnp.zeros_like(out_ref)
        pieces = []
        for k in range(5):
            mine = mine_ref[k]
            other = other_ref[k]
            pieces += [mine, other]
            first = jnp.where(fov == 0, mine, other)
            second = jnp.where(fov == 0, other, mine)
            for q in range(8):
                update_ref[k : k + 1, q * 256 : (q + 1) * 256] = first[q : q + 1]
                update_ref[k : k + 1, 2048 + q * 256 : 2048 + (q + 1) * 256] = second[q : q + 1]
        stacked = jnp.concatenate(pieces, axis=0)
        table_ref[...] = jnp.concatenate(split_parts(stacked, 3), axis=0)

    live = live_row(info_ref, step)
    idx = idx_ref[0] ^ (fov * 2048)
    high = rows_equal(16, idx >> 8)
    low = rows_equal(256, idx & 255, BF16)
    looked = dot_nn(table_ref[...], low)
    looked = looked[:80] + looked[80:160] + looked[160:240]
    chosen = [column_sum(looked[k * 16 : k * 16 + 16] * high) for k in range(5)]
    halves = []
    for h in range(NB // 128):
        lanes = slice(h * 128, (h + 1) * 128)
        spread = [jnp.broadcast_to(chosen[k][:, lanes], (8, 128)) for k in range(5)]
        sums = [None] * 17
        for o in range(OBS // 8):
            span = slice(o * 8, o * 8 + 8)
            model = srct_ref[0, span, lanes] * spread[0]
            for k in range(1, 5):
                model = model + srct_ref[k, span, lanes] * spread[k]
            residual = srct_ref[5, span, lanes] - model
            basis = spline_basis(extra_ref[4, span, lanes])
            weighted = [extra_ref[c, span, lanes] * residual for c in range(4)]
            terms = [b * w for b in basis for w in weighted] + [extra_ref[5, span, lanes] * residual]
            sums = terms if o == 0 else [s + t for s, t in zip(sums, terms)]
        halves.append([column_sum(s) for s in sums])
    sums = [jnp.concatenate([half[k] for half in halves], axis=1) for k in range(17)]
    seg = seg_ref[0]
    seg_high = rows_equal(8, seg >> 8) * live
    seg_low = rows_equal(256, seg & 255, BF16)
    stacked = jnp.concatenate([seg_high * sums[k] for k in range(16)], axis=0)
    accumulate(acc_ref, dot_nt(jnp.concatenate(split_parts(stacked, 2), axis=0), seg_low), step)
    owner = rows_equal(RANGES, unit_ref[0] >> 12, BF16)
    placed = rows_equal(CAP, rank_ref[0]) * (sums[16] * live)
    accumulate(slot_ref, dot_nt(jnp.concatenate(split_parts(placed, 2), axis=0), owner), step)

    @pl.when(step == STEPS - 1)
    def _():
        tm = info_ref[2]
        slots = jnp.concatenate(
            [slot_ref[:CAP] + slot_ref[CAP:], slots_ref[...], jnp.zeros((CAP, RANGES), F32)], axis=0
        )
        out_ref[pl.ds(0, RANGES, stride=PIECES), :] = slots.T
        for c in range(8):
            knots = knots_of(acc_ref, c) if c < 4 else diag_ref[c - 4]
            for r in range(2):
                for f in range(2):
                    start = r * 8 * PIECES + (tm * 2 + f) * PIECES + 1 + c
                    out_ref[pl.ds(start, 8, stride=16 * PIECES), :] = knots[:, r * 128 : (r + 1) * 128]


def final_kernel(info_ref, in_ref, att_ref, cal_ref, left_ref, right_ref):
    tm = info_ref[2]
    knots = None
    for s in range(16):
        for f in range(2):
            part = in_ref[pl.ds((s * 8 + tm * 2 + f) * PIECES + 1, 8), :]
            knots = part if knots is None else knots + part
    att_ref[...] = knots[:4] / (1.0 + knots[4:])
    slots = in_ref[pl.ds(0, RANGES, stride=PIECES), :].T
    unit = slots[64:96].astype(jnp.int32)
    for k in range(CAP):
        lanes = slice(k * 128, (k + 1) * 128)
        inner = unit[k : k + 1]
        right_ref[:, lanes] = rows_equal(128, inner & 127, BF16)
        high = rows_equal(32, inner >> 7)
        stacked = jnp.concatenate([high * slots[k : k + 1], high * slots[32 + k : 33 + k]], axis=0)
        left_ref[:, lanes] = jnp.concatenate(split_parts(stacked, 2), axis=0)
    sums = dot_nt(left_ref[...], right_ref[...])
    sums = sums[:64] + sums[64:]
    cal_ref[...] = sums[:32] / (1.0 + sums[32:])


SMEM = pl.BlockSpec(memory_space=pltpu.SMEM)
ROW = pl.BlockSpec((1, 1, NB), lambda s: (s, 0, 0))


def whole(shape):
    return pl.BlockSpec(shape, lambda s: (0,) * len(shape))


def shards(
    src_partials,
    att_partials,
    cal_partials,
    obs_phase,
    obs_residual,
    block_source,
    block_segment,
    block_unit,
    live_blocks,
):
    tm = lax.axis_index("tm")
    fov = lax.axis_index("fov")
    info = jnp.stack([live_blocks[0], fov.astype(jnp.int32), tm.astype(jnp.int32)])
    source = block_source.reshape(STEPS, 1, NB)
    segment = block_segment.reshape(STEPS, 1, NB)
    unit = block_unit.reshape(STEPS, 1, NB)
    src = jnp.transpose(src_partials, (1, 0, 2))
    att = att_partials.reshape(BLK * 4, OBS)
    sequential = pltpu.CompilerParams(dimension_semantics=("arbitrary",))
    keep, send, srct = pl.pallas_call(
        normals_kernel,
        grid=(STEPS,),
        in_specs=[
            SMEM,
            pl.BlockSpec((5, NB, OBS), lambda s: (0, s, 0)),
            pl.BlockSpec((NB, OBS), lambda s: (s, 0)),
            ROW,
        ],
        out_specs=[
            whole((20, 8, 256)),
            whole((20, 8, 256)),
            pl.BlockSpec((6, OBS, NB), lambda s: (0, 0, s)),
        ],
        out_shape=[
            jax.ShapeDtypeStruct((20, 8, 256), F32),
            jax.ShapeDtypeStruct((20, 8, 256), F32),
            jax.ShapeDtypeStruct((6, OBS, BLK), F32),
        ],
        scratch_shapes=[pltpu.VMEM((960, 256), F32)],
        compiler_params=sequential,
        name="normals",
    )(info, src, obs_residual, source)
    half = keep + lax.ppermute(send, "fov", [(0, 1), (1, 0)])
    half, info_later = lax.optimization_barrier((half, info))
    around = [lax.ppermute(half, "tm", [(i, (i + d) % 4) for i in range(4)]) for d in (1, 2, 3)]
    extra, rank, diag_knots, diag_slots = pl.pallas_call(
        diag_kernel,
        grid=(STEPS,),
        in_specs=[
            SMEM,
            pl.BlockSpec((NB * 4, OBS), lambda s: (s, 0)),
            pl.BlockSpec((NB, OBS), lambda s: (s, 0)),
            pl.BlockSpec((NB, OBS), lambda s: (s, 0)),
            ROW,
            ROW,
        ],
        out_specs=[
            pl.BlockSpec((6, OBS, NB), lambda s: (0, 0, s)),
            ROW,
            whole((4, 8, 256)),
            whole((64, RANGES)),
        ],
        out_shape=[
            jax.ShapeDtypeStruct((6, OBS, BLK), F32),
            jax.ShapeDtypeStruct((STEPS, 1, NB), jnp.int32),
            jax.ShapeDtypeStruct((4, 8, 256), F32),
            jax.ShapeDtypeStruct((64, RANGES), F32),
        ],
        scratch_shapes=[
            pltpu.VMEM((256, 256), F32),
            pltpu.VMEM((128, RANGES), F32),
            pltpu.VMEM((RANGES, NB), F32),
        ],
        compiler_params=sequential,
        cost_estimate=pl.CostEstimate(flops=200_000_000, bytes_accessed=12_000_000, transcendentals=0),
        name="diag",
    )(info_later, att, obs_phase, cal_partials, segment, unit)
    around, diag_knots = lax.optimization_barrier((around, diag_knots))
    mine = pl.pallas_call(
        solve_kernel,
        out_shape=jax.ShapeDtypeStruct((5, 8, 256), F32),
        name="solve",
    )(half, *around)
    other = lax.ppermute(mine, "fov", [(0, 1), (1, 0)])
    outgoing, src_update = pl.pallas_call(
        apply_kernel,
        grid=(STEPS,),
        in_specs=[
            SMEM,
            pl.BlockSpec((6, OBS, NB), lambda s: (0, 0, s)),
            pl.BlockSpec((6, OBS, NB), lambda s: (0, 0, s)),
            ROW,
            ROW,
            ROW,
            ROW,
            whole((5, 8, 256)),
            whole((5, 8, 256)),
            whole((4, 8, 256)),
            whole((64, RANGES)),
        ],
        out_specs=[whole((128 * PIECES, 128)), whole((5, 4096))],
        out_shape=[
            jax.ShapeDtypeStruct((128 * PIECES, 128), F32),
            jax.ShapeDtypeStruct((5, 4096), F32),
        ],
        scratch_shapes=[
            pltpu.VMEM((240, 256), BF16),
            pltpu.VMEM((256, 256), F32),
            pltpu.VMEM((64, RANGES), F32),
        ],
        compiler_params=sequential,
        name="apply",
    )(info, srct, extra, source, segment, unit, rank, mine, other, diag_knots, diag_slots)
    arrived = lax.all_to_all(
        outgoing.reshape(128, 1, PIECES * 128), ALL, split_axis=0, concat_axis=0, tiled=True
    ).reshape(128 * PIECES, 128)
    att_update, cal_update = pl.pallas_call(
        final_kernel,
        in_specs=[SMEM, pl.BlockSpec(memory_space=pltpu.VMEM)],
        out_shape=[
            jax.ShapeDtypeStruct((4, 128), F32),
            jax.ShapeDtypeStruct((32, 128), F32),
        ],
        scratch_shapes=[pltpu.VMEM((128, CAP * 128), BF16), pltpu.VMEM((128, CAP * 128), BF16)],
        name="final",
    )(info, arrived)
    return (src_update, att_update.reshape(4, 1, 128), cal_update.reshape(SHARE))


def solution(mesh):
    return jax.shard_map(
        shards,
        mesh=mesh,
        in_specs=(
            P(ALL, None, None),
            P(ALL, None, None),
            P(ALL, None),
            P(ALL, None),
            P(ALL, None),
            P(ALL),
            P(ALL),
            P(ALL),
            P(ALL),
        ),
        out_specs=(P(None, "sky"), P(None, "tm", "sky"), P(ALL)),
        check_vma=False,
    )
```

profile of v0, /device:TPU:1, one launch (start us, length us, event | category | flops | bytes accessed | tf_op | source)
XLA Modules:
  0.0 74.7 jit_solution(9302529907988458910)
XLA Ops:
  1.3 0.6 pad_add_fusion.info_ref
  1.9 10.1 %normals.1 = (f32[20,8,256]{2,1,0:T(8,128)}, f32[20,8,256]{2,1,0:T(8,128)}, f32[6,128,2048]{2,1,0:T(8,128)}) custom-call(s32[3]{0:T(128)} %pad_add_fusion.info_ref, f32[5,2048,128]{2,1,0:T(8,128)} %bitcast.13, f32[2048,128]{1,0:T(8,128)} %res_ref.1, s32[8,1,256]{2,1,0:T(1,128)} %bitcast.17), custom_call_target="tpu_custom_call" | custom-call | tf_op jit(solution)/shard_map/normals/pallas_call | solution.py:339
  12.0 1.4 %collective-permute-start = (f32[20,8,256]{2,1,0:T(8,128)}, f32[20,8,256]{2,1,0:T(8,128)S(1)}, u32[]{:S(2)}, u32[]{:S(2)}) collective-permute-start(f32[20,8,256]{2,1,0:T(8,128)} %get-tuple-element.22), channel_id=1, source_target_pairs={{0,1},{1,0},{2,3},{3,2},{4,5},{5,4},{6,7},{7,6},{8,9},{9,8},{10,11... | collective-permute-start | bytes 491528 | tf_op jit(solution)/shard_map/ppermute | solution.py:362
  13.3 1.2 %collective-permute-done = f32[20,8,256]{2,1,0:T(8,128)S(1)} collective-permute-done((f32[20,8,256]{2,1,0:T(8,128)}, f32[20,8,256]{2,1,0:T(8,128)S(1)}, u32[]{:S(2)}, u32[]{:S(2)}) %collective-permute-start) | collective-permute-done | bytes 163872 | tf_op jit(solution)/shard_map/ppermute | solution.py:362
  14.6 0.9 %add.3.a_ref = f32[20,8,256]{2,1,0:T(8,128)S(1)} add(f32[20,8,256]{2,1,0:T(8,128)} %get-tuple-element.21, f32[20,8,256]{2,1,0:T(8,128)S(1)} %collective-permute-done) | non-fusion elementwise | flops 40960 | bytes 491520 | tf_op jit(solution)/shard_map/add | solution.py:362
  15.5 0.0 copy-start
  15.5 3.9 %collective-permute-start.3 = (f32[20,8,256]{2,1,0:T(8,128)S(1)}, f32[20,8,256]{2,1,0:T(8,128)S(1)}, u32[]{:S(2)}, u32[]{:S(2)}) collective-permute-start(f32[20,8,256]{2,1,0:T(8,128)S(1)} %add.3.a_ref), channel_id=1, source_target_pairs={{0,6},{2,0},{4,2},{6,4},{1,7},{3,1},{5,3},{7,5},{8,14},{10,8},{12,... | collective-permute-start | bytes 491528 | tf_op jit(solution)/shard_map/ppermute | solution.py:364
  19.5 0.0 collective-permute-start.2
  19.5 0.7 collective-permute-start.1
  20.2 11.5 %diag.1 = (f32[6,128,2048]{2,1,0:T(8,128)}, s32[8,1,256]{2,1,0:T(1,128)}, f32[4,8,256]{2,1,0:T(8,128)}, f32[64,128]{1,0:T(8,128)}) custom-call(s32[3]{0:T(128)} %pad_add_fusion.info_ref, f32[8192,128]{1,0:T(8,128)} %bitcast.14, f32[2048,128]{1,0:T(8,128)} %pha_ref.1, f32[2048,128]{1,0:T(8,128)} %cal_ref.1, s32[8,1,256]{2,1,0:T(1,128)} %bitcast.19, ...), custom_call_target="tpu_custom_call" | custom-call | flops 200000000 | bytes 12000000 | tf_op jit(solution)/shard_map/diag/pallas_call | solution.py:365
  31.7 0.0 collective-permute-done.3.d_ref
  31.7 0.0 copy-start.1
  31.7 0.0 collective-permute-done.2.c_ref
  31.7 0.0 copy-start.2
  31.7 0.0 collective-permute-done.1.b_ref
  31.7 0.0 copy-start.3
  31.7 0.0 copy-done
  31.7 0.6 copy-done.1
  32.3 0.1 copy-done.2
  32.4 0.1 copy-done.3
  32.5 1.9 %solve.1.mine_ref = f32[5,8,256]{2,1,0:T(8,128)} custom-call(f32[20,8,256]{2,1,0:T(8,128)} %copy-done, f32[20,8,256]{2,1,0:T(8,128)} %copy-done.3, f32[20,8,256]{2,1,0:T(8,128)} %copy-done.2, f32[20,8,256]{2,1,0:T(8,128)} %copy-done.1), custom_call_target="tpu_custom_call" | custom-call | tf_op jit(solution)/shard_map/solve/pallas_call | solution.py:398
  34.4 1.2 %collective-permute-start.4 = (f32[5,8,256]{2,1,0:T(8,128)}, f32[5,8,256]{2,1,0:T(8,128)S(1)}, u32[]{:S(2)}, u32[]{:S(2)}) collective-permute-start(f32[5,8,256]{2,1,0:T(8,128)} %solve.1.mine_ref), channel_id=1, source_target_pairs={{0,1},{1,0},{2,3},{3,2},{4,5},{5,4},{6,7},{7,6},{8,9},{9,8},{10,11... | collective-permute-start | bytes 122888 | tf_op jit(solution)/shard_map/ppermute | solution.py:403
  35.6 1.1 %collective-permute-done.4.other_ref = f32[5,8,256]{2,1,0:T(8,128)S(1)} collective-permute-done((f32[5,8,256]{2,1,0:T(8,128)}, f32[5,8,256]{2,1,0:T(8,128)S(1)}, u32[]{:S(2)}, u32[]{:S(2)}) %collective-permute-start.4) | collective-permute-done | bytes 40992 | tf_op jit(solution)/shard_map/ppermute | solution.py:403
  36.7 0.0 copy-start.4
  36.7 0.6 copy-done.4
  37.3 11.8 %apply.1 = (f32[1152,128]{1,0:T(8,128)}, f32[5,4096]{1,0:T(8,128)}) custom-call(s32[3]{0:T(128)} %pad_add_fusion.info_ref, f32[6,128,2048]{2,1,0:T(8,128)} %get-tuple-element.20.srct_ref, f32[6,128,2048]{2,1,0:T(8,128)} %get-tuple-element.24.extra_ref, s32[8,1,256]{2,1,0:T(1,128)} %bitcast.18, s32[8,1,256]{2,1,0:T(1,128)} %bitcast.20, ...), custom_call_target="tpu_custom_call" | custom-call | tf_op jit(solution)/shard_map/apply/pallas_call | solution.py:404
  49.1 22.9 %all_to_all.5 = f32[128,1,1152]{2,1,0:T(1,128)} all-to-all(f32[128,1,1152]{2,1,0:T(1,128)} %bitcast.16), channel_id=1, replica_groups=mesh['sky'=16,'tm'=4,'fov'=2] {'sky','tm','fov'}, dimensions={0} | all-to-all | bytes 1179648 | tf_op jit(solution)/shard_map/all_to_all | solution.py:433
  72.0 2.7 %final.1 = (f32[4,128]{1,0:T(4,128)}, f32[32,128]{1,0:T(8,128)}) custom-call(s32[3]{0:T(128)} %pad_add_fusion.info_ref, f32[1152,128]{1,0:T(8,128)} %bitcast.15), custom_call_target="tpu_custom_call" | custom-call | tf_op jit(solution)/shard_map/final/pallas_call | solution.py:436
Async XLA Ops:
  12.0 2.6 %collective-permute-start = (f32[20,8,256]{2,1,0:T(8,128)}, f32[20,8,256]{2,1,0:T(8,128)S(1)}, u32[]{:S(2)}, u32[]{:S(2)}) collective-permute-start(f32[20,8,256]{2,1,0:T(8,128)} %get-tuple-element.22), channel_id=1, source_target_pairs={{0,1},{1,0},{2,3},{3,2},{4,5},{5,4},{6,7},{7,6},{8,9},{9,8},{10,11... | collective-permute-start | bytes 491528 | tf_op jit(solution)/shard_map/ppermute | solution.py:362
  15.5 16.2 %copy-start = (f32[20,8,256]{2,1,0:T(8,128)}, f32[20,8,256]{2,1,0:T(8,128)S(1)}, u32[]{:S(2)}) copy-start(f32[20,8,256]{2,1,0:T(8,128)S(1)} %add.3.a_ref) | copy-start | bytes 491524
  15.5 16.1 %collective-permute-start.3 = (f32[20,8,256]{2,1,0:T(8,128)S(1)}, f32[20,8,256]{2,1,0:T(8,128)S(1)}, u32[]{:S(2)}, u32[]{:S(2)}) collective-permute-start(f32[20,8,256]{2,1,0:T(8,128)S(1)} %add.3.a_ref), channel_id=1, source_target_pairs={{0,6},{2,0},{4,2},{6,4},{1,7},{3,1},{5,3},{7,5},{8,14},{10,8},{12,... | collective-permute-start | bytes 491528 | tf_op jit(solution)/shard_map/ppermute | solution.py:364
  19.5 12.2 %collective-permute-start.2 = (f32[20,8,256]{2,1,0:T(8,128)S(1)}, f32[20,8,256]{2,1,0:T(8,128)S(1)}, u32[]{:S(2)}, u32[]{:S(2)}) collective-permute-start(f32[20,8,256]{2,1,0:T(8,128)S(1)} %add.3.a_ref), channel_id=1, source_target_pairs={{0,4},{2,6},{4,0},{6,2},{1,5},{3,7},{5,1},{7,3},{8,12},{10,14},{12... | collective-permute-start | bytes 491528 | tf_op jit(solution)/shard_map/ppermute | solution.py:364
  19.5 12.2 %collective-permute-start.1 = (f32[20,8,256]{2,1,0:T(8,128)S(1)}, f32[20,8,256]{2,1,0:T(8,128)S(1)}, u32[]{:S(2)}, u32[]{:S(2)}) collective-permute-start(f32[20,8,256]{2,1,0:T(8,128)S(1)} %add.3.a_ref), channel_id=1, source_target_pairs={{0,2},{2,4},{4,6},{6,0},{1,3},{3,5},{5,7},{7,1},{8,10},{10,12},{12... | collective-permute-start | bytes 491528 | tf_op jit(solution)/shard_map/ppermute | solution.py:364
  31.7 0.7 copy-start.1
  31.7 0.7 copy-start.2
  31.7 0.8 %copy-start.3 = (f32[20,8,256]{2,1,0:T(8,128)}, f32[20,8,256]{2,1,0:T(8,128)S(1)}, u32[]{:S(2)}) copy-start(f32[20,8,256]{2,1,0:T(8,128)S(1)} %collective-permute-done.1.b_ref) | copy-start | bytes 491524
  34.4 2.3 %collective-permute-start.4 = (f32[5,8,256]{2,1,0:T(8,128)}, f32[5,8,256]{2,1,0:T(8,128)S(1)}, u32[]{:S(2)}, u32[]{:S(2)}) collective-permute-start(f32[5,8,256]{2,1,0:T(8,128)} %solve.1.mine_ref), channel_id=1, source_target_pairs={{0,1},{1,0},{2,3},{3,2},{4,5},{5,4},{6,7},{7,6},{8,9},{9,8},{10,11... | collective-permute-start | bytes 122888 | tf_op jit(solution)/shard_map/ppermute | solution.py:403
  36.7 0.6 copy-start.4
where the time goes:
time: 75.5 us; the launch traced here: 74.7 us
  Pallas kernels  37.9 us (50%)
  blocking collectives  22.9 us (30%)
  starting transfers between devices  7.23 us (10%)
  waiting for transfers between devices  2.33 us (3%)
  other arithmetic  1.55 us (2%)
  local copies, waits for them, and re-layouts  1.39 us (2%)
  between operations  1.35 us (2%)
    all_to_all x1, blocking collectives, shards(): lax.all_to_all(outgoing.reshape(128, 1, PIECES * 128), ALL, split_axis=0,...  22.9 us
    pallas_call x1, Pallas kernels, shards(): pl.pallas_call(apply_kernel, grid=(STEPS,), in_specs=[SMEM, pl.BlockSpec(...  11.8 us
    pallas_call x1, Pallas kernels, shards(): pl.pallas_call(diag_kernel, grid=(STEPS,), in_specs=[SMEM, pl.BlockSpec((...  11.5 us
    pallas_call x1, Pallas kernels, shards(): pl.pallas_call(normals_kernel, grid=(STEPS,), in_specs=[SMEM, pl.BlockSpe...  10.1 us
    ppermute x3, starting transfers between devices, shards(): lax.ppermute(half, 'tm', [(i, (i + d) % 4) for i in range(4)])  4.64 us
    pallas_call x1, Pallas kernels, shards(): pl.pallas_call(final_kernel, in_specs=[SMEM, pl.BlockSpec(memory_space=pl...  2.73 us
    pallas_call x1, Pallas kernels, shards(): pl.pallas_call(solve_kernel, out_shape=jax.ShapeDtypeStruct((5, 8, 256),...  1.89 us
  transfers between devices with their start and end apart: 5, of which 2 were waited for; matrix products, arithmetic and copies ran while one was open for 0% of the time, Pallas kernels for 15%

commit v1 on v0

--- a/solution.py
+++ b/solution.py
@@ -12,7 +12,7 @@
 CAP = 32
 RANGES = 128
 SHARE = 4096
-PIECES = 9
+PIECES = 5
 F32 = jnp.float32
 BF16 = jnp.bfloat16
 ALL = ("sky", "tm", "fov")
@@ -38,9 +38,21 @@
     return lax.dot_general(a, b, (((1,), (0,)), ((), ())), preferred_element_type=F32)
 
 
-def rows_equal(count, row, dtype=F32):
+def packed_dot(left, right, count):
+    return dot_nt(
+        jnp.concatenate(split_parts(left, count), axis=1), jnp.concatenate([right] * count, axis=1)
+    )
+
+
+def rows_equal(count, row):
     iota = lax.broadcasted_iota(jnp.int32, (count, row.shape[1]), 0)
-    return jnp.where(iota == row, 1.0, 0.0).astype(dtype)
+    return jnp.where(iota == row, 1.0, 0.0)
+
+
+def narrow_rows_equal(count, row):
+    iota = lax.broadcasted_iota(jnp.int32, (count, row.shape[1]), 0).astype(F32).astype(BF16)
+    wide = jnp.broadcast_to(row.astype(F32), (count, row.shape[1])).astype(BF16)
+    return jnp.where(iota == wide, jnp.ones((), BF16), jnp.zeros((), BF16))
 
 
 def accumulate(ref, product, step):
@@ -53,9 +65,9 @@
         ref[...] += product
 
 
-def live_row(info_ref, step):
+def live_row(live_ref, step):
     position = step * NB + lax.broadcasted_iota(jnp.int32, (1, NB), 1)
-    return jnp.where(position < info_ref[0], 1.0, 0.0)
+    return jnp.where(position < live_ref[0], 1.0, 0.0)
 
 
 def column_sum(x):
@@ -75,14 +87,25 @@
     )
 
 
-def normals_kernel(info_ref, src_ref, res_ref, idx_ref, keep_ref, send_ref, srct_ref, acc_ref):
+def spline_from_moments(m, j):
+    sixth = 1.0 / 6.0
+    if j == 0:
+        return (m[0] - m[3]) * sixth + 0.5 * (m[2] - m[1])
+    if j == 1:
+        return m[0] * (2.0 / 3.0) - m[2] + 0.5 * m[3]
+    if j == 2:
+        return m[0] * sixth + 0.5 * (m[1] + m[2] - m[3])
+    return m[3] * sixth
+
+
+def normals_kernel(live_ref, src_ref, res_ref, idx_ref, keep_ref, send_ref, srct_ref, acc_ref):
     step = pl.program_id(0)
     for i in range(5):
         srct_ref[i] = src_ref[i].T
     srct_ref[5] = res_ref[...].T
-    idx = idx_ref[0] ^ (info_ref[1] * 2048)
-    high = rows_equal(16, idx >> 8) * live_row(info_ref, step)
-    low = rows_equal(256, idx & 255, BF16)
+    idx = idx_ref[0] ^ (lax.axis_index("fov") * 2048)
+    high = rows_equal(16, idx >> 8) * live_row(live_ref, step)
+    low = narrow_rows_equal(256, idx & 255)
     halves = []
     for h in range(NB // 128):
         lanes = slice(h * 128, (h + 1) * 128)
@@ -97,24 +120,16 @@
         row = jnp.concatenate([half[k] for half in halves], axis=1)
         pieces.append(high * row)
     stacked = jnp.concatenate(pieces, axis=0)
-    left = jnp.concatenate(split_parts(stacked, 3), axis=0)
-    accumulate(acc_ref, dot_nt(left, low), step)
+    accumulate(acc_ref, packed_dot(stacked, low, 3), step)
 
     @pl.when(step == STEPS - 1)
     def _():
         for k in range(20):
-            total = (
-                acc_ref[k * 16 : k * 16 + 16]
-                + acc_ref[320 + k * 16 : 320 + k * 16 + 16]
-                + acc_ref[640 + k * 16 : 640 + k * 16 + 16]
-            )
-            keep_ref[k] = total[:8]
-            send_ref[k] = total[8:]
+            keep_ref[k] = acc_ref[k * 16 : k * 16 + 8]
+            send_ref[k] = acc_ref[k * 16 + 8 : k * 16 + 16]
 
 
 def shifted(rows, distance):
-    if distance == 0:
-        return rows
     moved = pltpu.roll(rows, distance, 1)
     below = pltpu.roll(moved, 1, 0)
     row = lax.broadcasted_iota(jnp.int32, rows.shape, 0)
@@ -122,22 +137,19 @@
     return jnp.where(lane >= distance, moved, jnp.where(row > 0, below, 0.0))
 
 
-def knots_of(acc_ref, c):
-    total = None
-    for j in range(4):
-        start = (j * 4 + c) * 8
-        part = acc_ref[start : start + 8] + acc_ref[128 + start : 128 + start + 8]
-        part = shifted(part, j)
-        total = part if total is None else total + part
+def knots_of(parts):
+    total = parts[0]
+    for j in range(1, 4):
+        total = total + shifted(parts[j], j)
     return total
 
 
 def diag_kernel(
-    info_ref, att_ref, pha_ref, cal_ref, seg_ref, unit_ref,
+    live_ref, att_ref, pha_ref, cal_ref, seg_ref, unit_ref,
     extra_ref, rank_ref, knots_ref, slots_ref, acc_ref, slot_ref, carry_ref,
 ):
     step = pl.program_id(0)
-    live = live_row(info_ref, step)
+    live = live_row(live_ref, step)
     for c in range(4):
         for h in range(NB // 128):
             rows = att_ref[pl.ds(h * 512 + c, 128, stride=4), :]
@@ -146,7 +158,7 @@
     extra_ref[5] = cal_ref[...].T
     seg = seg_ref[0]
     seg_high = rows_equal(8, seg >> 8) * live
-    seg_low = rows_equal(256, seg & 255, BF16)
+    seg_low = narrow_rows_equal(256, seg & 255)
     halves = []
     for h in range(NB // 128):
         lanes = slice(h * 128, (h + 1) * 128)
@@ -160,7 +172,7 @@
         halves.append([column_sum(s) for s in sums])
     sums = [jnp.concatenate([half[k] for half in halves], axis=1) for k in range(17)]
     stacked = jnp.concatenate([seg_high * sums[k] for k in range(16)], axis=0)
-    accumulate(acc_ref, dot_nt(jnp.concatenate(split_parts(stacked, 2), axis=0), seg_low), step)
+    accumulate(acc_ref, packed_dot(stacked, seg_low, 2), step)
 
     unit = unit_ref[0]
     owner = rows_equal(RANGES, unit >> 12)
@@ -175,13 +187,13 @@
     place = rows_equal(CAP, rank)
     inner = (unit & (SHARE - 1)).astype(F32)
     stacked = jnp.concatenate([place * (sums[16] * live), place * inner], axis=0)
-    accumulate(slot_ref, dot_nt(jnp.concatenate(split_parts(stacked, 2), axis=0), owner_low), step)
+    accumulate(slot_ref, packed_dot(stacked, owner_low, 2), step)
 
     @pl.when(step == STEPS - 1)
     def _():
         for c in range(4):
-            knots_ref[c] = knots_of(acc_ref, c)
-        slots_ref[...] = slot_ref[:64] + slot_ref[64:]
+            knots_ref[c] = knots_of([acc_ref[(j * 4 + c) * 8 : (j * 4 + c) * 8 + 8] for j in range(4)])
+        slots_ref[...] = slot_ref[...]
 
 
 def solve_kernel(a_ref, b_ref, c_ref, d_ref, out_ref):
@@ -216,11 +228,11 @@
 
 
 def apply_kernel(
-    info_ref, srct_ref, extra_ref, idx_ref, seg_ref, unit_ref, rank_ref, mine_ref, other_ref,
+    live_ref, srct_ref, extra_ref, idx_ref, seg_ref, unit_ref, rank_ref, mine_ref, other_ref,
     diag_ref, slots_ref, out_ref, update_ref, table_ref, acc_ref, slot_ref,
 ):
     step = pl.program_id(0)
-    fov = info_ref[1]
+    fov = lax.axis_index("fov")
 
     @pl.when(step == 0)
     def _():
@@ -236,14 +248,13 @@
                 update_ref[k : k + 1, q * 256 : (q + 1) * 256] = first[q : q + 1]
                 update_ref[k : k + 1, 2048 + q * 256 : 2048 + (q + 1) * 256] = second[q : q + 1]
         stacked = jnp.concatenate(pieces, axis=0)
-        table_ref[...] = jnp.concatenate(split_parts(stacked, 3), axis=0)
-
-    live = live_row(info_ref, step)
+        table_ref[...] = jnp.concatenate(split_parts(stacked, 3), axis=1)
+
+    live = live_row(live_ref, step)
     idx = idx_ref[0] ^ (fov * 2048)
     high = rows_equal(16, idx >> 8)
-    low = rows_equal(256, idx & 255, BF16)
-    looked = dot_nn(table_ref[...], low)
-    looked = looked[:80] + looked[80:160] + looked[160:240]
+    low = narrow_rows_equal(256, idx & 255)
+    looked = dot_nn(table_ref[...], jnp.concatenate([low] * 3, axis=0))
     chosen = [column_sum(looked[k * 16 : k * 16 + 16] * high) for k in range(5)]
     halves = []
     for h in range(NB // 128):
@@ -256,50 +267,63 @@
             for k in range(1, 5):
                 model = model + srct_ref[k, span, lanes] * spread[k]
             residual = srct_ref[5, span, lanes] - model
-            basis = spline_basis(extra_ref[4, span, lanes])
-            weighted = [extra_ref[c, span, lanes] * residual for c in range(4)]
-            terms = [b * w for b in basis for w in weighted] + [extra_ref[5, span, lanes] * residual]
+            phase = extra_ref[4, span, lanes]
+            moments = [extra_ref[c, span, lanes] * residual for c in range(4)]
+            terms = list(moments)
+            for _ in range(3):
+                moments = [m * phase for m in moments]
+                terms += moments
+            terms.append(extra_ref[5, span, lanes] * residual)
             sums = terms if o == 0 else [s + t for s, t in zip(sums, terms)]
         halves.append([column_sum(s) for s in sums])
     sums = [jnp.concatenate([half[k] for half in halves], axis=1) for k in range(17)]
     seg = seg_ref[0]
     seg_high = rows_equal(8, seg >> 8) * live
-    seg_low = rows_equal(256, seg & 255, BF16)
+    seg_low = narrow_rows_equal(256, seg & 255)
     stacked = jnp.concatenate([seg_high * sums[k] for k in range(16)], axis=0)
-    accumulate(acc_ref, dot_nt(jnp.concatenate(split_parts(stacked, 2), axis=0), seg_low), step)
-    owner = rows_equal(RANGES, unit_ref[0] >> 12, BF16)
+    accumulate(acc_ref, packed_dot(stacked, seg_low, 2), step)
+    owner = narrow_rows_equal(RANGES, unit_ref[0] >> 12)
     placed = rows_equal(CAP, rank_ref[0]) * (sums[16] * live)
-    accumulate(slot_ref, dot_nt(jnp.concatenate(split_parts(placed, 2), axis=0), owner), step)
+    accumulate(slot_ref, packed_dot(placed, owner, 2), step)
 
     @pl.when(step == STEPS - 1)
     def _():
-        tm = info_ref[2]
-        slots = jnp.concatenate(
-            [slot_ref[:CAP] + slot_ref[CAP:], slots_ref[...], jnp.zeros((CAP, RANGES), F32)], axis=0
-        )
+        tm = lax.axis_index("tm")
+        slots = jnp.concatenate([slot_ref[...], slots_ref[...], jnp.zeros((CAP, RANGES), F32)], axis=0)
         out_ref[pl.ds(0, RANGES, stride=PIECES), :] = slots.T
-        for c in range(8):
-            knots = knots_of(acc_ref, c) if c < 4 else diag_ref[c - 4]
+        first_half = lax.broadcasted_iota(jnp.int32, (8, 128), 1) < 64
+        for c in range(4):
+            moments = [acc_ref[(k * 4 + c) * 8 : (k * 4 + c) * 8 + 8] for k in range(4)]
+            right = knots_of([spline_from_moments(moments, j) for j in range(4)])
             for r in range(2):
-                for f in range(2):
-                    start = r * 8 * PIECES + (tm * 2 + f) * PIECES + 1 + c
-                    out_ref[pl.ds(start, 8, stride=16 * PIECES), :] = knots[:, r * 128 : (r + 1) * 128]
-
-
-def final_kernel(info_ref, in_ref, att_ref, cal_ref, left_ref, right_ref):
-    tm = info_ref[2]
+                columns = slice(r * 128, (r + 1) * 128)
+                near, far = right[:, columns], diag_ref[c, :, columns]
+                start = (r * 8 + tm * 2) * PIECES + 1 + c
+                out_ref[pl.ds(start, 8, stride=16 * PIECES), :] = jnp.where(first_half, near, pltpu.roll(far, 64, 1))
+                out_ref[pl.ds(start + PIECES, 8, stride=16 * PIECES), :] = jnp.where(
+                    first_half, pltpu.roll(far, 64, 1), near
+                )
+
+
+def attitude_kernel(in_ref, att_ref):
+    base = lax.axis_index("tm") * 2 * PIECES + 1
     knots = None
     for s in range(16):
         for f in range(2):
-            part = in_ref[pl.ds((s * 8 + tm * 2 + f) * PIECES + 1, 8), :]
+            part = in_ref[pl.ds(base + (s * 8 + f) * PIECES, 4), :]
             knots = part if knots is None else knots + part
-    att_ref[...] = knots[:4] / (1.0 + knots[4:])
+    lower = lax.broadcasted_iota(jnp.int32, (4, 128), 1) < 64
+    mine = lower == (lax.axis_index("fov") == 0)
+    att_ref[...] = jnp.where(mine, knots / (1.0 + pltpu.roll(knots, 64, 1)), 0.0)
+
+
+def calibration_kernel(in_ref, cal_ref, left_ref, right_ref):
     slots = in_ref[pl.ds(0, RANGES, stride=PIECES), :].T
     unit = slots[64:96].astype(jnp.int32)
     for k in range(CAP):
         lanes = slice(k * 128, (k + 1) * 128)
         inner = unit[k : k + 1]
-        right_ref[:, lanes] = rows_equal(128, inner & 127, BF16)
+        right_ref[:, lanes] = narrow_rows_equal(128, inner & 127)
         high = rows_equal(32, inner >> 7)
         stacked = jnp.concatenate([high * slots[k : k + 1], high * slots[32 + k : 33 + k]], axis=0)
         left_ref[:, lanes] = jnp.concatenate(split_parts(stacked, 2), axis=0)
@@ -308,8 +332,13 @@
     cal_ref[...] = sums[:32] / (1.0 + sums[32:])
 
 
+VMEM = pl.BlockSpec(memory_space=pltpu.VMEM)
 SMEM = pl.BlockSpec(memory_space=pltpu.SMEM)
 ROW = pl.BlockSpec((1, 1, NB), lambda s: (s, 0, 0))
+
+
+def on_chip(*arrays):
+    return [pltpu.with_memory_space_constraint(a, pltpu.VMEM) for a in arrays]
 
 
 def whole(shape):
@@ -327,9 +356,6 @@
     block_unit,
     live_blocks,
 ):
-    tm = lax.axis_index("tm")
-    fov = lax.axis_index("fov")
-    info = jnp.stack([live_blocks[0], fov.astype(jnp.int32), tm.astype(jnp.int32)])
     source = block_source.reshape(STEPS, 1, NB)
     segment = block_segment.reshape(STEPS, 1, NB)
     unit = block_unit.reshape(STEPS, 1, NB)
@@ -346,21 +372,21 @@
             ROW,
         ],
         out_specs=[
-            whole((20, 8, 256)),
-            whole((20, 8, 256)),
+            VMEM,
+            VMEM,
             pl.BlockSpec((6, OBS, NB), lambda s: (0, 0, s)),
         ],
         out_shape=[
-            jax.ShapeDtypeStruct((20, 8, 256), F32),
-            jax.ShapeDtypeStruct((20, 8, 256), F32),
+            pltpu.VMEM((20, 8, 256), F32),
+            pltpu.VMEM((20, 8, 256), F32),
             jax.ShapeDtypeStruct((6, OBS, BLK), F32),
         ],
-        scratch_shapes=[pltpu.VMEM((960, 256), F32)],
+        scratch_shapes=[pltpu.VMEM((320, 256), F32)],
         compiler_params=sequential,
         name="normals",
-    )(info, src, obs_residual, source)
+    )(live_blocks, src, obs_residual, source)
     half = keep + lax.ppermute(send, "fov", [(0, 1), (1, 0)])
-    half, info_later = lax.optimization_barrier((half, info))
+    half, live_later = lax.optimization_barrier((half, live_blocks))
     around = [lax.ppermute(half, "tm", [(i, (i + d) % 4) for i in range(4)]) for d in (1, 2, 3)]
     extra, rank, diag_knots, diag_slots = pl.pallas_call(
         diag_kernel,
@@ -376,30 +402,32 @@
         out_specs=[
             pl.BlockSpec((6, OBS, NB), lambda s: (0, 0, s)),
             ROW,
-            whole((4, 8, 256)),
-            whole((64, RANGES)),
+            VMEM,
+            VMEM,
         ],
         out_shape=[
             jax.ShapeDtypeStruct((6, OBS, BLK), F32),
             jax.ShapeDtypeStruct((STEPS, 1, NB), jnp.int32),
-            jax.ShapeDtypeStruct((4, 8, 256), F32),
-            jax.ShapeDtypeStruct((64, RANGES), F32),
+            pltpu.VMEM((4, 8, 256), F32),
+            pltpu.VMEM((64, RANGES), F32),
         ],
         scratch_shapes=[
-            pltpu.VMEM((256, 256), F32),
-            pltpu.VMEM((128, RANGES), F32),
+            pltpu.VMEM((128, 256), F32),
+            pltpu.VMEM((64, RANGES), F32),
             pltpu.VMEM((RANGES, NB), F32),
         ],
         compiler_params=sequential,
         cost_estimate=pl.CostEstimate(flops=200_000_000, bytes_accessed=12_000_000, transcendentals=0),
         name="diag",
-    )(info_later, att, obs_phase, cal_partials, segment, unit)
+    )(live_later, att, obs_phase, cal_partials, segment, unit)
     around, diag_knots = lax.optimization_barrier((around, diag_knots))
     mine = pl.pallas_call(
         solve_kernel,
-        out_shape=jax.ShapeDtypeStruct((5, 8, 256), F32),
+        in_specs=[VMEM] * 4,
+        out_specs=VMEM,
+        out_shape=pltpu.VMEM((5, 8, 256), F32),
         name="solve",
-    )(half, *around)
+    )(*on_chip(half, *around))
     other = lax.ppermute(mine, "fov", [(0, 1), (1, 0)])
     outgoing, src_update = pl.pallas_call(
         apply_kernel,
@@ -412,37 +440,45 @@
             ROW,
             ROW,
             ROW,
-            whole((5, 8, 256)),
-            whole((5, 8, 256)),
-            whole((4, 8, 256)),
-            whole((64, RANGES)),
-        ],
-        out_specs=[whole((128 * PIECES, 128)), whole((5, 4096))],
+            VMEM,
+            VMEM,
+            VMEM,
+            VMEM,
+        ],
+        out_specs=[VMEM, whole((5, 4096))],
         out_shape=[
-            jax.ShapeDtypeStruct((128 * PIECES, 128), F32),
+            pltpu.VMEM((128 * PIECES, 128), F32),
             jax.ShapeDtypeStruct((5, 4096), F32),
         ],
         scratch_shapes=[
-            pltpu.VMEM((240, 256), BF16),
-            pltpu.VMEM((256, 256), F32),
-            pltpu.VMEM((64, RANGES), F32),
+            pltpu.VMEM((80, 768), BF16),
+            pltpu.VMEM((128, 256), F32),
+            pltpu.VMEM((CAP, RANGES), F32),
         ],
         compiler_params=sequential,
         name="apply",
-    )(info, srct, extra, source, segment, unit, rank, mine, other, diag_knots, diag_slots)
+    )(live_blocks, srct, extra, source, segment, unit, rank, *on_chip(mine, other, diag_knots, diag_slots))
     arrived = lax.all_to_all(
         outgoing.reshape(128, 1, PIECES * 128), ALL, split_axis=0, concat_axis=0, tiled=True
     ).reshape(128 * PIECES, 128)
-    att_update, cal_update = pl.pallas_call(
-        final_kernel,
-        in_specs=[SMEM, pl.BlockSpec(memory_space=pltpu.VMEM)],
-        out_shape=[
-            jax.ShapeDtypeStruct((4, 128), F32),
-            jax.ShapeDtypeStruct((32, 128), F32),
-        ],
+    att_half = pl.pallas_call(
+        attitude_kernel,
+        in_specs=[VMEM],
+        out_specs=VMEM,
+        out_shape=pltpu.VMEM((4, 128), F32),
+        name="attitude",
+    )(*on_chip(arrived))
+    att_other = lax.ppermute(att_half, "fov", [(0, 1), (1, 0)])
+    cal_update = pl.pallas_call(
+        calibration_kernel,
+        in_specs=[VMEM],
+        out_specs=VMEM,
+        out_shape=jax.ShapeDtypeStruct((32, 128), F32),
         scratch_shapes=[pltpu.VMEM((128, CAP * 128), BF16), pltpu.VMEM((128, CAP * 128), BF16)],
-        name="final",
-    )(info, arrived)
+        cost_estimate=pl.CostEstimate(flops=100_000_000, bytes_accessed=400_000, transcendentals=0),
+        name="calibration",
+    )(*on_chip(arrived))
+    att_update = att_half + att_other
     return (src_update, att_update.reshape(4, 1, 128), cal_update.reshape(SHARE))
 
 

time: 75.5 us -> 66.6 us (0.88)
  Pallas kernels: 37.9 us -> 33.7 us
  blocking collectives: 22.9 us -> 19.9 us
  local copies, waits for them, and re-layouts: 1.39 us -> 0 us
  starting transfers between devices: 7.23 us -> 8.48 us
  other arithmetic: 1.55 us -> 0.6 us
    all_to_all x1, blocking collectives: 22.9 us -> 19.9 us  [shards(): lax.all_to_all(outgoing.reshape(128, 1, PIECES * 128), ALL, split_axis=0,...]
    pallas_call x2 -> x3, Pallas kernels: 4.62 us -> 1.78 us  [the longest x1 1.53 us: shards(): pl.pallas_call(calibration_kernel, in_specs=[VMEM], out_specs=VMEM, out_s...]
    unnamed x10 -> x0, local copies, waits for them, and re-layouts: 1.39 us -> none
    ppermute x0 -> x1, starting transfers between devices: none -> 1.18 us  [shards(): att_other = lax.ppermute(att_half, 'fov', [(0, 1), (1, 0)])]
    add x1, other arithmetic: 0.94 us -> 0.02 us  [shards(): half = keep + lax.ppermute(send, 'fov', [(0, 1), (1, 0)])]
    pallas_call x1, Pallas kernels: 11.8 us -> 11 us  [shards(): pl.pallas_call(apply_kernel, grid=(STEPS,), in_specs=[SMEM, pl.BlockSpec(...]
  transfers between devices with their start and end apart: 5 -> 6, of which waited for: 2 -> 2; matrix products, arithmetic and copies ran while one was open for 0% -> 0% of each run, Pallas kernels for 15% -> 20%
where the time goes in v1:
time: 66.6 us; the launch traced here: 65.9 us
  Pallas kernels  33.7 us (51%)
  blocking collectives  19.9 us (30%)
  starting transfers between devices  8.48 us (13%)
  waiting for transfers between devices  1.91 us (3%)
  between operations  1.31 us (2%)
    all_to_all x1, blocking collectives, shards(): lax.all_to_all(outgoing.reshape(128, 1, PIECES * 128), ALL, split_axis=0,...  19.9 us
    pallas_call x1, Pallas kernels, shards(): pl.pallas_call(diag_kernel, grid=(STEPS,), in_specs=[SMEM, pl.BlockSpec((...  11.4 us
    pallas_call x1, Pallas kernels, shards(): pl.pallas_call(apply_kernel, grid=(STEPS,), in_specs=[SMEM, pl.BlockSpec(...  11 us
    pallas_call x1, Pallas kernels, shards(): pl.pallas_call(normals_kernel, grid=(STEPS,), in_specs=[SMEM, pl.BlockSpe...  9.54 us
    ppermute x3, starting transfers between devices, shards(): lax.ppermute(half, 'tm', [(i, (i + d) % 4) for i in range(4)])  4.64 us
    pallas_call x1, Pallas kernels, shards(): pl.pallas_call(calibration_kernel, in_specs=[VMEM], out_specs=VMEM, out_s...  1.53 us
    ppermute x1, starting transfers between devices, shards(): half = keep + lax.ppermute(send, 'fov', [(0, 1), (1, 0)])  1.38 us
  transfers between devices with their start and end apart: 6, of which 2 were waited for; matrix products, arithmetic and copies ran while one was open for 0% of the time, Pallas kernels for 20%

profile of v1, /device:TPU:1, one launch (start us, length us, event | category | flops | bytes accessed | tf_op | source)
XLA Modules:
  0.0 65.9 jit_solution(7233856819479935973)
XLA Ops:
  1.3 9.5 %normals.1 = (f32[20,8,256]{2,1,0:T(8,128)S(1)}, f32[20,8,256]{2,1,0:T(8,128)S(1)}, f32[6,128,2048]{2,1,0:T(8,128)}) custom-call(s32[1]{0:T(128)S(6)} %copy.15.live_ref, f32[5,2048,128]{2,1,0:T(8,128)} %bitcast.14, f32[2048,128]{1,0:T(8,128)} %res_ref.1, s32[8,1,256]{2,1,0:T(1,128)} %bitcast.16), custom_call_target="tpu_custom_call" | custom-call | tf_op jit(solution)/shard_map/normals/pallas_call | solution.py:365
  10.8 1.4 %collective-permute-start = (f32[20,8,256]{2,1,0:T(8,128)S(1)}, f32[20,8,256]{2,1,0:T(8,128)S(1)}, u32[]{:S(2)}, u32[]{:S(2)}) collective-permute-start(f32[20,8,256]{2,1,0:T(8,128)S(1)} %get-tuple-element.20), channel_id=1, source_target_pairs={{0,1},{1,0},{2,3},{3,2},{4,5},{5,4},{6,7},{7,6},{8,9},{9,8},{10,11... | collective-permute-start | bytes 491528 | tf_op jit(solution)/shard_map/ppermute | solution.py:388
  12.2 1.0 %collective-permute-done = f32[20,8,256]{2,1,0:T(8,128)S(1)} collective-permute-done((f32[20,8,256]{2,1,0:T(8,128)S(1)}, f32[20,8,256]{2,1,0:T(8,128)S(1)}, u32[]{:S(2)}, u32[]{:S(2)}) %collective-permute-start) | collective-permute-done | bytes 163872 | tf_op jit(solution)/shard_map/ppermute | solution.py:388
  13.3 3.9 %collective-permute-start.3 = (f32[20,8,256]{2,1,0:T(8,128)S(1)}, f32[20,8,256]{2,1,0:T(8,128)S(1)}, u32[]{:S(2)}, u32[]{:S(2)}) collective-permute-start(f32[20,8,256]{2,1,0:T(8,128)S(1)} %add.6.a_ref), channel_id=1, source_target_pairs={{0,6},{2,0},{4,2},{6,4},{1,7},{3,1},{5,3},{7,5},{8,14},{10,8},{12,... | collective-permute-start | bytes 491528 | tf_op jit(solution)/shard_map/ppermute | solution.py:390
  17.2 0.0 collective-permute-start.2
  17.2 0.7 %collective-permute-start.1 = (f32[20,8,256]{2,1,0:T(8,128)S(1)}, f32[20,8,256]{2,1,0:T(8,128)S(1)}, u32[]{:S(2)}, u32[]{:S(2)}) collective-permute-start(f32[20,8,256]{2,1,0:T(8,128)S(1)} %add.6.a_ref), channel_id=1, source_target_pairs={{0,2},{2,4},{4,6},{6,0},{1,3},{3,5},{5,7},{7,1},{8,10},{10,12},{12... | collective-permute-start | bytes 491528 | tf_op jit(solution)/shard_map/ppermute | solution.py:390
  17.9 11.4 %diag.1 = (f32[6,128,2048]{2,1,0:T(8,128)}, s32[8,1,256]{2,1,0:T(1,128)}, f32[4,8,256]{2,1,0:T(8,128)S(1)}, f32[64,128]{1,0:T(8,128)S(1)}) custom-call(s32[1]{0:T(128)S(6)} %copy.15.live_ref, f32[8192,128]{1,0:T(8,128)} %bitcast.15, f32[2048,128]{1,0:T(8,128)} %pha_ref.1, f32[2048,128]{1,0:T(8,128)} %cal_ref.1, s32[8,1,256]{2,1,0:T(1,128)} %bitcast.18, ...), custom_call_target="tpu_custom_call" | custom-call | flops 200000000 | bytes 12000000 | tf_op jit(solution)/shard_map/diag/pallas_call | solution.py:391
  29.3 0.0 collective-permute-done.3.d_ref
  29.3 0.0 collective-permute-done.2.c_ref
  29.3 0.0 collective-permute-done.1.b_ref
  29.4 0.1 solve.1.mine_ref
  29.5 1.3 %collective-permute-start.4 = (f32[5,8,256]{2,1,0:T(8,128)S(1)}, f32[5,8,256]{2,1,0:T(8,128)S(1)}, u32[]{:S(2)}, u32[]{:S(2)}) collective-permute-start(f32[5,8,256]{2,1,0:T(8,128)S(1)} %solve.1.mine_ref), channel_id=1, source_target_pairs={{0,1},{1,0},{2,3},{3,2},{4,5},{5,4},{6,7},{7,6},{8,9},{9,8},{10,11... | collective-permute-start | bytes 122888 | tf_op jit(solution)/shard_map/ppermute | solution.py:431
  30.8 0.9 %collective-permute-done.4.other_ref = f32[5,8,256]{2,1,0:T(8,128)S(1)} collective-permute-done((f32[5,8,256]{2,1,0:T(8,128)S(1)}, f32[5,8,256]{2,1,0:T(8,128)S(1)}, u32[]{:S(2)}, u32[]{:S(2)}) %collective-permute-start.4) | collective-permute-done | bytes 40992 | tf_op jit(solution)/shard_map/ppermute | solution.py:431
  31.6 11.0 %apply.1 = (f32[640,128]{1,0:T(8,128)S(1)}, f32[5,4096]{1,0:T(8,128)}) custom-call(s32[1]{0:T(128)S(6)} %copy.15.live_ref, f32[6,128,2048]{2,1,0:T(8,128)} %get-tuple-element.18.srct_ref, f32[6,128,2048]{2,1,0:T(8,128)} %get-tuple-element.22.extra_ref, s32[8,1,256]{2,1,0:T(1,128)} %bitcast.17, s32[8,1,256]{2,1,0:T(1,128)} %bitcast.19, ...), custom_call_target="tpu_custom_call" | custom-call | tf_op jit(solution)/shard_map/apply/pallas_call | solution.py:432
  42.6 19.9 %all_to_all.5 = f32[128,1,640]{2,1,0:T(1,128)S(1)} all-to-all(f32[128,1,640]{2,1,0:T(1,128)S(1)} %bitcast.13), channel_id=1, replica_groups=mesh['sky'=16,'tm'=4,'fov'=2] {'sky','tm','fov'}, dimensions={0} | all-to-all | bytes 655360 | tf_op jit(solution)/shard_map/all_to_all | solution.py:461
  62.5 0.1 attitude.1
  62.6 1.2 %collective-permute-start.5 = (f32[4,128]{1,0:T(4,128)S(1)}, f32[4,128]{1,0:T(4,128)S(1)}, u32[]{:S(2)}, u32[]{:S(2)}) collective-permute-start(f32[4,128]{1,0:T(4,128)S(1)} %attitude.1), channel_id=1, source_target_pairs={{0,1},{1,0},{2,3},{3,2},{4,5},{5,4},{6,7},{7,6},{8,9},{9,8},{10,11... | collective-permute-start | bytes 6152 | tf_op jit(solution)/shard_map/ppermute | solution.py:471
  63.8 1.5 %calibration.1 = f32[32,128]{1,0:T(8,128)} custom-call(f32[640,128]{1,0:T(8,128)S(1)} %bitcast.12), custom_call_target="tpu_custom_call" | custom-call | flops 100000000 | bytes 400000 | tf_op jit(solution)/shard_map/calibration/pallas_call | solution.py:472
  65.3 0.0 collective-permute-done.5
  65.3 0.6 add.7
  (1 shorter events, 0.0 us)
Async XLA Ops:
  10.8 2.4 %collective-permute-start = (f32[20,8,256]{2,1,0:T(8,128)S(1)}, f32[20,8,256]{2,1,0:T(8,128)S(1)}, u32[]{:S(2)}, u32[]{:S(2)}) collective-permute-start(f32[20,8,256]{2,1,0:T(8,128)S(1)} %get-tuple-element.20), channel_id=1, source_target_pairs={{0,1},{1,0},{2,3},{3,2},{4,5},{5,4},{6,7},{7,6},{8,9},{9,8},{10,11... | collective-permute-start | bytes 491528 | tf_op jit(solution)/shard_map/ppermute | solution.py:388
  13.3 16.1 %collective-permute-start.3 = (f32[20,8,256]{2,1,0:T(8,128)S(1)}, f32[20,8,256]{2,1,0:T(8,128)S(1)}, u32[]{:S(2)}, u32[]{:S(2)}) collective-permute-start(f32[20,8,256]{2,1,0:T(8,128)S(1)} %add.6.a_ref), channel_id=1, source_target_pairs={{0,6},{2,0},{4,2},{6,4},{1,7},{3,1},{5,3},{7,5},{8,14},{10,8},{12,... | collective-permute-start | bytes 491528 | tf_op jit(solution)/shard_map/ppermute | solution.py:390
  17.2 12.1 %collective-permute-start.2 = (f32[20,8,256]{2,1,0:T(8,128)S(1)}, f32[20,8,256]{2,1,0:T(8,128)S(1)}, u32[]{:S(2)}, u32[]{:S(2)}) collective-permute-start(f32[20,8,256]{2,1,0:T(8,128)S(1)} %add.6.a_ref), channel_id=1, source_target_pairs={{0,4},{2,6},{4,0},{6,2},{1,5},{3,7},{5,1},{7,3},{8,12},{10,14},{12... | collective-permute-start | bytes 491528 | tf_op jit(solution)/shard_map/ppermute | solution.py:390
  17.2 12.1 %collective-permute-start.1 = (f32[20,8,256]{2,1,0:T(8,128)S(1)}, f32[20,8,256]{2,1,0:T(8,128)S(1)}, u32[]{:S(2)}, u32[]{:S(2)}) collective-permute-start(f32[20,8,256]{2,1,0:T(8,128)S(1)} %add.6.a_ref), channel_id=1, source_target_pairs={{0,2},{2,4},{4,6},{6,0},{1,3},{3,5},{5,7},{7,1},{8,10},{10,12},{12... | collective-permute-start | bytes 491528 | tf_op jit(solution)/shard_map/ppermute | solution.py:390
  29.5 2.2 %collective-permute-start.4 = (f32[5,8,256]{2,1,0:T(8,128)S(1)}, f32[5,8,256]{2,1,0:T(8,128)S(1)}, u32[]{:S(2)}, u32[]{:S(2)}) collective-permute-start(f32[5,8,256]{2,1,0:T(8,128)S(1)} %solve.1.mine_ref), channel_id=1, source_target_pairs={{0,1},{1,0},{2,3},{3,2},{4,5},{5,4},{6,7},{7,6},{8,9},{9,8},{10,11... | collective-permute-start | bytes 122888 | tf_op jit(solution)/shard_map/ppermute | solution.py:431
  62.6 2.7 %collective-permute-start.5 = (f32[4,128]{1,0:T(4,128)S(1)}, f32[4,128]{1,0:T(4,128)S(1)}, u32[]{:S(2)}, u32[]{:S(2)}) collective-permute-start(f32[4,128]{1,0:T(4,128)S(1)} %attitude.1), channel_id=1, source_target_pairs={{0,1},{1,0},{2,3},{3,2},{4,5},{5,4},{6,7},{7,6},{8,9},{9,8},{10,11... | collective-permute-start | bytes 6152 | tf_op jit(solution)/shard_map/ppermute | solution.py:471

commit v2 on v1

--- a/solution.py
+++ b/solution.py
@@ -70,6 +70,10 @@
     return jnp.where(position < live_ref[0], 1.0, 0.0)
 
 
+def columns_of(ref, step):
+    return ref.at[:, :, pl.ds(pl.multiple_of(step * NB, NB), NB)]
+
+
 def column_sum(x):
     return jnp.sum(x, axis=0, keepdims=True)
 
@@ -98,8 +102,9 @@
     return m[3] * sixth
 
 
-def normals_kernel(live_ref, src_ref, res_ref, idx_ref, keep_ref, send_ref, srct_ref, acc_ref):
+def normals_kernel(live_ref, src_ref, res_ref, idx_ref, keep_ref, send_ref, all_src_ref, acc_ref):
     step = pl.program_id(0)
+    srct_ref = columns_of(all_src_ref, step)
     for i in range(5):
         srct_ref[i] = src_ref[i].T
     srct_ref[5] = res_ref[...].T
@@ -146,9 +151,10 @@
 
 def diag_kernel(
     live_ref, att_ref, pha_ref, cal_ref, seg_ref, unit_ref,
-    extra_ref, rank_ref, knots_ref, slots_ref, acc_ref, slot_ref, carry_ref,
+    all_extra_ref, rank_ref, knots_ref, slots_ref, acc_ref, slot_ref, carry_ref,
 ):
     step = pl.program_id(0)
+    extra_ref = columns_of(all_extra_ref, step)
     live = live_row(live_ref, step)
     for c in range(4):
         for h in range(NB // 128):
@@ -194,6 +200,10 @@
         for c in range(4):
             knots_ref[c] = knots_of([acc_ref[(j * 4 + c) * 8 : (j * 4 + c) * 8 + 8] for j in range(4)])
         slots_ref[...] = slot_ref[...]
+
+
+def join_kernel(a_ref, b_ref, out_ref):
+    out_ref[...] = a_ref[...] + b_ref[...]
 
 
 def solve_kernel(a_ref, b_ref, c_ref, d_ref, out_ref):
@@ -228,10 +238,12 @@
 
 
 def apply_kernel(
-    live_ref, srct_ref, extra_ref, idx_ref, seg_ref, unit_ref, rank_ref, mine_ref, other_ref,
+    live_ref, all_src_ref, all_extra_ref, idx_ref, seg_ref, unit_ref, rank_ref, mine_ref, other_ref,
     diag_ref, slots_ref, out_ref, update_ref, table_ref, acc_ref, slot_ref,
 ):
     step = pl.program_id(0)
+    srct_ref = columns_of(all_src_ref, step)
+    extra_ref = columns_of(all_extra_ref, step)
     fov = lax.axis_index("fov")
 
     @pl.when(step == 0)
@@ -341,6 +353,10 @@
     return [pltpu.with_memory_space_constraint(a, pltpu.VMEM) for a in arrays]
 
 
+def off_chip(*arrays):
+    return [pltpu.with_memory_space_constraint(a, pltpu.HBM) for a in arrays]
+
+
 def whole(shape):
     return pl.BlockSpec(shape, lambda s: (0,) * len(shape))
 
@@ -361,7 +377,8 @@
     unit = block_unit.reshape(STEPS, 1, NB)
     src = jnp.transpose(src_partials, (1, 0, 2))
     att = att_partials.reshape(BLK * 4, OBS)
-    sequential = pltpu.CompilerParams(dimension_semantics=("arbitrary",))
+    sequential = pltpu.CompilerParams(dimension_semantics=("arbitrary",), vmem_limit_bytes=24 * 1024 * 1024)
+    small = pltpu.CompilerParams(vmem_limit_bytes=4 * 1024 * 1024)
     keep, send, srct = pl.pallas_call(
         normals_kernel,
         grid=(STEPS,),
@@ -374,18 +391,25 @@
         out_specs=[
             VMEM,
             VMEM,
-            pl.BlockSpec((6, OBS, NB), lambda s: (0, 0, s)),
+            VMEM,
         ],
         out_shape=[
             pltpu.VMEM((20, 8, 256), F32),
             pltpu.VMEM((20, 8, 256), F32),
-            jax.ShapeDtypeStruct((6, OBS, BLK), F32),
+            pltpu.VMEM((6, OBS, BLK), F32),
         ],
         scratch_shapes=[pltpu.VMEM((320, 256), F32)],
         compiler_params=sequential,
         name="normals",
-    )(live_blocks, src, obs_residual, source)
-    half = keep + lax.ppermute(send, "fov", [(0, 1), (1, 0)])
+    )(live_blocks, *off_chip(src, obs_residual, source))
+    half = pl.pallas_call(
+        join_kernel,
+        in_specs=[VMEM] * 2,
+        out_specs=VMEM,
+        out_shape=pltpu.VMEM((20, 8, 256), F32),
+        compiler_params=small,
+        name="join",
+    )(*on_chip(keep, lax.ppermute(send, "fov", [(0, 1), (1, 0)])))
     half, live_later = lax.optimization_barrier((half, live_blocks))
     around = [lax.ppermute(half, "tm", [(i, (i + d) % 4) for i in range(4)]) for d in (1, 2, 3)]
     extra, rank, diag_knots, diag_slots = pl.pallas_call(
@@ -400,13 +424,13 @@
             ROW,
         ],
         out_specs=[
-            pl.BlockSpec((6, OBS, NB), lambda s: (0, 0, s)),
+            VMEM,
             ROW,
             VMEM,
             VMEM,
         ],
         out_shape=[
-            jax.ShapeDtypeStruct((6, OBS, BLK), F32),
+            pltpu.VMEM((6, OBS, BLK), F32),
             jax.ShapeDtypeStruct((STEPS, 1, NB), jnp.int32),
             pltpu.VMEM((4, 8, 256), F32),
             pltpu.VMEM((64, RANGES), F32),
@@ -426,6 +450,7 @@
         in_specs=[VMEM] * 4,
         out_specs=VMEM,
         out_shape=pltpu.VMEM((5, 8, 256), F32),
+        compiler_params=small,
         name="solve",
     )(*on_chip(half, *around))
     other = lax.ppermute(mine, "fov", [(0, 1), (1, 0)])
@@ -434,8 +459,8 @@
         grid=(STEPS,),
         in_specs=[
             SMEM,
-            pl.BlockSpec((6, OBS, NB), lambda s: (0, 0, s)),
-            pl.BlockSpec((6, OBS, NB), lambda s: (0, 0, s)),
+            VMEM,
+            VMEM,
             ROW,
             ROW,
             ROW,
@@ -457,7 +482,7 @@
         ],
         compiler_params=sequential,
         name="apply",
-    )(live_blocks, srct, extra, source, segment, unit, rank, *on_chip(mine, other, diag_knots, diag_slots))
+    )(live_blocks, *on_chip(srct, extra), source, segment, unit, rank, *on_chip(mine, other, diag_knots, diag_slots))
     arrived = lax.all_to_all(
         outgoing.reshape(128, 1, PIECES * 128), ALL, split_axis=0, concat_axis=0, tiled=True
     ).reshape(128 * PIECES, 128)
@@ -466,6 +491,7 @@
         in_specs=[VMEM],
         out_specs=VMEM,
         out_shape=pltpu.VMEM((4, 128), F32),
+        compiler_params=small,
         name="attitude",
     )(*on_chip(arrived))
     att_other = lax.ppermute(att_half, "fov", [(0, 1), (1, 0)])

time: 66.6 us -> 58.8 us (0.88)
  Pallas kernels: 33.7 us -> 26 us
  waiting for transfers between devices: 1.91 us -> 3.8 us
  blocking collectives: 19.9 us -> 18.5 us
    pallas_call x1, Pallas kernels: 11.4 us -> 7.91 us  [shards(): pl.pallas_call(diag_kernel, grid=(STEPS,), in_specs=[SMEM, pl.BlockSpec((...]
    pallas_call x1 -> x2, Pallas kernels: 11 us -> 8.11 us  [the longest x1 8.09 us: shards(): pl.pallas_call(apply_kernel, grid=(STEPS,), in_specs=[SMEM, VMEM, VMEM, R...]
    ppermute x3, waiting for transfers between devices: 0.01 us -> 1.9 us  [shards(): lax.ppermute(half, 'tm', [(i, (i + d) % 4) for i in range(4)])]
    all_to_all x1, blocking collectives: 19.9 us -> 18.5 us  [shards(): lax.all_to_all(outgoing.reshape(128, 1, PIECES * 128), ALL, split_axis=0,...]
    pallas_call x1, Pallas kernels: 9.54 us -> 8.24 us  [shards(): pl.pallas_call(normals_kernel, grid=(STEPS,), in_specs=[SMEM, pl.BlockSpe...]
  transfers between devices with their start and end apart: 6 -> 6, of which waited for: 2 -> 3; matrix products, arithmetic and copies ran while one was open for 0% -> 0% of each run, Pallas kernels for 20% -> 16%
where the time goes in v2:
time: 58.8 us; the launch traced here: 58.6 us
  Pallas kernels  26 us (44%)
  blocking collectives  18.5 us (31%)
  starting transfers between devices  8.14 us (14%)
  waiting for transfers between devices  3.8 us (6%)
  between operations  1.53 us (3%)
    all_to_all x1, blocking collectives, shards(): lax.all_to_all(outgoing.reshape(128, 1, PIECES * 128), ALL, split_axis=0,...  18.5 us
    pallas_call x1, Pallas kernels, shards(): pl.pallas_call(normals_kernel, grid=(STEPS,), in_specs=[SMEM, pl.BlockSpe...  8.24 us
    pallas_call x1, Pallas kernels, shards(): pl.pallas_call(apply_kernel, grid=(STEPS,), in_specs=[SMEM, VMEM, VMEM, R...  8.09 us
    pallas_call x1, Pallas kernels, shards(): pl.pallas_call(diag_kernel, grid=(STEPS,), in_specs=[SMEM, pl.BlockSpec((...  7.91 us
    ppermute x3, starting transfers between devices, shards(): lax.ppermute(half, 'tm', [(i, (i + d) % 4) for i in range(4)])  4.64 us
    ppermute x3, waiting for transfers between devices, shards(): lax.ppermute(half, 'tm', [(i, (i + d) % 4) for i in range(4)])  1.9 us
    pallas_call x1, Pallas kernels, shards(): pl.pallas_call(calibration_kernel, in_specs=[VMEM], out_specs=VMEM, out_s...  1.53 us
    ppermute x1, starting transfers between devices, shards(): lax.ppermute(send, 'fov', [(0, 1), (1, 0)])  1.46 us
  transfers between devices with their start and end apart: 6, of which 3 were waited for; matrix products, arithmetic and copies ran while one was open for 0% of the time, Pallas kernels for 16%

profile of v2, /device:TPU:1, one launch (start us, length us, event | category | flops | bytes accessed | tf_op | source)
XLA Modules:
  0.0 58.6 jit_solution(12369631077273693237)
XLA Ops:
  0.6 0.0 copy-start.5
  0.6 0.0 copy-start.4
  0.7 0.0 copy-start.1
  0.7 0.0 copy-start.2
  0.7 0.0 copy-start
  1.5 0.0 copy-start.3
  1.5 8.2 %normals.1 = (f32[20,8,256]{2,1,0:T(8,128)S(1)}, f32[20,8,256]{2,1,0:T(8,128)S(1)}, f32[6,128,2048]{2,1,0:T(8,128)S(1)}) custom-call(s32[1]{0:T(128)S(6)} %copy.15.live_ref, f32[5,2048,128]{2,1,0:T(8,128)} %bitcast.21, f32[2048,128]{1,0:T(8,128)} %res_ref.1, s32[8,1,256]{2,1,0:T(1,128)} %bitcast.15), custom_call_target="tpu_custom_call" | custom-call | tf_op jit(solution)/shard_map/normals/pallas_call | solution.py:382
  9.7 1.5 %collective-permute-start = (f32[20,8,256]{2,1,0:T(8,128)S(1)}, f32[20,8,256]{2,1,0:T(8,128)S(1)}, u32[]{:S(2)}, u32[]{:S(2)}) collective-permute-start(f32[20,8,256]{2,1,0:T(8,128)S(1)} %get-tuple-element.20), channel_id=1, source_target_pairs={{0,1},{1,0},{2,3},{3,2},{4,5},{5,4},{6,7},{7,6},{8,9},{9,8},{10,11... | collective-permute-start | bytes 491528 | tf_op jit(solution)/shard_map/ppermute | solution.py:412
  11.2 1.0 %collective-permute-done.b_ref = f32[20,8,256]{2,1,0:T(8,128)S(1)} collective-permute-done((f32[20,8,256]{2,1,0:T(8,128)S(1)}, f32[20,8,256]{2,1,0:T(8,128)S(1)}, u32[]{:S(2)}, u32[]{:S(2)}) %collective-permute-start) | collective-permute-done | bytes 163872 | tf_op jit(solution)/shard_map/ppermute | solution.py:412
  12.2 3.9 %collective-permute-start.3 = (f32[20,8,256]{2,1,0:T(8,128)S(1)}, f32[20,8,256]{2,1,0:T(8,128)S(1)}, u32[]{:S(2)}, u32[]{:S(2)}) collective-permute-start(f32[20,8,256]{2,1,0:T(8,128)S(1)} %join.1.a_ref), channel_id=1, source_target_pairs={{0,6},{2,0},{4,2},{6,4},{1,7},{3,1},{5,3},{7,5},{8,14},{10,8},{12,... | collective-permute-start | bytes 491528 | tf_op jit(solution)/shard_map/ppermute | solution.py:414
  16.2 0.0 collective-permute-start.2
  16.2 0.7 %collective-permute-start.1 = (f32[20,8,256]{2,1,0:T(8,128)S(1)}, f32[20,8,256]{2,1,0:T(8,128)S(1)}, u32[]{:S(2)}, u32[]{:S(2)}) collective-permute-start(f32[20,8,256]{2,1,0:T(8,128)S(1)} %join.1.a_ref), channel_id=1, source_target_pairs={{0,2},{2,4},{4,6},{6,0},{1,3},{3,5},{5,7},{7,1},{8,10},{10,12},{12... | collective-permute-start | bytes 491528 | tf_op jit(solution)/shard_map/ppermute | solution.py:414
  16.9 0.0 copy-done.5
  16.9 0.0 copy-done.4
  16.9 0.0 copy-done.1
  16.9 0.0 copy-done.2
  16.9 0.0 copy-done
  16.9 7.9 %diag.1 = (f32[6,128,2048]{2,1,0:T(8,128)S(1)}, s32[8,1,256]{2,1,0:T(1,128)S(1)}, f32[4,8,256]{2,1,0:T(8,128)S(1)}, f32[64,128]{1,0:T(8,128)S(1)}) custom-call(s32[1]{0:T(128)S(6)} %copy.15.live_ref, f32[8192,128]{1,0:T(8,128)S(1)} %bitcast.11, f32[2048,128]{1,0:T(8,128)S(1)} %copy-done.1, f32[2048,128]{1,0:T(8,128)S(1)} %copy-done.2, ...), custom_call_target="tpu_custom_call" | custom-call | flops 200000000 | bytes 12000000 | tf_op jit(solution)/shard_map/diag/pallas_call | solution.py:415
  24.8 0.0 collective-permute-done.3.d_ref
  24.8 0.0 collective-permute-done.2.c_ref
  24.8 1.9 %collective-permute-done.1.b_ref = f32[20,8,256]{2,1,0:T(8,128)S(1)} collective-permute-done((f32[20,8,256]{2,1,0:T(8,128)S(1)}, f32[20,8,256]{2,1,0:T(8,128)S(1)}, u32[]{:S(2)}, u32[]{:S(2)}) %collective-permute-start.1) | collective-permute-done | bytes 163872 | tf_op jit(solution)/shard_map/ppermute | solution.py:414
  26.7 0.1 solve.1.mine_ref
  26.9 0.9 %collective-permute-start.4 = (f32[5,8,256]{2,1,0:T(8,128)S(1)}, f32[5,8,256]{2,1,0:T(8,128)S(1)}, u32[]{:S(2)}, u32[]{:S(2)}) collective-permute-start(f32[5,8,256]{2,1,0:T(8,128)S(1)} %solve.1.mine_ref), channel_id=1, source_target_pairs={{0,1},{1,0},{2,3},{3,2},{4,5},{5,4},{6,7},{7,6},{8,9},{9,8},{10,11... | collective-permute-start | bytes 122888 | tf_op jit(solution)/shard_map/ppermute | solution.py:456
  27.7 0.9 %collective-permute-done.4.other_ref = f32[5,8,256]{2,1,0:T(8,128)S(1)} collective-permute-done((f32[5,8,256]{2,1,0:T(8,128)S(1)}, f32[5,8,256]{2,1,0:T(8,128)S(1)}, u32[]{:S(2)}, u32[]{:S(2)}) %collective-permute-start.4) | collective-permute-done | bytes 40992 | tf_op jit(solution)/shard_map/ppermute | solution.py:456
  28.6 0.0 copy-done.3
  28.6 8.1 %apply.1 = (f32[640,128]{1,0:T(8,128)S(1)}, f32[5,4096]{1,0:T(8,128)}) custom-call(s32[1]{0:T(128)S(6)} %copy.15.live_ref, f32[6,128,2048]{2,1,0:T(8,128)S(1)} %get-tuple-element.18.all_src_ref, f32[6,128,2048]{2,1,0:T(8,128)S(1)} %get-tuple-element.22.all_extra_ref, s32[8,1,256]{2,1,0:T(1,128)S(1)} %bitcast.16, s32[8,1,256]{2,1,0:T(1,128)S(1)} %bitcast.18, ...), custom_call_target="tpu_custom_call" | custom-call | tf_op jit(solution)/shard_map/apply/pallas_call | solution.py:457
  36.7 18.5 %all_to_all.5 = f32[128,1,640]{2,1,0:T(1,128)S(1)} all-to-all(f32[128,1,640]{2,1,0:T(1,128)S(1)} %bitcast.14), channel_id=1, replica_groups=mesh['sky'=16,'tm'=4,'fov'=2] {'sky','tm','fov'}, dimensions={0} | all-to-all | bytes 655360 | tf_op jit(solution)/shard_map/all_to_all | solution.py:486
  55.2 0.1 attitude.1
  55.3 1.2 %collective-permute-start.5 = (f32[4,128]{1,0:T(4,128)S(1)}, f32[4,128]{1,0:T(4,128)S(1)}, u32[]{:S(2)}, u32[]{:S(2)}) collective-permute-start(f32[4,128]{1,0:T(4,128)S(1)} %attitude.1), channel_id=1, source_target_pairs={{0,1},{1,0},{2,3},{3,2},{4,5},{5,4},{6,7},{7,6},{8,9},{9,8},{10,11... | collective-permute-start | bytes 6152 | tf_op jit(solution)/shard_map/ppermute | solution.py:497
  56.5 1.5 %calibration.1 = f32[32,128]{1,0:T(8,128)} custom-call(f32[640,128]{1,0:T(8,128)S(1)} %bitcast.13), custom_call_target="tpu_custom_call" | custom-call | flops 100000000 | bytes 400000 | tf_op jit(solution)/shard_map/calibration/pallas_call | solution.py:498
  58.0 0.0 collective-permute-done.5
  58.0 0.6 add.3
  (1 shorter events, 0.0 us)
Async XLA Ops:
  0.6 16.3 %copy-start.5 = (s32[2048]{0:T(1024)S(1)}, s32[2048]{0:T(1024)}, u32[]{:S(2)}) copy-start(s32[2048]{0:T(1024)} %param.16) | copy-start | bytes 24580
  0.6 16.2 %copy-start.4 = (s32[2048]{0:T(1024)S(1)}, s32[2048]{0:T(1024)}, u32[]{:S(2)}) copy-start(s32[2048]{0:T(1024)} %param.15) | copy-start | bytes 24580
  0.7 16.2 %copy-start.1 = (f32[2048,128]{1,0:T(8,128)S(1)}, f32[2048,128]{1,0:T(8,128)}, u32[]{:S(2)}) copy-start(f32[2048,128]{1,0:T(8,128)} %pha_ref.1) | copy-start | bytes 3145732
  0.7 16.2 %copy-start.2 = (f32[2048,128]{1,0:T(8,128)S(1)}, f32[2048,128]{1,0:T(8,128)}, u32[]{:S(2)}) copy-start(f32[2048,128]{1,0:T(8,128)} %cal_ref.1) | copy-start | bytes 3145732
  0.7 16.2 %copy-start = (f32[2048,4,128]{2,1,0:T(4,128)S(1)}, f32[2048,4,128]{2,1,0:T(4,128)}, u32[]{:S(2)}) copy-start(f32[2048,4,128]{2,1,0:T(4,128)} %param.10) | copy-start | bytes 12582916
  1.5 27.1 %copy-start.3 = (s32[2048]{0:T(1024)S(1)}, s32[2048]{0:T(1024)}, u32[]{:S(2)}) copy-start(s32[2048]{0:T(1024)} %param.14) | copy-start | bytes 24580
  9.7 2.5 %collective-permute-start = (f32[20,8,256]{2,1,0:T(8,128)S(1)}, f32[20,8,256]{2,1,0:T(8,128)S(1)}, u32[]{:S(2)}, u32[]{:S(2)}) collective-permute-start(f32[20,8,256]{2,1,0:T(8,128)S(1)} %get-tuple-element.20), channel_id=1, source_target_pairs={{0,1},{1,0},{2,3},{3,2},{4,5},{5,4},{6,7},{7,6},{8,9},{9,8},{10,11... | collective-permute-start | bytes 491528 | tf_op jit(solution)/shard_map/ppermute | solution.py:412
  12.2 12.6 %collective-permute-start.3 = (f32[20,8,256]{2,1,0:T(8,128)S(1)}, f32[20,8,256]{2,1,0:T(8,128)S(1)}, u32[]{:S(2)}, u32[]{:S(2)}) collective-permute-start(f32[20,8,256]{2,1,0:T(8,128)S(1)} %join.1.a_ref), channel_id=1, source_target_pairs={{0,6},{2,0},{4,2},{6,4},{1,7},{3,1},{5,3},{7,5},{8,14},{10,8},{12,... | collective-permute-start | bytes 491528 | tf_op jit(solution)/shard_map/ppermute | solution.py:414
  16.2 8.7 %collective-permute-start.2 = (f32[20,8,256]{2,1,0:T(8,128)S(1)}, f32[20,8,256]{2,1,0:T(8,128)S(1)}, u32[]{:S(2)}, u32[]{:S(2)}) collective-permute-start(f32[20,8,256]{2,1,0:T(8,128)S(1)} %join.1.a_ref), channel_id=1, source_target_pairs={{0,4},{2,6},{4,0},{6,2},{1,5},{3,7},{5,1},{7,3},{8,12},{10,14},{12... | collective-permute-start | bytes 491528 | tf_op jit(solution)/shard_map/ppermute | solution.py:414
  16.2 10.6 %collective-permute-start.1 = (f32[20,8,256]{2,1,0:T(8,128)S(1)}, f32[20,8,256]{2,1,0:T(8,128)S(1)}, u32[]{:S(2)}, u32[]{:S(2)}) collective-permute-start(f32[20,8,256]{2,1,0:T(8,128)S(1)} %join.1.a_ref), channel_id=1, source_target_pairs={{0,2},{2,4},{4,6},{6,0},{1,3},{3,5},{5,7},{7,1},{8,10},{10,12},{12... | collective-permute-start | bytes 491528 | tf_op jit(solution)/shard_map/ppermute | solution.py:414
  26.9 1.7 %collective-permute-start.4 = (f32[5,8,256]{2,1,0:T(8,128)S(1)}, f32[5,8,256]{2,1,0:T(8,128)S(1)}, u32[]{:S(2)}, u32[]{:S(2)}) collective-permute-start(f32[5,8,256]{2,1,0:T(8,128)S(1)} %solve.1.mine_ref), channel_id=1, source_target_pairs={{0,1},{1,0},{2,3},{3,2},{4,5},{5,4},{6,7},{7,6},{8,9},{9,8},{10,11... | collective-permute-start | bytes 122888 | tf_op jit(solution)/shard_map/ppermute | solution.py:456
  55.3 2.7 %collective-permute-start.5 = (f32[4,128]{1,0:T(4,128)S(1)}, f32[4,128]{1,0:T(4,128)S(1)}, u32[]{:S(2)}, u32[]{:S(2)}) collective-permute-start(f32[4,128]{1,0:T(4,128)S(1)} %attitude.1), channel_id=1, source_target_pairs={{0,1},{1,0},{2,3},{3,2},{4,5},{5,4},{6,7},{7,6},{8,9},{9,8},{10,11... | collective-permute-start | bytes 6152 | tf_op jit(solution)/shard_map/ppermute | solution.py:497

commit v3 on v2

--- a/solution.py
+++ b/solution.py
@@ -8,6 +8,8 @@
 BLK = 2048
 NB = 256
 STEPS = BLK // NB
+WIDE = 512
+WIDE_STEPS = BLK // WIDE
 OBS = 128
 CAP = 32
 RANGES = 128
@@ -38,12 +40,6 @@
     return lax.dot_general(a, b, (((1,), (0,)), ((), ())), preferred_element_type=F32)
 
 
-def packed_dot(left, right, count):
-    return dot_nt(
-        jnp.concatenate(split_parts(left, count), axis=1), jnp.concatenate([right] * count, axis=1)
-    )
-
-
 def rows_equal(count, row):
     iota = lax.broadcasted_iota(jnp.int32, (count, row.shape[1]), 0)
     return jnp.where(iota == row, 1.0, 0.0)
@@ -65,13 +61,60 @@
         ref[...] += product
 
 
-def live_row(live_ref, step):
-    position = step * NB + lax.broadcasted_iota(jnp.int32, (1, NB), 1)
+def live_row(live_ref, step, width):
+    position = step * width + lax.broadcasted_iota(jnp.int32, (1, width), 1)
     return jnp.where(position < live_ref[0], 1.0, 0.0)
 
 
-def columns_of(ref, step):
-    return ref.at[:, :, pl.ds(pl.multiple_of(step * NB, NB), NB)]
+def columns(step, width):
+    return pl.ds(pl.multiple_of(step * width, width), width)
+
+
+def row_bit(bit):
+    return (lax.broadcasted_iota(jnp.int32, (8, 128), 0) & bit) == 0
+
+
+def fold(accs):
+    upper = row_bit(4)
+    level = [
+        jnp.where(upper, accs[i], accs[i + 4]) + pltpu.roll(jnp.where(upper, accs[i + 4], accs[i]), 4, 0)
+        for i in range(4)
+    ]
+    upper = row_bit(2)
+    level = [
+        jnp.where(upper, level[i], level[i + 2])
+        + jnp.where(upper, pltpu.roll(level[i], 6, 0), pltpu.roll(level[i + 2], 2, 0))
+        for i in range(2)
+    ]
+    upper = row_bit(1)
+    return jnp.where(upper, level[0], level[1]) + jnp.where(
+        upper, pltpu.roll(level[0], 7, 0), pltpu.roll(level[1], 1, 0)
+    )
+
+
+def wide_parts(x, count):
+    parts = []
+    for _ in range(count - 1):
+        part = x.astype(BF16).astype(F32)
+        parts.append(part)
+        x = x - part
+    return parts + [x]
+
+
+def masked_rows(mask, blocks, count):
+    sides = []
+    split = [wide_parts(block, count) for block in blocks]
+    for n in range(count):
+        pieces = []
+        for parts in split:
+            for k in range(parts[n].shape[0]):
+                pieces.append(mask * jnp.broadcast_to(parts[n][k : k + 1], mask.shape).astype(BF16))
+        sides.append(jnp.concatenate(pieces, axis=0))
+    return jnp.concatenate(sides, axis=1)
+
+
+def repeated_dot(left, right, count):
+    return dot_nt(left, jnp.concatenate([right] * count, axis=1))
 
 
 def column_sum(x):
@@ -102,32 +145,36 @@
     return m[3] * sixth
 
 
-def normals_kernel(live_ref, src_ref, res_ref, idx_ref, keep_ref, send_ref, all_src_ref, acc_ref):
+def normals_kernel(live_ref, src_ref, res_ref, idx_ref, keep_ref, send_ref, all_src_ref, all_low_ref, acc_ref):
     step = pl.program_id(0)
-    srct_ref = columns_of(all_src_ref, step)
-    for i in range(5):
-        srct_ref[i] = src_ref[i].T
-    srct_ref[5] = res_ref[...].T
+    span = columns(step, WIDE)
+    srct_ref = all_src_ref.at[:, :, span]
     idx = idx_ref[0] ^ (lax.axis_index("fov") * 2048)
-    high = rows_equal(16, idx >> 8) * live_row(live_ref, step)
+    high = (rows_equal(16, idx >> 8) * live_row(live_ref, step, WIDE)).astype(BF16)
     low = narrow_rows_equal(256, idx & 255)
-    halves = []
-    for h in range(NB // 128):
+    all_low_ref[:, span] = low
+    groups = []
+    spare = []
+    for h in range(WIDE // 128):
         lanes = slice(h * 128, (h + 1) * 128)
+        for i in range(5):
+            srct_ref[i, :, lanes] = src_ref[i, lanes, :].T
+        srct_ref[5, :, lanes] = res_ref[lanes, :].T
         sums = [None] * 20
         for o in range(OBS // 8):
             rows = [srct_ref[i, o * 8 : o * 8 + 8, lanes] for i in range(6)]
             terms = [rows[i] * rows[j] for i, j in index_pairs] + [rows[i] * rows[5] for i in range(5)]
             sums = terms if o == 0 else [s + t for s, t in zip(sums, terms)]
-        halves.append([column_sum(s) for s in sums])
-    pieces = []
-    for k in range(20):
-        row = jnp.concatenate([half[k] for half in halves], axis=1)
-        pieces.append(high * row)
-    stacked = jnp.concatenate(pieces, axis=0)
-    accumulate(acc_ref, packed_dot(stacked, low, 3), step)
-
-    @pl.when(step == STEPS - 1)
+        groups.append(jnp.concatenate([fold(sums[:8]), fold(sums[8:16])], axis=0))
+        spare.append(sums[16:])
+    rest = []
+    for h in range(0, WIDE // 128, 2):
+        both = fold(spare[h] + spare[h + 1])
+        rest += [both[:4], both[4:]]
+    blocks = [jnp.concatenate(groups, axis=1), jnp.concatenate(rest, axis=1)]
+    accumulate(acc_ref, repeated_dot(masked_rows(high, blocks, 3), low, 3), step)
+
+    @pl.when(step == WIDE_STEPS - 1)
     def _():
         for k in range(20):
             keep_ref[k] = acc_ref[k * 16 : k * 16 + 8]
@@ -151,23 +198,38 @@
 
 def diag_kernel(
     live_ref, att_ref, pha_ref, cal_ref, seg_ref, unit_ref,
-    all_extra_ref, rank_ref, knots_ref, slots_ref, acc_ref, slot_ref, carry_ref,
+    all_extra_ref, all_low_ref, all_owner_ref, all_high_ref, all_place_ref, knots_ref, slots_ref,
+    acc_ref, slot_ref, carry_ref,
 ):
     step = pl.program_id(0)
-    extra_ref = columns_of(all_extra_ref, step)
-    live = live_row(live_ref, step)
-    for c in range(4):
-        for h in range(NB // 128):
-            rows = att_ref[pl.ds(h * 512 + c, 128, stride=4), :]
-            extra_ref[c, :, h * 128 : (h + 1) * 128] = rows.T
-    extra_ref[4] = pha_ref[...].T
-    extra_ref[5] = cal_ref[...].T
+    span = columns(step, NB)
+    extra_ref = all_extra_ref.at[:, :, span]
+    live = live_row(live_ref, step, NB)
+    unit = unit_ref[0]
+    owner = rows_equal(RANGES, unit >> 12)
+    owner_low = owner.astype(BF16)
+    all_owner_ref[:, span] = owner_low
+    before = lax.broadcasted_iota(jnp.int32, (NB, NB), 0) < lax.broadcasted_iota(jnp.int32, (NB, NB), 1)
+    before = jnp.where(before, 1.0, 0.0).astype(BF16)
+    earlier = dot_nn(owner_low, before) + jnp.where(step > 0, carry_ref[...], 0.0)
+    rank = column_sum(owner * earlier).astype(jnp.int32)
+    accumulate(carry_ref, dot_nn(owner_low, jnp.ones((NB, NB), BF16)), step)
+    place = rows_equal(CAP, rank)
+    place_live = (place * live).astype(BF16)
+    all_place_ref[:, span] = place_live
     seg = seg_ref[0]
-    seg_high = rows_equal(8, seg >> 8) * live
-    seg_low = narrow_rows_equal(256, seg & 255)
-    halves = []
+    seg_high = (rows_equal(16, seg >> 7) * live).astype(BF16)
+    seg_low = narrow_rows_equal(128, seg & 127)
+    all_high_ref[:, span] = seg_high
+    all_low_ref[:, span] = seg_low
+    groups = []
+    units = []
     for h in range(NB // 128):
         lanes = slice(h * 128, (h + 1) * 128)
+        for c in range(4):
+            extra_ref[c, :, lanes] = att_ref[pl.ds(h * 512 + c, 128, stride=4), :].T
+        extra_ref[4, :, lanes] = pha_ref[lanes, :].T
+        extra_ref[5, :, lanes] = cal_ref[lanes, :].T
         sums = [None] * 17
         for o in range(OBS // 8):
             rows = [extra_ref[i, o * 8 : o * 8 + 8, lanes] for i in range(6)]
@@ -175,30 +237,24 @@
             squares = [rows[c] * rows[c] for c in range(4)]
             terms = [b * s for b in basis for s in squares] + [rows[5] * rows[5]]
             sums = terms if o == 0 else [s + t for s, t in zip(sums, terms)]
-        halves.append([column_sum(s) for s in sums])
-    sums = [jnp.concatenate([half[k] for half in halves], axis=1) for k in range(17)]
-    stacked = jnp.concatenate([seg_high * sums[k] for k in range(16)], axis=0)
-    accumulate(acc_ref, packed_dot(stacked, seg_low, 2), step)
-
-    unit = unit_ref[0]
-    owner = rows_equal(RANGES, unit >> 12)
-    owner_low = owner.astype(BF16)
-    before = lax.broadcasted_iota(jnp.int32, (NB, NB), 0) < lax.broadcasted_iota(jnp.int32, (NB, NB), 1)
-    before = jnp.where(before, 1.0, 0.0).astype(BF16)
-    earlier = dot_nn(owner_low, before) + jnp.where(step > 0, carry_ref[...], 0.0)
-    rank = column_sum(owner * earlier)
-    accumulate(carry_ref, dot_nn(owner_low, jnp.ones((NB, NB), BF16)), step)
-    rank = rank.astype(jnp.int32)
-    rank_ref[0] = rank
-    place = rows_equal(CAP, rank)
+        groups.append(jnp.concatenate([fold(sums[:8]), fold(sums[8:16])], axis=0))
+        units.append(column_sum(sums[16]))
+    left = masked_rows(seg_high, [jnp.concatenate(groups, axis=1)], 2)
+    accumulate(acc_ref, repeated_dot(left, seg_low, 2), step)
     inner = (unit & (SHARE - 1)).astype(F32)
-    stacked = jnp.concatenate([place * (sums[16] * live), place * inner], axis=0)
-    accumulate(slot_ref, packed_dot(stacked, owner_low, 2), step)
+    left = jnp.concatenate(
+        [
+            masked_rows(place_live, [jnp.concatenate(units, axis=1)], 2),
+            masked_rows(place.astype(BF16), [inner], 2),
+        ],
+        axis=0,
+    )
+    accumulate(slot_ref, repeated_dot(left, owner_low, 2), step)
 
     @pl.when(step == STEPS - 1)
     def _():
         for c in range(4):
-            knots_ref[c] = knots_of([acc_ref[(j * 4 + c) * 8 : (j * 4 + c) * 8 + 8] for j in range(4)])
+            knots_ref[c] = knots_of([acc_ref[(j * 4 + c) * 16 : (j * 4 + c) * 16 + 16] for j in range(4)])
         slots_ref[...] = slot_ref[...]
 
 
@@ -238,12 +294,13 @@
 
 
 def apply_kernel(
-    live_ref, all_src_ref, all_extra_ref, idx_ref, seg_ref, unit_ref, rank_ref, mine_ref, other_ref,
-    diag_ref, slots_ref, out_ref, update_ref, table_ref, acc_ref, slot_ref,
+    all_src_ref, all_extra_ref, src_low_ref, seg_low_ref, owner_ref, seg_high_ref, place_ref, idx_ref,
+    mine_ref, other_ref, diag_ref, slots_ref, out_ref, update_ref, table_ref, acc_ref, slot_ref,
 ):
     step = pl.program_id(0)
-    srct_ref = columns_of(all_src_ref, step)
-    extra_ref = columns_of(all_extra_ref, step)
+    span = columns(step, WIDE)
+    srct_ref = all_src_ref.at[:, :, span]
+    extra_ref = all_extra_ref.at[:, :, span]
     fov = lax.axis_index("fov")
 
     @pl.when(step == 0)
@@ -262,59 +319,51 @@
         stacked = jnp.concatenate(pieces, axis=0)
         table_ref[...] = jnp.concatenate(split_parts(stacked, 3), axis=1)
 
-    live = live_row(live_ref, step)
     idx = idx_ref[0] ^ (fov * 2048)
     high = rows_equal(16, idx >> 8)
-    low = narrow_rows_equal(256, idx & 255)
+    low = src_low_ref[:, span]
     looked = dot_nn(table_ref[...], jnp.concatenate([low] * 3, axis=0))
     chosen = [column_sum(looked[k * 16 : k * 16 + 16] * high) for k in range(5)]
-    halves = []
-    for h in range(NB // 128):
+    groups = []
+    units = []
+    for h in range(WIDE // 128):
         lanes = slice(h * 128, (h + 1) * 128)
         spread = [jnp.broadcast_to(chosen[k][:, lanes], (8, 128)) for k in range(5)]
         sums = [None] * 17
         for o in range(OBS // 8):
-            span = slice(o * 8, o * 8 + 8)
-            model = srct_ref[0, span, lanes] * spread[0]
+            rows = slice(o * 8, o * 8 + 8)
+            model = srct_ref[0, rows, lanes] * spread[0]
             for k in range(1, 5):
-                model = model + srct_ref[k, span, lanes] * spread[k]
-            residual = srct_ref[5, span, lanes] - model
-            phase = extra_ref[4, span, lanes]
-            moments = [extra_ref[c, span, lanes] * residual for c in range(4)]
+                model = model + srct_ref[k, rows, lanes] * spread[k]
+            residual = srct_ref[5, rows, lanes] - model
+            phase = extra_ref[4, rows, lanes]
+            moments = [extra_ref[c, rows, lanes] * residual for c in range(4)]
             terms = list(moments)
             for _ in range(3):
                 moments = [m * phase for m in moments]
                 terms += moments
-            terms.append(extra_ref[5, span, lanes] * residual)
+            terms.append(extra_ref[5, rows, lanes] * residual)
             sums = terms if o == 0 else [s + t for s, t in zip(sums, terms)]
-        halves.append([column_sum(s) for s in sums])
-    sums = [jnp.concatenate([half[k] for half in halves], axis=1) for k in range(17)]
-    seg = seg_ref[0]
-    seg_high = rows_equal(8, seg >> 8) * live
-    seg_low = narrow_rows_equal(256, seg & 255)
-    stacked = jnp.concatenate([seg_high * sums[k] for k in range(16)], axis=0)
-    accumulate(acc_ref, packed_dot(stacked, seg_low, 2), step)
-    owner = narrow_rows_equal(RANGES, unit_ref[0] >> 12)
-    placed = rows_equal(CAP, rank_ref[0]) * (sums[16] * live)
-    accumulate(slot_ref, packed_dot(placed, owner, 2), step)
-
-    @pl.when(step == STEPS - 1)
+        groups.append(jnp.concatenate([fold(sums[:8]), fold(sums[8:16])], axis=0))
+        units.append(column_sum(sums[16]))
+    left = masked_rows(seg_high_ref[:, span], [jnp.concatenate(groups, axis=1)], 2)
+    accumulate(acc_ref, repeated_dot(left, seg_low_ref[:, span], 2), step)
+    left = masked_rows(place_ref[:, span], [jnp.concatenate(units, axis=1)], 2)
+    accumulate(slot_ref, repeated_dot(left, owner_ref[:, span], 2), step)
+
+    @pl.when(step == WIDE_STEPS - 1)
     def _():
         tm = lax.axis_index("tm")
         slots = jnp.concatenate([slot_ref[...], slots_ref[...], jnp.zeros((CAP, RANGES), F32)], axis=0)
         out_ref[pl.ds(0, RANGES, stride=PIECES), :] = slots.T
-        first_half = lax.broadcasted_iota(jnp.int32, (8, 128), 1) < 64
+        first_half = lax.broadcasted_iota(jnp.int32, (16, 128), 1) < 64
         for c in range(4):
-            moments = [acc_ref[(k * 4 + c) * 8 : (k * 4 + c) * 8 + 8] for k in range(4)]
+            moments = [acc_ref[(k * 4 + c) * 16 : (k * 4 + c) * 16 + 16] for k in range(4)]
             right = knots_of([spline_from_moments(moments, j) for j in range(4)])
-            for r in range(2):
-                columns = slice(r * 128, (r + 1) * 128)
-                near, far = right[:, columns], diag_ref[c, :, columns]
-                start = (r * 8 + tm * 2) * PIECES + 1 + c
-                out_ref[pl.ds(start, 8, stride=16 * PIECES), :] = jnp.where(first_half, near, pltpu.roll(far, 64, 1))
-                out_ref[pl.ds(start + PIECES, 8, stride=16 * PIECES), :] = jnp.where(
-                    first_half, pltpu.roll(far, 64, 1), near
-                )
+            far = pltpu.roll(diag_ref[c], 64, 1)
+            start = tm * 2 * PIECES + 1 + c
+            out_ref[pl.ds(start, 16, stride=8 * PIECES), :] = jnp.where(first_half, right, far)
+            out_ref[pl.ds(start + PIECES, 16, stride=8 * PIECES), :] = jnp.where(first_half, far, right)
 
 
 def attitude_kernel(in_ref, att_ref):
@@ -332,13 +381,16 @@
 def calibration_kernel(in_ref, cal_ref, left_ref, right_ref):
     slots = in_ref[pl.ds(0, RANGES, stride=PIECES), :].T
     unit = slots[64:96].astype(jnp.int32)
+    parts = wide_parts(slots[:64], 2)
     for k in range(CAP):
         lanes = slice(k * 128, (k + 1) * 128)
         inner = unit[k : k + 1]
         right_ref[:, lanes] = narrow_rows_equal(128, inner & 127)
-        high = rows_equal(32, inner >> 7)
-        stacked = jnp.concatenate([high * slots[k : k + 1], high * slots[32 + k : 33 + k]], axis=0)
-        left_ref[:, lanes] = jnp.concatenate(split_parts(stacked, 2), axis=0)
+        high = narrow_rows_equal(32, inner >> 7)
+        for n in range(2):
+            for v in range(2):
+                row = jnp.broadcast_to(parts[n][v * 32 + k : v * 32 + k + 1], (32, 128)).astype(BF16)
+                left_ref[(n * 2 + v) * 32 : (n * 2 + v + 1) * 32, lanes] = high * row
     sums = dot_nt(left_ref[...], right_ref[...])
     sums = sums[:64] + sums[64:]
     cal_ref[...] = sums[:32] / (1.0 + sums[32:])
@@ -347,6 +399,7 @@
 VMEM = pl.BlockSpec(memory_space=pltpu.VMEM)
 SMEM = pl.BlockSpec(memory_space=pltpu.SMEM)
 ROW = pl.BlockSpec((1, 1, NB), lambda s: (s, 0, 0))
+WIDE_ROW = pl.BlockSpec((1, 1, WIDE), lambda s: (s, 0, 0))
 
 
 def on_chip(*arrays):
@@ -372,31 +425,28 @@
     block_unit,
     live_blocks,
 ):
-    source = block_source.reshape(STEPS, 1, NB)
+    source = block_source.reshape(WIDE_STEPS, 1, WIDE)
     segment = block_segment.reshape(STEPS, 1, NB)
     unit = block_unit.reshape(STEPS, 1, NB)
     src = jnp.transpose(src_partials, (1, 0, 2))
     att = att_partials.reshape(BLK * 4, OBS)
     sequential = pltpu.CompilerParams(dimension_semantics=("arbitrary",), vmem_limit_bytes=24 * 1024 * 1024)
     small = pltpu.CompilerParams(vmem_limit_bytes=4 * 1024 * 1024)
-    keep, send, srct = pl.pallas_call(
+    keep, send, srct, src_low = pl.pallas_call(
         normals_kernel,
-        grid=(STEPS,),
+        grid=(WIDE_STEPS,),
         in_specs=[
             SMEM,
-            pl.BlockSpec((5, NB, OBS), lambda s: (0, s, 0)),
-            pl.BlockSpec((NB, OBS), lambda s: (s, 0)),
-            ROW,
-        ],
-        out_specs=[
-            VMEM,
-            VMEM,
-            VMEM,
-        ],
+            pl.BlockSpec((5, WIDE, OBS), lambda s: (0, s, 0)),
+            pl.BlockSpec((WIDE, OBS), lambda s: (s, 0)),
+            WIDE_ROW,
+        ],
+        out_specs=[VMEM] * 4,
         out_shape=[
             pltpu.VMEM((20, 8, 256), F32),
             pltpu.VMEM((20, 8, 256), F32),
             pltpu.VMEM((6, OBS, BLK), F32),
+            pltpu.VMEM((256, BLK), BF16),
         ],
         scratch_shapes=[pltpu.VMEM((320, 256), F32)],
         compiler_params=sequential,
@@ -412,7 +462,7 @@
     )(*on_chip(keep, lax.ppermute(send, "fov", [(0, 1), (1, 0)])))
     half, live_later = lax.optimization_barrier((half, live_blocks))
     around = [lax.ppermute(half, "tm", [(i, (i + d) % 4) for i in range(4)]) for d in (1, 2, 3)]
-    extra, rank, diag_knots, diag_slots = pl.pallas_call(
+    extra, seg_low, owner, seg_high, place, diag_knots, diag_slots = pl.pallas_call(
         diag_kernel,
         grid=(STEPS,),
         in_specs=[
@@ -423,20 +473,18 @@
             ROW,
             ROW,
         ],
-        out_specs=[
-            VMEM,
-            ROW,
-            VMEM,
-            VMEM,
-        ],
+        out_specs=[VMEM] * 7,
         out_shape=[
             pltpu.VMEM((6, OBS, BLK), F32),
-            jax.ShapeDtypeStruct((STEPS, 1, NB), jnp.int32),
-            pltpu.VMEM((4, 8, 256), F32),
+            pltpu.VMEM((128, BLK), BF16),
+            pltpu.VMEM((RANGES, BLK), BF16),
+            pltpu.VMEM((16, BLK), BF16),
+            pltpu.VMEM((CAP, BLK), BF16),
+            pltpu.VMEM((4, 16, 128), F32),
             pltpu.VMEM((64, RANGES), F32),
         ],
         scratch_shapes=[
-            pltpu.VMEM((128, 256), F32),
+            pltpu.VMEM((256, 128), F32),
             pltpu.VMEM((64, RANGES), F32),
             pltpu.VMEM((RANGES, NB), F32),
         ],
@@ -456,20 +504,8 @@
     other = lax.ppermute(mine, "fov", [(0, 1), (1, 0)])
     outgoing, src_update = pl.pallas_call(
         apply_kernel,
-        grid=(STEPS,),
-        in_specs=[
-            SMEM,
-            VMEM,
-            VMEM,
-            ROW,
-            ROW,
-            ROW,
-            ROW,
-            VMEM,
-            VMEM,
-            VMEM,
-            VMEM,
-        ],
+        grid=(WIDE_STEPS,),
+        in_specs=[VMEM] * 7 + [WIDE_ROW] + [VMEM] * 4,
         out_specs=[VMEM, whole((5, 4096))],
         out_shape=[
             pltpu.VMEM((128 * PIECES, 128), F32),
@@ -477,12 +513,16 @@
         ],
         scratch_shapes=[
             pltpu.VMEM((80, 768), BF16),
-            pltpu.VMEM((128, 256), F32),
+            pltpu.VMEM((256, 128), F32),
             pltpu.VMEM((CAP, RANGES), F32),
         ],
         compiler_params=sequential,
         name="apply",
-    )(live_blocks, *on_chip(srct, extra), source, segment, unit, rank, *on_chip(mine, other, diag_knots, diag_slots))
+    )(
+        *on_chip(srct, extra, src_low, seg_low, owner, seg_high, place),
+        source,
+        *on_chip(mine, other, diag_knots, diag_slots),
+    )
     arrived = lax.all_to_all(
         outgoing.reshape(128, 1, PIECES * 128), ALL, split_axis=0, concat_axis=0, tiled=True
     ).reshape(128 * PIECES, 128)

time: 58.8 us -> 54.8 us (0.932)
  Pallas kernels: 26 us -> 22.2 us
    pallas_call x2, Pallas kernels: 16.3 us -> 12.4 us  [the longest x1 6.23 us: shards(): pl.pallas_call(normals_kernel, grid=(WIDE_STEPS,), in_specs=[SMEM, pl.Blo...]
  transfers between devices with their start and end apart: 6 -> 6, of which waited for: 3 -> 3; matrix products, arithmetic and copies ran while one was open for 0% -> 0% of each run, Pallas kernels for 16% -> 17%
where the time goes in v3:
time: 54.8 us; the launch traced here: 54.7 us
  Pallas kernels  22.2 us (41%)
  blocking collectives  18.6 us (34%)
  starting transfers between devices  8.15 us (15%)
  waiting for transfers between devices  3.61 us (7%)
  between operations  1.53 us (3%)
  other arithmetic  0.58 us (1%)
    all_to_all x1, blocking collectives, shards(): lax.all_to_all(outgoing.reshape(128, 1, PIECES * 128), ALL, split_axis=0,...  18.6 us
    pallas_call x1, Pallas kernels, shards(): pl.pallas_call(diag_kernel, grid=(STEPS,), in_specs=[SMEM, pl.BlockSpec((...  8.1 us
    pallas_call x1, Pallas kernels, shards(): pl.pallas_call(normals_kernel, grid=(WIDE_STEPS,), in_specs=[SMEM, pl.Blo...  6.23 us
    pallas_call x1, Pallas kernels, shards(): pl.pallas_call(apply_kernel, grid=(WIDE_STEPS,), in_specs=[VMEM] * 7 + [W...  6.13 us
    ppermute x3, starting transfers between devices, shards(): lax.ppermute(half, 'tm', [(i, (i + d) % 4) for i in range(4)])  4.64 us
    ppermute x3, waiting for transfers between devices, shards(): lax.ppermute(half, 'tm', [(i, (i + d) % 4) for i in range(4)])  1.71 us
    ppermute x1, starting transfers between devices, shards(): lax.ppermute(send, 'fov', [(0, 1), (1, 0)])  1.47 us
    pallas_call x1, Pallas kernels, shards(): pl.pallas_call(calibration_kernel, in_specs=[VMEM], out_specs=VMEM, out_s...  1.43 us
  transfers between devices with their start and end apart: 6, of which 3 were waited for; matrix products, arithmetic and copies ran while one was open for 0% of the time, Pallas kernels for 17%

profile of v3, /device:TPU:1, one launch (start us, length us, event | category | flops | bytes accessed | tf_op | source)
XLA Modules:
  0.0 54.7 jit_solution(11009493053314256666)
XLA Ops:
  0.6 0.0 copy-start.5
  0.6 0.0 copy-start.4
  0.7 0.0 copy-start.1
  0.7 0.0 copy-start.2
  0.7 0.0 copy-start
  1.5 0.0 copy-start.3
  1.5 6.2 %normals.1 = (f32[20,8,256]{2,1,0:T(8,128)S(1)}, f32[20,8,256]{2,1,0:T(8,128)S(1)}, f32[6,128,2048]{2,1,0:T(8,128)S(1)}, bf16[256,2048]{1,0:T(8,128)(2,1)S(1)}) custom-call(s32[1]{0:T(128)S(6)} %copy.15.live_ref, f32[5,2048,128]{2,1,0:T(8,128)} %bitcast.19, f32[2048,128]{1,0:T(8,128)} %res_ref.1, s32[4,1,512]{2,1,0:T(1,128)} %bitcast.15), custom_call_target="tpu_custom_call" | custom-call | tf_op jit(solution)/shard_map/normals/pallas_call | solution.py:435
  7.7 1.5 %collective-permute-start = (f32[20,8,256]{2,1,0:T(8,128)S(1)}, f32[20,8,256]{2,1,0:T(8,128)S(1)}, u32[]{:S(2)}, u32[]{:S(2)}) collective-permute-start(f32[20,8,256]{2,1,0:T(8,128)S(1)} %get-tuple-element.24), channel_id=1, source_target_pairs={{0,1},{1,0},{2,3},{3,2},{4,5},{5,4},{6,7},{7,6},{8,9},{9,8},{10,11... | collective-permute-start | bytes 491528 | tf_op jit(solution)/shard_map/ppermute | solution.py:462
  9.2 1.0 %collective-permute-done.b_ref = f32[20,8,256]{2,1,0:T(8,128)S(1)} collective-permute-done((f32[20,8,256]{2,1,0:T(8,128)S(1)}, f32[20,8,256]{2,1,0:T(8,128)S(1)}, u32[]{:S(2)}, u32[]{:S(2)}) %collective-permute-start) | collective-permute-done | bytes 163872 | tf_op jit(solution)/shard_map/ppermute | solution.py:462
  10.2 3.9 %collective-permute-start.3 = (f32[20,8,256]{2,1,0:T(8,128)S(1)}, f32[20,8,256]{2,1,0:T(8,128)S(1)}, u32[]{:S(2)}, u32[]{:S(2)}) collective-permute-start(f32[20,8,256]{2,1,0:T(8,128)S(1)} %join.1.a_ref), channel_id=1, source_target_pairs={{0,6},{2,0},{4,2},{6,4},{1,7},{3,1},{5,3},{7,5},{8,14},{10,8},{12,... | collective-permute-start | bytes 491528 | tf_op jit(solution)/shard_map/ppermute | solution.py:464
  14.2 0.0 collective-permute-start.2
  14.2 0.7 %collective-permute-start.1 = (f32[20,8,256]{2,1,0:T(8,128)S(1)}, f32[20,8,256]{2,1,0:T(8,128)S(1)}, u32[]{:S(2)}, u32[]{:S(2)}) collective-permute-start(f32[20,8,256]{2,1,0:T(8,128)S(1)} %join.1.a_ref), channel_id=1, source_target_pairs={{0,2},{2,4},{4,6},{6,0},{1,3},{3,5},{5,7},{7,1},{8,10},{10,12},{12... | collective-permute-start | bytes 491528 | tf_op jit(solution)/shard_map/ppermute | solution.py:464
  14.9 0.0 copy-done.5
  14.9 0.0 copy-done.4
  14.9 0.0 copy-done.1
  14.9 0.0 copy-done.2
  14.9 0.0 copy-done
  14.9 8.1 %diag.1 = (f32[6,128,2048]{2,1,0:T(8,128)S(1)}, bf16[128,2048]{1,0:T(8,128)(2,1)S(1)}, bf16[128,2048]{1,0:T(8,128)(2,1)S(1)}, bf16[16,2048]{1,0:T(8,128)(2,1)S(1...) custom-call(s32[1]{0:T(128)S(6)} %copy.15.live_ref, f32[8192,128]{1,0:T(8,128)S(1)} %bitcast.11, ...), custom_call_target="tpu_custom_call" | custom-call | flops 200000000 | bytes 12000000 | tf_op jit(solution)/shard_map/diag/pallas_call | solution.py:465
  23.0 0.0 collective-permute-done.3.d_ref
  23.0 0.0 collective-permute-done.2.c_ref
  23.0 1.7 %collective-permute-done.1.b_ref = f32[20,8,256]{2,1,0:T(8,128)S(1)} collective-permute-done((f32[20,8,256]{2,1,0:T(8,128)S(1)}, f32[20,8,256]{2,1,0:T(8,128)S(1)}, u32[]{:S(2)}, u32[]{:S(2)}) %collective-permute-start.1) | collective-permute-done | bytes 163872 | tf_op jit(solution)/shard_map/ppermute | solution.py:464
  24.7 0.1 solve.1.mine_ref
  24.9 0.9 %collective-permute-start.4 = (f32[5,8,256]{2,1,0:T(8,128)S(1)}, f32[5,8,256]{2,1,0:T(8,128)S(1)}, u32[]{:S(2)}, u32[]{:S(2)}) collective-permute-start(f32[5,8,256]{2,1,0:T(8,128)S(1)} %solve.1.mine_ref), channel_id=1, source_target_pairs={{0,1},{1,0},{2,3},{3,2},{4,5},{5,4},{6,7},{7,6},{8,9},{9,8},{10,11... | collective-permute-start | bytes 122888 | tf_op jit(solution)/shard_map/ppermute | solution.py:504
  25.7 0.9 %collective-permute-done.4.other_ref = f32[5,8,256]{2,1,0:T(8,128)S(1)} collective-permute-done((f32[5,8,256]{2,1,0:T(8,128)S(1)}, f32[5,8,256]{2,1,0:T(8,128)S(1)}, u32[]{:S(2)}, u32[]{:S(2)}) %collective-permute-start.4) | collective-permute-done | bytes 40992 | tf_op jit(solution)/shard_map/ppermute | solution.py:504
  26.6 0.0 copy-done.3
  26.6 6.1 %apply.1 = (f32[640,128]{1,0:T(8,128)S(1)}, f32[5,4096]{1,0:T(8,128)}) custom-call(f32[6,128,2048]{2,1,0:T(8,128)S(1)} %get-tuple-element.22.all_src_ref, f32[6,128,2048]{2,1,0:T(8,128)S(1)} %get-tuple-element.26.all_extra_ref, bf16[256,2048]{1,0:T(8,128)(2,1)S(1)} %get-tuple-element.27.src_low_ref, bf16[128,2048]{1,0:T(8,128)(2,1)S(1)} %get-tuple-element.28.seg_low_ref, ...), custom_call_target="tpu_custom_call" | custom-call | tf_op jit(solution)/shard_map/apply/pallas_call | solution.py:505
  32.7 18.6 %all_to_all.5 = f32[128,1,640]{2,1,0:T(1,128)S(1)} all-to-all(f32[128,1,640]{2,1,0:T(1,128)S(1)} %bitcast.14), channel_id=1, replica_groups=mesh['sky'=16,'tm'=4,'fov'=2] {'sky','tm','fov'}, dimensions={0} | all-to-all | bytes 655360 | tf_op jit(solution)/shard_map/all_to_all | solution.py:526
  51.4 0.1 attitude.1
  51.5 1.2 %collective-permute-start.5 = (f32[4,128]{1,0:T(4,128)S(1)}, f32[4,128]{1,0:T(4,128)S(1)}, u32[]{:S(2)}, u32[]{:S(2)}) collective-permute-start(f32[4,128]{1,0:T(4,128)S(1)} %attitude.1), channel_id=1, source_target_pairs={{0,1},{1,0},{2,3},{3,2},{4,5},{5,4},{6,7},{7,6},{8,9},{9,8},{10,11... | collective-permute-start | bytes 6152 | tf_op jit(solution)/shard_map/ppermute | solution.py:537
  52.6 1.4 %calibration.1 = f32[32,128]{1,0:T(8,128)} custom-call(f32[640,128]{1,0:T(8,128)S(1)} %bitcast.13), custom_call_target="tpu_custom_call" | custom-call | flops 100000000 | bytes 400000 | tf_op jit(solution)/shard_map/calibration/pallas_call | solution.py:538
  54.1 0.0 collective-permute-done.5
  54.1 0.6 %add.3 = f32[4,128]{1,0:T(4,128)} add(f32[4,128]{1,0:T(4,128)S(1)} %attitude.1, f32[4,128]{1,0:T(4,128)S(1)} %collective-permute-done.5) | non-fusion elementwise | flops 512 | bytes 6144 | tf_op jit(solution)/shard_map/add | solution.py:547
  (1 shorter events, 0.0 us)
Async XLA Ops:
  0.6 14.3 %copy-start.5 = (s32[2048]{0:T(1024)S(1)}, s32[2048]{0:T(1024)}, u32[]{:S(2)}) copy-start(s32[2048]{0:T(1024)} %param.16) | copy-start | bytes 24580
  0.6 14.3 %copy-start.4 = (s32[2048]{0:T(1024)S(1)}, s32[2048]{0:T(1024)}, u32[]{:S(2)}) copy-start(s32[2048]{0:T(1024)} %param.15) | copy-start | bytes 24580
  0.7 14.2 %copy-start.1 = (f32[2048,128]{1,0:T(8,128)S(1)}, f32[2048,128]{1,0:T(8,128)}, u32[]{:S(2)}) copy-start(f32[2048,128]{1,0:T(8,128)} %pha_ref.1) | copy-start | bytes 3145732
  0.7 14.2 %copy-start.2 = (f32[2048,128]{1,0:T(8,128)S(1)}, f32[2048,128]{1,0:T(8,128)}, u32[]{:S(2)}) copy-start(f32[2048,128]{1,0:T(8,128)} %cal_ref.1) | copy-start | bytes 3145732
  0.7 14.2 %copy-start = (f32[2048,4,128]{2,1,0:T(4,128)S(1)}, f32[2048,4,128]{2,1,0:T(4,128)}, u32[]{:S(2)}) copy-start(f32[2048,4,128]{2,1,0:T(4,128)} %param.10) | copy-start | bytes 12582916
  1.5 25.1 %copy-start.3 = (s32[2048]{0:T(1024)S(1)}, s32[2048]{0:T(1024)}, u32[]{:S(2)}) copy-start(s32[2048]{0:T(1024)} %param.14) | copy-start | bytes 24580
  7.7 2.5 %collective-permute-start = (f32[20,8,256]{2,1,0:T(8,128)S(1)}, f32[20,8,256]{2,1,0:T(8,128)S(1)}, u32[]{:S(2)}, u32[]{:S(2)}) collective-permute-start(f32[20,8,256]{2,1,0:T(8,128)S(1)} %get-tuple-element.24), channel_id=1, source_target_pairs={{0,1},{1,0},{2,3},{3,2},{4,5},{5,4},{6,7},{7,6},{8,9},{9,8},{10,11... | collective-permute-start | bytes 491528 | tf_op jit(solution)/shard_map/ppermute | solution.py:462
  10.2 12.8 %collective-permute-start.3 = (f32[20,8,256]{2,1,0:T(8,128)S(1)}, f32[20,8,256]{2,1,0:T(8,128)S(1)}, u32[]{:S(2)}, u32[]{:S(2)}) collective-permute-start(f32[20,8,256]{2,1,0:T(8,128)S(1)} %join.1.a_ref), channel_id=1, source_target_pairs={{0,6},{2,0},{4,2},{6,4},{1,7},{3,1},{5,3},{7,5},{8,14},{10,8},{12,... | collective-permute-start | bytes 491528 | tf_op jit(solution)/shard_map/ppermute | solution.py:464
  14.2 8.8 %collective-permute-start.2 = (f32[20,8,256]{2,1,0:T(8,128)S(1)}, f32[20,8,256]{2,1,0:T(8,128)S(1)}, u32[]{:S(2)}, u32[]{:S(2)}) collective-permute-start(f32[20,8,256]{2,1,0:T(8,128)S(1)} %join.1.a_ref), channel_id=1, source_target_pairs={{0,4},{2,6},{4,0},{6,2},{1,5},{3,7},{5,1},{7,3},{8,12},{10,14},{12... | collective-permute-start | bytes 491528 | tf_op jit(solution)/shard_map/ppermute | solution.py:464
  14.2 10.6 %collective-permute-start.1 = (f32[20,8,256]{2,1,0:T(8,128)S(1)}, f32[20,8,256]{2,1,0:T(8,128)S(1)}, u32[]{:S(2)}, u32[]{:S(2)}) collective-permute-start(f32[20,8,256]{2,1,0:T(8,128)S(1)} %join.1.a_ref), channel_id=1, source_target_pairs={{0,2},{2,4},{4,6},{6,0},{1,3},{3,5},{5,7},{7,1},{8,10},{10,12},{12... | collective-permute-start | bytes 491528 | tf_op jit(solution)/shard_map/ppermute | solution.py:464
  24.9 1.7 %collective-permute-start.4 = (f32[5,8,256]{2,1,0:T(8,128)S(1)}, f32[5,8,256]{2,1,0:T(8,128)S(1)}, u32[]{:S(2)}, u32[]{:S(2)}) collective-permute-start(f32[5,8,256]{2,1,0:T(8,128)S(1)} %solve.1.mine_ref), channel_id=1, source_target_pairs={{0,1},{1,0},{2,3},{3,2},{4,5},{5,4},{6,7},{7,6},{8,9},{9,8},{10,11... | collective-permute-start | bytes 122888 | tf_op jit(solution)/shard_map/ppermute | solution.py:504
  51.5 2.6 %collective-permute-start.5 = (f32[4,128]{1,0:T(4,128)S(1)}, f32[4,128]{1,0:T(4,128)S(1)}, u32[]{:S(2)}, u32[]{:S(2)}) collective-permute-start(f32[4,128]{1,0:T(4,128)S(1)} %attitude.1), channel_id=1, source_target_pairs={{0,1},{1,0},{2,3},{3,2},{4,5},{5,4},{6,7},{7,6},{8,9},{9,8},{10,11... | collective-permute-start | bytes 6152 | tf_op jit(solution)/shard_map/ppermute | solution.py:537

commit v4 on v3

--- a/solution.py
+++ b/solution.py
@@ -6,8 +6,7 @@
 from jax.sharding import PartitionSpec as P
 
 BLK = 2048
-NB = 256
-STEPS = BLK // NB
+CUT = 256
 WIDE = 512
 WIDE_STEPS = BLK // WIDE
 OBS = 128
@@ -202,18 +201,24 @@
     acc_ref, slot_ref, carry_ref,
 ):
     step = pl.program_id(0)
-    span = columns(step, NB)
+    span = columns(step, WIDE)
     extra_ref = all_extra_ref.at[:, :, span]
-    live = live_row(live_ref, step, NB)
+    live = live_row(live_ref, step, WIDE)
     unit = unit_ref[0]
     owner = rows_equal(RANGES, unit >> 12)
     owner_low = owner.astype(BF16)
     all_owner_ref[:, span] = owner_low
-    before = lax.broadcasted_iota(jnp.int32, (NB, NB), 0) < lax.broadcasted_iota(jnp.int32, (NB, NB), 1)
+    before = lax.broadcasted_iota(jnp.int32, (CUT, CUT), 0) < lax.broadcasted_iota(jnp.int32, (CUT, CUT), 1)
     before = jnp.where(before, 1.0, 0.0).astype(BF16)
-    earlier = dot_nn(owner_low, before) + jnp.where(step > 0, carry_ref[...], 0.0)
-    rank = column_sum(owner * earlier).astype(jnp.int32)
-    accumulate(carry_ref, dot_nn(owner_low, jnp.ones((NB, NB), BF16)), step)
+    carry = jnp.where(step > 0, carry_ref[...], 0.0)
+    ranks = []
+    for h in range(WIDE // CUT):
+        part = slice(h * CUT, (h + 1) * CUT)
+        earlier = dot_nn(owner_low[:, part], before) + carry
+        ranks.append(column_sum(owner[:, part] * earlier))
+        carry = carry + dot_nn(owner_low[:, part], jnp.ones((CUT, CUT), BF16))
+    carry_ref[...] = carry
+    rank = jnp.concatenate(ranks, axis=1).astype(jnp.int32)
     place = rows_equal(CAP, rank)
     place_live = (place * live).astype(BF16)
     all_place_ref[:, span] = place_live
@@ -224,7 +229,7 @@
     all_low_ref[:, span] = seg_low
     groups = []
     units = []
-    for h in range(NB // 128):
+    for h in range(WIDE // 128):
         lanes = slice(h * 128, (h + 1) * 128)
         for c in range(4):
             extra_ref[c, :, lanes] = att_ref[pl.ds(h * 512 + c, 128, stride=4), :].T
@@ -251,7 +256,7 @@
     )
     accumulate(slot_ref, repeated_dot(left, owner_low, 2), step)
 
-    @pl.when(step == STEPS - 1)
+    @pl.when(step == WIDE_STEPS - 1)
     def _():
         for c in range(4):
             knots_ref[c] = knots_of([acc_ref[(j * 4 + c) * 16 : (j * 4 + c) * 16 + 16] for j in range(4)])
@@ -398,7 +403,6 @@
 
 VMEM = pl.BlockSpec(memory_space=pltpu.VMEM)
 SMEM = pl.BlockSpec(memory_space=pltpu.SMEM)
-ROW = pl.BlockSpec((1, 1, NB), lambda s: (s, 0, 0))
 WIDE_ROW = pl.BlockSpec((1, 1, WIDE), lambda s: (s, 0, 0))
 
 
@@ -426,8 +430,8 @@
     live_blocks,
 ):
     source = block_source.reshape(WIDE_STEPS, 1, WIDE)
-    segment = block_segment.reshape(STEPS, 1, NB)
-    unit = block_unit.reshape(STEPS, 1, NB)
+    segment = block_segment.reshape(WIDE_STEPS, 1, WIDE)
+    unit = block_unit.reshape(WIDE_STEPS, 1, WIDE)
     src = jnp.transpose(src_partials, (1, 0, 2))
     att = att_partials.reshape(BLK * 4, OBS)
     sequential = pltpu.CompilerParams(dimension_semantics=("arbitrary",), vmem_limit_bytes=24 * 1024 * 1024)
@@ -461,17 +465,17 @@
         name="join",
     )(*on_chip(keep, lax.ppermute(send, "fov", [(0, 1), (1, 0)])))
     half, live_later = lax.optimization_barrier((half, live_blocks))
-    around = [lax.ppermute(half, "tm", [(i, (i + d) % 4) for i in range(4)]) for d in (1, 2, 3)]
+    around = [lax.ppermute(half, "tm", [(i, i ^ d) for i in range(4)]) for d in (1, 2, 3)]
     extra, seg_low, owner, seg_high, place, diag_knots, diag_slots = pl.pallas_call(
         diag_kernel,
-        grid=(STEPS,),
+        grid=(WIDE_STEPS,),
         in_specs=[
             SMEM,
-            pl.BlockSpec((NB * 4, OBS), lambda s: (s, 0)),
-            pl.BlockSpec((NB, OBS), lambda s: (s, 0)),
-            pl.BlockSpec((NB, OBS), lambda s: (s, 0)),
-            ROW,
-            ROW,
+            pl.BlockSpec((WIDE * 4, OBS), lambda s: (s, 0)),
+            pl.BlockSpec((WIDE, OBS), lambda s: (s, 0)),
+            pl.BlockSpec((WIDE, OBS), lambda s: (s, 0)),
+            WIDE_ROW,
+            WIDE_ROW,
         ],
         out_specs=[VMEM] * 7,
         out_shape=[
@@ -486,7 +490,7 @@
         scratch_shapes=[
             pltpu.VMEM((256, 128), F32),
             pltpu.VMEM((64, RANGES), F32),
-            pltpu.VMEM((RANGES, NB), F32),
+            pltpu.VMEM((RANGES, CUT), F32),
         ],
         compiler_params=sequential,
         cost_estimate=pl.CostEstimate(flops=200_000_000, bytes_accessed=12_000_000, transcendentals=0),

time: 54.8 us -> 54.7 us (level)
  Pallas kernels: 22.2 us -> 19.4 us
  blocking collectives: 18.6 us -> 20.4 us
    pallas_call x1, Pallas kernels: 8.1 us -> 5.33 us  [shards(): pl.pallas_call(diag_kernel, grid=(WIDE_STEPS,), in_specs=[SMEM, pl.BlockS...]
    all_to_all x1, blocking collectives: 18.6 us -> 20.4 us  [shards(): lax.all_to_all(outgoing.reshape(128, 1, PIECES * 128), ALL, split_axis=0,...]
  transfers between devices with their start and end apart: 6 -> 6, of which waited for: 3 -> 4; matrix products, arithmetic and copies ran while one was open for 0% -> 0% of each run, Pallas kernels for 17% -> 12%
where the time goes in v4:
time: 54.7 us; the launch traced here: 54.5 us
  blocking collectives  20.4 us (37%)
  Pallas kernels  19.4 us (35%)
  starting transfers between devices  8.57 us (16%)
  waiting for transfers between devices  4.02 us (7%)
  between operations  1.52 us (3%)
  other arithmetic  0.58 us (1%)
    all_to_all x1, blocking collectives, shards(): lax.all_to_all(outgoing.reshape(128, 1, PIECES * 128), ALL, split_axis=0,...  20.4 us
    pallas_call x1, Pallas kernels, shards(): pl.pallas_call(normals_kernel, grid=(WIDE_STEPS,), in_specs=[SMEM, pl.Blo...  6.23 us
    pallas_call x1, Pallas kernels, shards(): pl.pallas_call(apply_kernel, grid=(WIDE_STEPS,), in_specs=[VMEM] * 7 + [W...  6.13 us
    pallas_call x1, Pallas kernels, shards(): pl.pallas_call(diag_kernel, grid=(WIDE_STEPS,), in_specs=[SMEM, pl.BlockS...  5.33 us
    ppermute x3, starting transfers between devices, shards(): lax.ppermute(half, 'tm', [(i, i ^ d) for i in range(4)])  4.62 us
    ppermute x3, waiting for transfers between devices, shards(): lax.ppermute(half, 'tm', [(i, i ^ d) for i in range(4)])  2.12 us
    ppermute x1, starting transfers between devices, shards(): lax.ppermute(send, 'fov', [(0, 1), (1, 0)])  1.47 us
    pallas_call x1, Pallas kernels, shards(): pl.pallas_call(calibration_kernel, in_specs=[VMEM], out_specs=VMEM, out_s...  1.43 us
  transfers between devices with their start and end apart: 6, of which 4 were waited for; matrix products, arithmetic and copies ran while one was open for 0% of the time, Pallas kernels for 12%

profile of v4, /device:TPU:1, one launch (start us, length us, event | category | flops | bytes accessed | tf_op | source)
XLA Modules:
  0.0 54.5 jit_solution(2549790447844022796)
XLA Ops:
  0.6 0.0 copy-start.5
  0.6 0.0 copy-start.4
  0.7 0.0 copy-start.1
  0.7 0.0 copy-start.2
  0.7 0.0 copy-start
  1.5 0.0 copy-start.3
  1.5 6.2 %normals.1 = (f32[20,8,256]{2,1,0:T(8,128)S(1)}, f32[20,8,256]{2,1,0:T(8,128)S(1)}, f32[6,128,2048]{2,1,0:T(8,128)S(1)}, bf16[256,2048]{1,0:T(8,128)(2,1)S(1)}) custom-call(s32[1]{0:T(128)S(6)} %copy.15.live_ref, f32[5,2048,128]{2,1,0:T(8,128)} %bitcast.19, f32[2048,128]{1,0:T(8,128)} %res_ref.1, s32[4,1,512]{2,1,0:T(1,128)} %bitcast.15), custom_call_target="tpu_custom_call" | custom-call | tf_op jit(solution)/shard_map/normals/pallas_call | solution.py:439
  7.7 1.5 %collective-permute-start = (f32[20,8,256]{2,1,0:T(8,128)S(1)}, f32[20,8,256]{2,1,0:T(8,128)S(1)}, u32[]{:S(2)}, u32[]{:S(2)}) collective-permute-start(f32[20,8,256]{2,1,0:T(8,128)S(1)} %get-tuple-element.24), channel_id=1, source_target_pairs={{0,1},{1,0},{2,3},{3,2},{4,5},{5,4},{6,7},{7,6},{8,9},{9,8},{10,11... | collective-permute-start | bytes 491528 | tf_op jit(solution)/shard_map/ppermute | solution.py:466
  9.2 1.0 %collective-permute-done.b_ref = f32[20,8,256]{2,1,0:T(8,128)S(1)} collective-permute-done((f32[20,8,256]{2,1,0:T(8,128)S(1)}, f32[20,8,256]{2,1,0:T(8,128)S(1)}, u32[]{:S(2)}, u32[]{:S(2)}) %collective-permute-start) | collective-permute-done | bytes 163872 | tf_op jit(solution)/shard_map/ppermute | solution.py:466
  10.2 4.0 %collective-permute-start.3 = (f32[20,8,256]{2,1,0:T(8,128)S(1)}, f32[20,8,256]{2,1,0:T(8,128)S(1)}, u32[]{:S(2)}, u32[]{:S(2)}) collective-permute-start(f32[20,8,256]{2,1,0:T(8,128)S(1)} %join.1.a_ref), channel_id=1, source_target_pairs={{0,6},{2,4},{4,2},{6,0},{1,7},{3,5},{5,3},{7,1},{8,14},{10,12},{12... | collective-permute-start | bytes 491528 | tf_op jit(solution)/shard_map/ppermute | solution.py:468
  14.2 0.0 collective-permute-start.2
  14.2 0.7 %collective-permute-start.1 = (f32[20,8,256]{2,1,0:T(8,128)S(1)}, f32[20,8,256]{2,1,0:T(8,128)S(1)}, u32[]{:S(2)}, u32[]{:S(2)}) collective-permute-start(f32[20,8,256]{2,1,0:T(8,128)S(1)} %join.1.a_ref), channel_id=1, source_target_pairs={{0,2},{2,0},{4,6},{6,4},{1,3},{3,1},{5,7},{7,5},{8,10},{10,8},{12,... | collective-permute-start | bytes 491528 | tf_op jit(solution)/shard_map/ppermute | solution.py:468
  14.9 0.0 copy-done.5
  14.9 0.0 copy-done.4
  14.9 0.0 copy-done.1
  14.9 0.0 copy-done.2
  14.9 0.0 copy-done
  14.9 5.3 %diag.1 = (f32[6,128,2048]{2,1,0:T(8,128)S(1)}, bf16[128,2048]{1,0:T(8,128)(2,1)S(1)}, bf16[128,2048]{1,0:T(8,128)(2,1)S(1)}, bf16[16,2048]{1,0:T(8,128)(2,1)S(1...) custom-call(s32[1]{0:T(128)S(6)} %copy.15.live_ref, f32[8192,128]{1,0:T(8,128)S(1)} %bitcast.11, ...), custom_call_target="tpu_custom_call" | custom-call | flops 200000000 | bytes 12000000 | tf_op jit(solution)/shard_map/diag/pallas_call | solution.py:469
  20.2 1.0 %collective-permute-done.3.d_ref = f32[20,8,256]{2,1,0:T(8,128)S(1)} collective-permute-done((f32[20,8,256]{2,1,0:T(8,128)S(1)}, f32[20,8,256]{2,1,0:T(8,128)S(1)}, u32[]{:S(2)}, u32[]{:S(2)}) %collective-permute-start.3) | collective-permute-done | bytes 163872 | tf_op jit(solution)/shard_map/ppermute | solution.py:468
  21.2 0.0 collective-permute-done.2.c_ref
  21.2 1.1 %collective-permute-done.1.b_ref = f32[20,8,256]{2,1,0:T(8,128)S(1)} collective-permute-done((f32[20,8,256]{2,1,0:T(8,128)S(1)}, f32[20,8,256]{2,1,0:T(8,128)S(1)}, u32[]{:S(2)}, u32[]{:S(2)}) %collective-permute-start.1) | collective-permute-done | bytes 163872 | tf_op jit(solution)/shard_map/ppermute | solution.py:468
  22.4 0.1 solve.1.mine_ref
  22.5 1.3 %collective-permute-start.4 = (f32[5,8,256]{2,1,0:T(8,128)S(1)}, f32[5,8,256]{2,1,0:T(8,128)S(1)}, u32[]{:S(2)}, u32[]{:S(2)}) collective-permute-start(f32[5,8,256]{2,1,0:T(8,128)S(1)} %solve.1.mine_ref), channel_id=1, source_target_pairs={{0,1},{1,0},{2,3},{3,2},{4,5},{5,4},{6,7},{7,6},{8,9},{9,8},{10,11... | collective-permute-start | bytes 122888 | tf_op jit(solution)/shard_map/ppermute | solution.py:508
  23.8 0.9 %collective-permute-done.4.other_ref = f32[5,8,256]{2,1,0:T(8,128)S(1)} collective-permute-done((f32[5,8,256]{2,1,0:T(8,128)S(1)}, f32[5,8,256]{2,1,0:T(8,128)S(1)}, u32[]{:S(2)}, u32[]{:S(2)}) %collective-permute-start.4) | collective-permute-done | bytes 40992 | tf_op jit(solution)/shard_map/ppermute | solution.py:508
  24.7 0.0 copy-done.3
  24.7 6.1 %apply.1 = (f32[640,128]{1,0:T(8,128)S(1)}, f32[5,4096]{1,0:T(8,128)}) custom-call(f32[6,128,2048]{2,1,0:T(8,128)S(1)} %get-tuple-element.22.all_src_ref, f32[6,128,2048]{2,1,0:T(8,128)S(1)} %get-tuple-element.26.all_extra_ref, bf16[256,2048]{1,0:T(8,128)(2,1)S(1)} %get-tuple-element.27.src_low_ref, bf16[128,2048]{1,0:T(8,128)(2,1)S(1)} %get-tuple-element.28.seg_low_ref, ...), custom_call_target="tpu_custom_call" | custom-call | tf_op jit(solution)/shard_map/apply/pallas_call | solution.py:509
  30.8 20.4 %all_to_all.5 = f32[128,1,640]{2,1,0:T(1,128)S(1)} all-to-all(f32[128,1,640]{2,1,0:T(1,128)S(1)} %bitcast.14), channel_id=1, replica_groups=mesh['sky'=16,'tm'=4,'fov'=2] {'sky','tm','fov'}, dimensions={0} | all-to-all | bytes 655360 | tf_op jit(solution)/shard_map/all_to_all | solution.py:530
  51.2 0.1 attitude.1
  51.4 1.2 %collective-permute-start.5 = (f32[4,128]{1,0:T(4,128)S(1)}, f32[4,128]{1,0:T(4,128)S(1)}, u32[]{:S(2)}, u32[]{:S(2)}) collective-permute-start(f32[4,128]{1,0:T(4,128)S(1)} %attitude.1), channel_id=1, source_target_pairs={{0,1},{1,0},{2,3},{3,2},{4,5},{5,4},{6,7},{7,6},{8,9},{9,8},{10,11... | collective-permute-start | bytes 6152 | tf_op jit(solution)/shard_map/ppermute | solution.py:541
  52.5 1.4 %calibration.1 = f32[32,128]{1,0:T(8,128)} custom-call(f32[640,128]{1,0:T(8,128)S(1)} %bitcast.13), custom_call_target="tpu_custom_call" | custom-call | flops 100000000 | bytes 400000 | tf_op jit(solution)/shard_map/calibration/pallas_call | solution.py:542
  54.0 0.0 collective-permute-done.5
  54.0 0.6 %add.3 = f32[4,128]{1,0:T(4,128)} add(f32[4,128]{1,0:T(4,128)S(1)} %attitude.1, f32[4,128]{1,0:T(4,128)S(1)} %collective-permute-done.5) | non-fusion elementwise | flops 512 | bytes 6144 | tf_op jit(solution)/shard_map/add | solution.py:551
  (1 shorter events, 0.0 us)
Async XLA Ops:
  0.6 14.2 %copy-start.5 = (s32[2048]{0:T(1024)S(1)}, s32[2048]{0:T(1024)}, u32[]{:S(2)}) copy-start(s32[2048]{0:T(1024)} %param.16) | copy-start | bytes 24580
  0.6 14.2 %copy-start.4 = (s32[2048]{0:T(1024)S(1)}, s32[2048]{0:T(1024)}, u32[]{:S(2)}) copy-start(s32[2048]{0:T(1024)} %param.15) | copy-start | bytes 24580
  0.7 14.2 %copy-start.1 = (f32[2048,128]{1,0:T(8,128)S(1)}, f32[2048,128]{1,0:T(8,128)}, u32[]{:S(2)}) copy-start(f32[2048,128]{1,0:T(8,128)} %pha_ref.1) | copy-start | bytes 3145732
  0.7 14.2 %copy-start.2 = (f32[2048,128]{1,0:T(8,128)S(1)}, f32[2048,128]{1,0:T(8,128)}, u32[]{:S(2)}) copy-start(f32[2048,128]{1,0:T(8,128)} %cal_ref.1) | copy-start | bytes 3145732
  0.7 14.2 %copy-start = (f32[2048,4,128]{2,1,0:T(4,128)S(1)}, f32[2048,4,128]{2,1,0:T(4,128)}, u32[]{:S(2)}) copy-start(f32[2048,4,128]{2,1,0:T(4,128)} %param.10) | copy-start | bytes 12582916
  1.5 23.2 %copy-start.3 = (s32[2048]{0:T(1024)S(1)}, s32[2048]{0:T(1024)}, u32[]{:S(2)}) copy-start(s32[2048]{0:T(1024)} %param.14) | copy-start | bytes 24580
  7.7 2.5 %collective-permute-start = (f32[20,8,256]{2,1,0:T(8,128)S(1)}, f32[20,8,256]{2,1,0:T(8,128)S(1)}, u32[]{:S(2)}, u32[]{:S(2)}) collective-permute-start(f32[20,8,256]{2,1,0:T(8,128)S(1)} %get-tuple-element.24), channel_id=1, source_target_pairs={{0,1},{1,0},{2,3},{3,2},{4,5},{5,4},{6,7},{7,6},{8,9},{9,8},{10,11... | collective-permute-start | bytes 491528 | tf_op jit(solution)/shard_map/ppermute | solution.py:466
  10.2 11.0 %collective-permute-start.3 = (f32[20,8,256]{2,1,0:T(8,128)S(1)}, f32[20,8,256]{2,1,0:T(8,128)S(1)}, u32[]{:S(2)}, u32[]{:S(2)}) collective-permute-start(f32[20,8,256]{2,1,0:T(8,128)S(1)} %join.1.a_ref), channel_id=1, source_target_pairs={{0,6},{2,4},{4,2},{6,0},{1,7},{3,5},{5,3},{7,1},{8,14},{10,12},{12... | collective-permute-start | bytes 491528 | tf_op jit(solution)/shard_map/ppermute | solution.py:468
  14.2 7.0 %collective-permute-start.2 = (f32[20,8,256]{2,1,0:T(8,128)S(1)}, f32[20,8,256]{2,1,0:T(8,128)S(1)}, u32[]{:S(2)}, u32[]{:S(2)}) collective-permute-start(f32[20,8,256]{2,1,0:T(8,128)S(1)} %join.1.a_ref), channel_id=1, source_target_pairs={{0,4},{2,6},{4,0},{6,2},{1,5},{3,7},{5,1},{7,3},{8,12},{10,14},{12... | collective-permute-start | bytes 491528 | tf_op jit(solution)/shard_map/ppermute | solution.py:468
  14.2 8.1 %collective-permute-start.1 = (f32[20,8,256]{2,1,0:T(8,128)S(1)}, f32[20,8,256]{2,1,0:T(8,128)S(1)}, u32[]{:S(2)}, u32[]{:S(2)}) collective-permute-start(f32[20,8,256]{2,1,0:T(8,128)S(1)} %join.1.a_ref), channel_id=1, source_target_pairs={{0,2},{2,0},{4,6},{6,4},{1,3},{3,1},{5,7},{7,5},{8,10},{10,8},{12,... | collective-permute-start | bytes 491528 | tf_op jit(solution)/shard_map/ppermute | solution.py:468
  22.5 2.2 %collective-permute-start.4 = (f32[5,8,256]{2,1,0:T(8,128)S(1)}, f32[5,8,256]{2,1,0:T(8,128)S(1)}, u32[]{:S(2)}, u32[]{:S(2)}) collective-permute-start(f32[5,8,256]{2,1,0:T(8,128)S(1)} %solve.1.mine_ref), channel_id=1, source_target_pairs={{0,1},{1,0},{2,3},{3,2},{4,5},{5,4},{6,7},{7,6},{8,9},{9,8},{10,11... | collective-permute-start | bytes 122888 | tf_op jit(solution)/shard_map/ppermute | solution.py:508
  51.4 2.6 %collective-permute-start.5 = (f32[4,128]{1,0:T(4,128)S(1)}, f32[4,128]{1,0:T(4,128)S(1)}, u32[]{:S(2)}, u32[]{:S(2)}) collective-permute-start(f32[4,128]{1,0:T(4,128)S(1)} %attitude.1), channel_id=1, source_target_pairs={{0,1},{1,0},{2,3},{3,2},{4,5},{5,4},{6,7},{7,6},{8,9},{9,8},{10,11... | collective-permute-start | bytes 6152 | tf_op jit(solution)/shard_map/ppermute | solution.py:541

commit v5 on v4

--- a/solution.py
+++ b/solution.py
@@ -9,6 +9,8 @@
 CUT = 256
 WIDE = 512
 WIDE_STEPS = BLK // WIDE
+LONG = 1024
+LONG_STEPS = BLK // LONG
 OBS = 128
 CAP = 32
 RANGES = 128
@@ -149,29 +151,32 @@
     span = columns(step, WIDE)
     srct_ref = all_src_ref.at[:, :, span]
     idx = idx_ref[0] ^ (lax.axis_index("fov") * 2048)
-    high = (rows_equal(16, idx >> 8) * live_row(live_ref, step, WIDE)).astype(BF16)
-    low = narrow_rows_equal(256, idx & 255)
-    all_low_ref[:, span] = low
-    groups = []
-    spare = []
-    for h in range(WIDE // 128):
-        lanes = slice(h * 128, (h + 1) * 128)
-        for i in range(5):
-            srct_ref[i, :, lanes] = src_ref[i, lanes, :].T
-        srct_ref[5, :, lanes] = res_ref[lanes, :].T
-        sums = [None] * 20
-        for o in range(OBS // 8):
-            rows = [srct_ref[i, o * 8 : o * 8 + 8, lanes] for i in range(6)]
-            terms = [rows[i] * rows[j] for i, j in index_pairs] + [rows[i] * rows[5] for i in range(5)]
-            sums = terms if o == 0 else [s + t for s, t in zip(sums, terms)]
-        groups.append(jnp.concatenate([fold(sums[:8]), fold(sums[8:16])], axis=0))
-        spare.append(sums[16:])
-    rest = []
-    for h in range(0, WIDE // 128, 2):
-        both = fold(spare[h] + spare[h + 1])
-        rest += [both[:4], both[4:]]
-    blocks = [jnp.concatenate(groups, axis=1), jnp.concatenate(rest, axis=1)]
-    accumulate(acc_ref, repeated_dot(masked_rows(high, blocks, 3), low, 3), step)
+    live = live_row(live_ref, step, WIDE)
+    total = None
+    for part in range(WIDE // CUT):
+        cut = slice(part * CUT, (part + 1) * CUT)
+        high = (rows_equal(16, idx[:, cut] >> 8) * live[:, cut]).astype(BF16)
+        low = narrow_rows_equal(256, idx[:, cut] & 255)
+        all_low_ref[:, columns(step * (WIDE // CUT) + part, CUT)] = low
+        groups = []
+        spare = []
+        for h in range(CUT // 128):
+            lanes = slice(part * CUT + h * 128, part * CUT + (h + 1) * 128)
+            for i in range(5):
+                srct_ref[i, :, lanes] = src_ref[i, lanes, :].T
+            srct_ref[5, :, lanes] = res_ref[lanes, :].T
+            sums = [None] * 20
+            for o in range(OBS // 8):
+                rows = [srct_ref[i, o * 8 : o * 8 + 8, lanes] for i in range(6)]
+                terms = [rows[i] * rows[j] for i, j in index_pairs] + [rows[i] * rows[5] for i in range(5)]
+                sums = terms if o == 0 else [s + t for s, t in zip(sums, terms)]
+            groups.append(jnp.concatenate([fold(sums[:8]), fold(sums[8:16])], axis=0))
+            spare.append(sums[16:])
+        both = fold(spare[0] + spare[1])
+        blocks = [jnp.concatenate(groups, axis=1), jnp.concatenate([both[:4], both[4:]], axis=1)]
+        product = repeated_dot(masked_rows(high, blocks, 3), low, 3)
+        total = product if part == 0 else total + product
+    accumulate(acc_ref, total, step)
 
     @pl.when(step == WIDE_STEPS - 1)
     def _():
@@ -303,7 +308,7 @@
     mine_ref, other_ref, diag_ref, slots_ref, out_ref, update_ref, table_ref, acc_ref, slot_ref,
 ):
     step = pl.program_id(0)
-    span = columns(step, WIDE)
+    span = columns(step, LONG)
     srct_ref = all_src_ref.at[:, :, span]
     extra_ref = all_extra_ref.at[:, :, span]
     fov = lax.axis_index("fov")
@@ -322,41 +327,50 @@
                 update_ref[k : k + 1, q * 256 : (q + 1) * 256] = first[q : q + 1]
                 update_ref[k : k + 1, 2048 + q * 256 : 2048 + (q + 1) * 256] = second[q : q + 1]
         stacked = jnp.concatenate(pieces, axis=0)
-        table_ref[...] = jnp.concatenate(split_parts(stacked, 3), axis=1)
+        table_ref[...] = jnp.concatenate(split_parts(stacked, 3), axis=0)
 
     idx = idx_ref[0] ^ (fov * 2048)
-    high = rows_equal(16, idx >> 8)
-    low = src_low_ref[:, span]
-    looked = dot_nn(table_ref[...], jnp.concatenate([low] * 3, axis=0))
-    chosen = [column_sum(looked[k * 16 : k * 16 + 16] * high) for k in range(5)]
-    groups = []
-    units = []
-    for h in range(WIDE // 128):
-        lanes = slice(h * 128, (h + 1) * 128)
-        spread = [jnp.broadcast_to(chosen[k][:, lanes], (8, 128)) for k in range(5)]
-        sums = [None] * 17
-        for o in range(OBS // 8):
-            rows = slice(o * 8, o * 8 + 8)
-            model = srct_ref[0, rows, lanes] * spread[0]
-            for k in range(1, 5):
-                model = model + srct_ref[k, rows, lanes] * spread[k]
-            residual = srct_ref[5, rows, lanes] - model
-            phase = extra_ref[4, rows, lanes]
-            moments = [extra_ref[c, rows, lanes] * residual for c in range(4)]
-            terms = list(moments)
-            for _ in range(3):
-                moments = [m * phase for m in moments]
-                terms += moments
-            terms.append(extra_ref[5, rows, lanes] * residual)
-            sums = terms if o == 0 else [s + t for s, t in zip(sums, terms)]
-        groups.append(jnp.concatenate([fold(sums[:8]), fold(sums[8:16])], axis=0))
-        units.append(column_sum(sums[16]))
-    left = masked_rows(seg_high_ref[:, span], [jnp.concatenate(groups, axis=1)], 2)
-    accumulate(acc_ref, repeated_dot(left, seg_low_ref[:, span], 2), step)
-    left = masked_rows(place_ref[:, span], [jnp.concatenate(units, axis=1)], 2)
-    accumulate(slot_ref, repeated_dot(left, owner_ref[:, span], 2), step)
-
-    @pl.when(step == WIDE_STEPS - 1)
+    knot_sums = None
+    slot_sums = None
+    for part in range(LONG // CUT):
+        cut = slice(part * CUT, (part + 1) * CUT)
+        place = columns(step * (LONG // CUT) + part, CUT)
+        high = rows_equal(16, idx[:, cut] >> 8)
+        looked = dot_nn(table_ref[...], src_low_ref[:, place])
+        looked = looked[:80] + looked[80:160] + looked[160:]
+        chosen = [column_sum(looked[k * 16 : k * 16 + 16] * high) for k in range(5)]
+        groups = []
+        units = []
+        for h in range(CUT // 128):
+            lanes = slice(part * CUT + h * 128, part * CUT + (h + 1) * 128)
+            spread = [jnp.broadcast_to(chosen[k][:, h * 128 : (h + 1) * 128], (8, 128)) for k in range(5)]
+            sums = [None] * 17
+            for o in range(OBS // 8):
+                rows = slice(o * 8, o * 8 + 8)
+                model = srct_ref[0, rows, lanes] * spread[0]
+                for k in range(1, 5):
+                    model = model + srct_ref[k, rows, lanes] * spread[k]
+                residual = srct_ref[5, rows, lanes] - model
+                phase = extra_ref[4, rows, lanes]
+                moments = [extra_ref[c, rows, lanes] * residual for c in range(4)]
+                terms = list(moments)
+                for _ in range(3):
+                    moments = [m * phase for m in moments]
+                    terms += moments
+                terms.append(extra_ref[5, rows, lanes] * residual)
+                sums = terms if o == 0 else [s + t for s, t in zip(sums, terms)]
+            groups.append(jnp.concatenate([fold(sums[:8]), fold(sums[8:16])], axis=0))
+            units.append(column_sum(sums[16]))
+        left = masked_rows(seg_high_ref[:, place], [jnp.concatenate(groups, axis=1)], 2)
+        knot_part = repeated_dot(left, seg_low_ref[:, place], 2)
+        left = masked_rows(place_ref[:, place], [jnp.concatenate(units, axis=1)], 2)
+        slot_part = repeated_dot(left, owner_ref[:, place], 2)
+        knot_sums = knot_part if part == 0 else knot_sums + knot_part
+        slot_sums = slot_part if part == 0 else slot_sums + slot_part
+    accumulate(acc_ref, knot_sums, step)
+    accumulate(slot_ref, slot_sums, step)
+
+    @pl.when(step == LONG_STEPS - 1)
     def _():
         tm = lax.axis_index("tm")
         slots = jnp.concatenate([slot_ref[...], slots_ref[...], jnp.zeros((CAP, RANGES), F32)], axis=0)
@@ -403,6 +417,7 @@
 
 VMEM = pl.BlockSpec(memory_space=pltpu.VMEM)
 SMEM = pl.BlockSpec(memory_space=pltpu.SMEM)
+LONG_ROW = pl.BlockSpec((1, 1, LONG), lambda s: (s, 0, 0))
 WIDE_ROW = pl.BlockSpec((1, 1, WIDE), lambda s: (s, 0, 0))
 
 
@@ -508,15 +523,15 @@
     other = lax.ppermute(mine, "fov", [(0, 1), (1, 0)])
     outgoing, src_update = pl.pallas_call(
         apply_kernel,
-        grid=(WIDE_STEPS,),
-        in_specs=[VMEM] * 7 + [WIDE_ROW] + [VMEM] * 4,
+        grid=(LONG_STEPS,),
+        in_specs=[VMEM] * 7 + [LONG_ROW] + [VMEM] * 4,
         out_specs=[VMEM, whole((5, 4096))],
         out_shape=[
             pltpu.VMEM((128 * PIECES, 128), F32),
             jax.ShapeDtypeStruct((5, 4096), F32),
         ],
         scratch_shapes=[
-            pltpu.VMEM((80, 768), BF16),
+            pltpu.VMEM((240, 256), BF16),
             pltpu.VMEM((256, 128), F32),
             pltpu.VMEM((CAP, RANGES), F32),
         ],
@@ -524,7 +539,7 @@
         name="apply",
     )(
         *on_chip(srct, extra, src_low, seg_low, owner, seg_high, place),
-        source,
+        source.reshape(LONG_STEPS, 1, LONG),
         *on_chip(mine, other, diag_knots, diag_slots),
     )
     arrived = lax.all_to_all(

time: 54.7 us -> 53.4 us (0.976)
  Pallas kernels: 19.4 us -> 18.1 us
    pallas_call x1, Pallas kernels: 6.13 us -> 4.89 us  [shards(): pl.pallas_call(apply_kernel, grid=(LONG_STEPS,), in_specs=[VMEM] * 7 + [L...]
  transfers between devices with their start and end apart: 6 -> 6, of which waited for: 4 -> 4; matrix products, arithmetic and copies ran while one was open for 0% -> 0% of each run, Pallas kernels for 12% -> 13%
where the time goes in v5:
time: 53.4 us; the launch traced here: 53.3 us
  blocking collectives  20.5 us (38%)
  Pallas kernels  18.1 us (34%)
  starting transfers between devices  8.57 us (16%)
  waiting for transfers between devices  4.02 us (8%)
  between operations  1.52 us (3%)
  other arithmetic  0.58 us (1%)
    all_to_all x1, blocking collectives, shards(): lax.all_to_all(outgoing.reshape(128, 1, PIECES * 128), ALL, split_axis=0,...  20.5 us
    pallas_call x1, Pallas kernels, shards(): pl.pallas_call(normals_kernel, grid=(WIDE_STEPS,), in_specs=[SMEM, pl.Blo...  6.21 us
    pallas_call x1, Pallas kernels, shards(): pl.pallas_call(diag_kernel, grid=(WIDE_STEPS,), in_specs=[SMEM, pl.BlockS...  5.33 us
    pallas_call x1, Pallas kernels, shards(): pl.pallas_call(apply_kernel, grid=(LONG_STEPS,), in_specs=[VMEM] * 7 + [L...  4.89 us
    ppermute x3, starting transfers between devices, shards(): lax.ppermute(half, 'tm', [(i, i ^ d) for i in range(4)])  4.62 us
    ppermute x3, waiting for transfers between devices, shards(): lax.ppermute(half, 'tm', [(i, i ^ d) for i in range(4)])  2.12 us
    ppermute x1, starting transfers between devices, shards(): lax.ppermute(send, 'fov', [(0, 1), (1, 0)])  1.46 us
    pallas_call x1, Pallas kernels, shards(): pl.pallas_call(calibration_kernel, in_specs=[VMEM], out_specs=VMEM, out_s...  1.43 us
  transfers between devices with their start and end apart: 6, of which 4 were waited for; matrix products, arithmetic and copies ran while one was open for 0% of the time, Pallas kernels for 13%

profile of v5, /device:TPU:1, one launch (start us, length us, event | category | flops | bytes accessed | tf_op | source)
XLA Modules:
  0.0 53.3 jit_solution(11271236416656447567)
XLA Ops:
  0.6 0.0 copy-start.5
  0.6 0.0 copy-start.4
  0.7 0.0 copy-start.1
  0.7 0.0 copy-start.2
  0.7 0.0 copy-start
  1.5 0.0 copy-start.3
  1.5 6.2 %normals.1 = (f32[20,8,256]{2,1,0:T(8,128)S(1)}, f32[20,8,256]{2,1,0:T(8,128)S(1)}, f32[6,128,2048]{2,1,0:T(8,128)S(1)}, bf16[256,2048]{1,0:T(8,128)(2,1)S(1)}) custom-call(s32[1]{0:T(128)S(6)} %copy.15.live_ref, f32[5,2048,128]{2,1,0:T(8,128)} %bitcast.20, f32[2048,128]{1,0:T(8,128)} %res_ref.1, s32[4,1,512]{2,1,0:T(1,128)} %bitcast.16), custom_call_target="tpu_custom_call" | custom-call | tf_op jit(solution)/shard_map/normals/pallas_call | solution.py:454
  7.7 1.5 %collective-permute-start = (f32[20,8,256]{2,1,0:T(8,128)S(1)}, f32[20,8,256]{2,1,0:T(8,128)S(1)}, u32[]{:S(2)}, u32[]{:S(2)}) collective-permute-start(f32[20,8,256]{2,1,0:T(8,128)S(1)} %get-tuple-element.24), channel_id=1, source_target_pairs={{0,1},{1,0},{2,3},{3,2},{4,5},{5,4},{6,7},{7,6},{8,9},{9,8},{10,11... | collective-permute-start | bytes 491528 | tf_op jit(solution)/shard_map/ppermute | solution.py:481
  9.2 1.0 %collective-permute-done.b_ref = f32[20,8,256]{2,1,0:T(8,128)S(1)} collective-permute-done((f32[20,8,256]{2,1,0:T(8,128)S(1)}, f32[20,8,256]{2,1,0:T(8,128)S(1)}, u32[]{:S(2)}, u32[]{:S(2)}) %collective-permute-start) | collective-permute-done | bytes 163872 | tf_op jit(solution)/shard_map/ppermute | solution.py:481
  10.2 4.0 %collective-permute-start.3 = (f32[20,8,256]{2,1,0:T(8,128)S(1)}, f32[20,8,256]{2,1,0:T(8,128)S(1)}, u32[]{:S(2)}, u32[]{:S(2)}) collective-permute-start(f32[20,8,256]{2,1,0:T(8,128)S(1)} %join.1.a_ref), channel_id=1, source_target_pairs={{0,6},{2,4},{4,2},{6,0},{1,7},{3,5},{5,3},{7,1},{8,14},{10,12},{12... | collective-permute-start | bytes 491528 | tf_op jit(solution)/shard_map/ppermute | solution.py:483
  14.2 0.0 collective-permute-start.2
  14.2 0.7 %collective-permute-start.1 = (f32[20,8,256]{2,1,0:T(8,128)S(1)}, f32[20,8,256]{2,1,0:T(8,128)S(1)}, u32[]{:S(2)}, u32[]{:S(2)}) collective-permute-start(f32[20,8,256]{2,1,0:T(8,128)S(1)} %join.1.a_ref), channel_id=1, source_target_pairs={{0,2},{2,0},{4,6},{6,4},{1,3},{3,1},{5,7},{7,5},{8,10},{10,8},{12,... | collective-permute-start | bytes 491528 | tf_op jit(solution)/shard_map/ppermute | solution.py:483
  14.8 0.0 copy-done.5
  14.8 0.0 copy-done.4
  14.9 0.0 copy-done.1
  14.9 0.0 copy-done.2
  14.9 0.0 copy-done
  14.9 5.3 %diag.1 = (f32[6,128,2048]{2,1,0:T(8,128)S(1)}, bf16[128,2048]{1,0:T(8,128)(2,1)S(1)}, bf16[128,2048]{1,0:T(8,128)(2,1)S(1)}, bf16[16,2048]{1,0:T(8,128)(2,1)S(1...) custom-call(s32[1]{0:T(128)S(6)} %copy.15.live_ref, f32[8192,128]{1,0:T(8,128)S(1)} %bitcast.12, ...), custom_call_target="tpu_custom_call" | custom-call | flops 200000000 | bytes 12000000 | tf_op jit(solution)/shard_map/diag/pallas_call | solution.py:484
  20.2 1.0 %collective-permute-done.3.d_ref = f32[20,8,256]{2,1,0:T(8,128)S(1)} collective-permute-done((f32[20,8,256]{2,1,0:T(8,128)S(1)}, f32[20,8,256]{2,1,0:T(8,128)S(1)}, u32[]{:S(2)}, u32[]{:S(2)}) %collective-permute-start.3) | collective-permute-done | bytes 163872 | tf_op jit(solution)/shard_map/ppermute | solution.py:483
  21.2 0.0 collective-permute-done.2.c_ref
  21.2 1.1 %collective-permute-done.1.b_ref = f32[20,8,256]{2,1,0:T(8,128)S(1)} collective-permute-done((f32[20,8,256]{2,1,0:T(8,128)S(1)}, f32[20,8,256]{2,1,0:T(8,128)S(1)}, u32[]{:S(2)}, u32[]{:S(2)}) %collective-permute-start.1) | collective-permute-done | bytes 163872 | tf_op jit(solution)/shard_map/ppermute | solution.py:483
  22.3 0.1 solve.1.mine_ref
  22.5 1.3 %collective-permute-start.4 = (f32[5,8,256]{2,1,0:T(8,128)S(1)}, f32[5,8,256]{2,1,0:T(8,128)S(1)}, u32[]{:S(2)}, u32[]{:S(2)}) collective-permute-start(f32[5,8,256]{2,1,0:T(8,128)S(1)} %solve.1.mine_ref), channel_id=1, source_target_pairs={{0,1},{1,0},{2,3},{3,2},{4,5},{5,4},{6,7},{7,6},{8,9},{9,8},{10,11... | collective-permute-start | bytes 122888 | tf_op jit(solution)/shard_map/ppermute | solution.py:523
  23.8 0.9 %collective-permute-done.4.other_ref = f32[5,8,256]{2,1,0:T(8,128)S(1)} collective-permute-done((f32[5,8,256]{2,1,0:T(8,128)S(1)}, f32[5,8,256]{2,1,0:T(8,128)S(1)}, u32[]{:S(2)}, u32[]{:S(2)}) %collective-permute-start.4) | collective-permute-done | bytes 40992 | tf_op jit(solution)/shard_map/ppermute | solution.py:523
  24.6 0.0 copy-done.3
  24.6 4.9 %apply.1 = (f32[640,128]{1,0:T(8,128)S(1)}, f32[5,4096]{1,0:T(8,128)}) custom-call(f32[6,128,2048]{2,1,0:T(8,128)S(1)} %get-tuple-element.22.all_src_ref, f32[6,128,2048]{2,1,0:T(8,128)S(1)} %get-tuple-element.26.all_extra_ref, bf16[256,2048]{1,0:T(8,128)(2,1)S(1)} %get-tuple-element.27.src_low_ref, bf16[128,2048]{1,0:T(8,128)(2,1)S(1)} %get-tuple-element.28.seg_low_ref, ...), custom_call_target="tpu_custom_call" | custom-call | tf_op jit(solution)/shard_map/apply/pallas_call | solution.py:524
  29.5 20.5 %all_to_all.5 = f32[128,1,640]{2,1,0:T(1,128)S(1)} all-to-all(f32[128,1,640]{2,1,0:T(1,128)S(1)} %bitcast.15), channel_id=1, replica_groups=mesh['sky'=16,'tm'=4,'fov'=2] {'sky','tm','fov'}, dimensions={0} | all-to-all | bytes 655360 | tf_op jit(solution)/shard_map/all_to_all | solution.py:545
  50.0 0.1 attitude.1
  50.1 1.2 %collective-permute-start.5 = (f32[4,128]{1,0:T(4,128)S(1)}, f32[4,128]{1,0:T(4,128)S(1)}, u32[]{:S(2)}, u32[]{:S(2)}) collective-permute-start(f32[4,128]{1,0:T(4,128)S(1)} %attitude.1), channel_id=1, source_target_pairs={{0,1},{1,0},{2,3},{3,2},{4,5},{5,4},{6,7},{7,6},{8,9},{9,8},{10,11... | collective-permute-start | bytes 6152 | tf_op jit(solution)/shard_map/ppermute | solution.py:556
  51.3 1.4 %calibration.1 = f32[32,128]{1,0:T(8,128)} custom-call(f32[640,128]{1,0:T(8,128)S(1)} %bitcast.14), custom_call_target="tpu_custom_call" | custom-call | flops 100000000 | bytes 400000 | tf_op jit(solution)/shard_map/calibration/pallas_call | solution.py:557
  52.7 0.0 collective-permute-done.5
  52.7 0.6 %add.3 = f32[4,128]{1,0:T(4,128)} add(f32[4,128]{1,0:T(4,128)S(1)} %attitude.1, f32[4,128]{1,0:T(4,128)S(1)} %collective-permute-done.5) | non-fusion elementwise | flops 512 | bytes 6144 | tf_op jit(solution)/shard_map/add | solution.py:566
  (1 shorter events, 0.0 us)
Async XLA Ops:
  0.6 14.2 %copy-start.5 = (s32[2048]{0:T(1024)S(1)}, s32[2048]{0:T(1024)}, u32[]{:S(2)}) copy-start(s32[2048]{0:T(1024)} %param.16) | copy-start | bytes 24580
  0.6 14.2 %copy-start.4 = (s32[2048]{0:T(1024)S(1)}, s32[2048]{0:T(1024)}, u32[]{:S(2)}) copy-start(s32[2048]{0:T(1024)} %param.15) | copy-start | bytes 24580
  0.7 14.2 %copy-start.1 = (f32[2048,128]{1,0:T(8,128)S(1)}, f32[2048,128]{1,0:T(8,128)}, u32[]{:S(2)}) copy-start(f32[2048,128]{1,0:T(8,128)} %pha_ref.1) | copy-start | bytes 3145732
  0.7 14.2 %copy-start.2 = (f32[2048,128]{1,0:T(8,128)S(1)}, f32[2048,128]{1,0:T(8,128)}, u32[]{:S(2)}) copy-start(f32[2048,128]{1,0:T(8,128)} %cal_ref.1) | copy-start | bytes 3145732
  0.7 14.2 %copy-start = (f32[2048,4,128]{2,1,0:T(4,128)S(1)}, f32[2048,4,128]{2,1,0:T(4,128)}, u32[]{:S(2)}) copy-start(f32[2048,4,128]{2,1,0:T(4,128)} %param.10) | copy-start | bytes 12582916
  1.5 23.2 %copy-start.3 = (s32[2048]{0:T(1024)S(1)}, s32[2048]{0:T(1024)}, u32[]{:S(2)}) copy-start(s32[2048]{0:T(1024)} %param.14) | copy-start | bytes 24580
  7.7 2.5 %collective-permute-start = (f32[20,8,256]{2,1,0:T(8,128)S(1)}, f32[20,8,256]{2,1,0:T(8,128)S(1)}, u32[]{:S(2)}, u32[]{:S(2)}) collective-permute-start(f32[20,8,256]{2,1,0:T(8,128)S(1)} %get-tuple-element.24), channel_id=1, source_target_pairs={{0,1},{1,0},{2,3},{3,2},{4,5},{5,4},{6,7},{7,6},{8,9},{9,8},{10,11... | collective-permute-start | bytes 491528 | tf_op jit(solution)/shard_map/ppermute | solution.py:481
  10.2 11.0 %collective-permute-start.3 = (f32[20,8,256]{2,1,0:T(8,128)S(1)}, f32[20,8,256]{2,1,0:T(8,128)S(1)}, u32[]{:S(2)}, u32[]{:S(2)}) collective-permute-start(f32[20,8,256]{2,1,0:T(8,128)S(1)} %join.1.a_ref), channel_id=1, source_target_pairs={{0,6},{2,4},{4,2},{6,0},{1,7},{3,5},{5,3},{7,1},{8,14},{10,12},{12... | collective-permute-start | bytes 491528 | tf_op jit(solution)/shard_map/ppermute | solution.py:483
  14.2 7.0 %collective-permute-start.2 = (f32[20,8,256]{2,1,0:T(8,128)S(1)}, f32[20,8,256]{2,1,0:T(8,128)S(1)}, u32[]{:S(2)}, u32[]{:S(2)}) collective-permute-start(f32[20,8,256]{2,1,0:T(8,128)S(1)} %join.1.a_ref), channel_id=1, source_target_pairs={{0,4},{2,6},{4,0},{6,2},{1,5},{3,7},{5,1},{7,3},{8,12},{10,14},{12... | collective-permute-start | bytes 491528 | tf_op jit(solution)/shard_map/ppermute | solution.py:483
  14.2 8.1 %collective-permute-start.1 = (f32[20,8,256]{2,1,0:T(8,128)S(1)}, f32[20,8,256]{2,1,0:T(8,128)S(1)}, u32[]{:S(2)}, u32[]{:S(2)}) collective-permute-start(f32[20,8,256]{2,1,0:T(8,128)S(1)} %join.1.a_ref), channel_id=1, source_target_pairs={{0,2},{2,0},{4,6},{6,4},{1,3},{3,1},{5,7},{7,5},{8,10},{10,8},{12,... | collective-permute-start | bytes 491528 | tf_op jit(solution)/shard_map/ppermute | solution.py:483
  22.5 2.2 %collective-permute-start.4 = (f32[5,8,256]{2,1,0:T(8,128)S(1)}, f32[5,8,256]{2,1,0:T(8,128)S(1)}, u32[]{:S(2)}, u32[]{:S(2)}) collective-permute-start(f32[5,8,256]{2,1,0:T(8,128)S(1)} %solve.1.mine_ref), channel_id=1, source_target_pairs={{0,1},{1,0},{2,3},{3,2},{4,5},{5,4},{6,7},{7,6},{8,9},{9,8},{10,11... | collective-permute-start | bytes 122888 | tf_op jit(solution)/shard_map/ppermute | solution.py:523
  50.1 2.6 %collective-permute-start.5 = (f32[4,128]{1,0:T(4,128)S(1)}, f32[4,128]{1,0:T(4,128)S(1)}, u32[]{:S(2)}, u32[]{:S(2)}) collective-permute-start(f32[4,128]{1,0:T(4,128)S(1)} %attitude.1), channel_id=1, source_target_pairs={{0,1},{1,0},{2,3},{3,2},{4,5},{5,4},{6,7},{7,6},{8,9},{9,8},{10,11... | collective-permute-start | bytes 6152 | tf_op jit(solution)/shard_map/ppermute | solution.py:556

commit v6 on v5

--- a/solution.py
+++ b/solution.py
@@ -9,7 +9,7 @@
 CUT = 256
 WIDE = 512
 WIDE_STEPS = BLK // WIDE
-LONG = 1024
+LONG = 2048
 LONG_STEPS = BLK // LONG
 OBS = 128
 CAP = 32
@@ -146,13 +146,16 @@
     return m[3] * sixth
 
 
-def normals_kernel(live_ref, src_ref, res_ref, idx_ref, keep_ref, send_ref, all_src_ref, all_low_ref, acc_ref):
+def normals_kernel(live_ref, src_ref, res_ref, idx_ref, keep_ref, send_ref, all_src_ref, all_low_ref, acc_ref, left_ref):
     step = pl.program_id(0)
     span = columns(step, WIDE)
     srct_ref = all_src_ref.at[:, :, span]
     idx = idx_ref[0] ^ (lax.axis_index("fov") * 2048)
     live = live_row(live_ref, step, WIDE)
-    total = None
+    earlier = columns(jnp.maximum(step - 1, 0), WIDE)
+    product = repeated_dot(left_ref[...], all_low_ref[:, earlier], 3)
+    acc_ref[...] = jnp.where(step > 1, acc_ref[...], 0.0) + jnp.where(step > 0, product, 0.0)
+    sides = []
     for part in range(WIDE // CUT):
         cut = slice(part * CUT, (part + 1) * CUT)
         high = (rows_equal(16, idx[:, cut] >> 8) * live[:, cut]).astype(BF16)
@@ -174,15 +177,18 @@
             spare.append(sums[16:])
         both = fold(spare[0] + spare[1])
         blocks = [jnp.concatenate(groups, axis=1), jnp.concatenate([both[:4], both[4:]], axis=1)]
-        product = repeated_dot(masked_rows(high, blocks, 3), low, 3)
-        total = product if part == 0 else total + product
-    accumulate(acc_ref, total, step)
+        sides.append(masked_rows(high, blocks, 3))
+    left_ref[...] = jnp.concatenate(
+        [side[:, n * CUT : (n + 1) * CUT] for n in range(3) for side in sides], axis=1
+    )
 
     @pl.when(step == WIDE_STEPS - 1)
     def _():
+        last = repeated_dot(left_ref[...], all_low_ref[:, columns(step, WIDE)], 3)
         for k in range(20):
-            keep_ref[k] = acc_ref[k * 16 : k * 16 + 8]
-            send_ref[k] = acc_ref[k * 16 + 8 : k * 16 + 16]
+            row = k * 16
+            keep_ref[k] = acc_ref[row : row + 8] + last[row : row + 8]
+            send_ref[k] = acc_ref[row + 8 : row + 16] + last[row + 8 : row + 16]
 
 
 def shifted(rows, distance):
@@ -467,7 +473,7 @@
             pltpu.VMEM((6, OBS, BLK), F32),
             pltpu.VMEM((256, BLK), BF16),
         ],
-        scratch_shapes=[pltpu.VMEM((320, 256), F32)],
+        scratch_shapes=[pltpu.VMEM((320, 256), F32), pltpu.VMEM((320, 3 * WIDE), BF16)],
         compiler_params=sequential,
         name="normals",
     )(live_blocks, *off_chip(src, obs_residual, source))

time: 53.4 us -> 53.3 us (level)
  no operation moved by 1% of the time
where the time goes in v6:
time: 53.3 us; the launch traced here: 53.1 us
  blocking collectives  20.5 us (38%)
  Pallas kernels  17.9 us (34%)
  starting transfers between devices  8.56 us (16%)
  waiting for transfers between devices  4.02 us (8%)
  between operations  1.52 us (3%)
  other arithmetic  0.58 us (1%)
    all_to_all x1, blocking collectives, shards(): lax.all_to_all(outgoing.reshape(128, 1, PIECES * 128), ALL, split_axis=0,...  20.5 us
    pallas_call x1, Pallas kernels, shards(): pl.pallas_call(normals_kernel, grid=(WIDE_STEPS,), in_specs=[SMEM, pl.Blo...  6.29 us
    pallas_call x1, Pallas kernels, shards(): pl.pallas_call(diag_kernel, grid=(WIDE_STEPS,), in_specs=[SMEM, pl.BlockS...  5.33 us
    pallas_call x1, Pallas kernels, shards(): pl.pallas_call(apply_kernel, grid=(LONG_STEPS,), in_specs=[VMEM] * 7 + [L...  4.64 us
    ppermute x3, starting transfers between devices, shards(): lax.ppermute(half, 'tm', [(i, i ^ d) for i in range(4)])  4.62 us
    ppermute x3, waiting for transfers between devices, shards(): lax.ppermute(half, 'tm', [(i, i ^ d) for i in range(4)])  2.12 us
    ppermute x1, starting transfers between devices, shards(): lax.ppermute(send, 'fov', [(0, 1), (1, 0)])  1.46 us
    pallas_call x1, Pallas kernels, shards(): pl.pallas_call(calibration_kernel, in_specs=[VMEM], out_specs=VMEM, out_s...  1.43 us
  transfers between devices with their start and end apart: 6, of which 4 were waited for; matrix products, arithmetic and copies ran while one was open for 0% of the time, Pallas kernels for 13%

profile of v6, /device:TPU:1, one launch (start us, length us, event | category | flops | bytes accessed | tf_op | source)
XLA Modules:
  0.0 53.1 jit_solution(8199111007364121132)
XLA Ops:
  0.6 0.0 copy-start.5
  0.6 0.0 copy-start.4
  0.7 0.0 copy-start.1
  0.7 0.0 copy-start.2
  0.7 0.0 copy-start
  1.5 0.0 copy-start.3
  1.5 6.3 %normals.1 = (f32[20,8,256]{2,1,0:T(8,128)S(1)}, f32[20,8,256]{2,1,0:T(8,128)S(1)}, f32[6,128,2048]{2,1,0:T(8,128)S(1)}, bf16[256,2048]{1,0:T(8,128)(2,1)S(1)}) custom-call(s32[1]{0:T(128)S(6)} %copy.15.live_ref, f32[5,2048,128]{2,1,0:T(8,128)} %bitcast.20, f32[2048,128]{1,0:T(8,128)} %res_ref.1, s32[4,1,512]{2,1,0:T(1,128)} %bitcast.16), custom_call_target="tpu_custom_call" | custom-call | tf_op jit(solution)/shard_map/normals/pallas_call | solution.py:460
  7.8 1.5 %collective-permute-start = (f32[20,8,256]{2,1,0:T(8,128)S(1)}, f32[20,8,256]{2,1,0:T(8,128)S(1)}, u32[]{:S(2)}, u32[]{:S(2)}) collective-permute-start(f32[20,8,256]{2,1,0:T(8,128)S(1)} %get-tuple-element.24), channel_id=1, source_target_pairs={{0,1},{1,0},{2,3},{3,2},{4,5},{5,4},{6,7},{7,6},{8,9},{9,8},{10,11... | collective-permute-start | bytes 491528 | tf_op jit(solution)/shard_map/ppermute | solution.py:487
  9.2 1.0 %collective-permute-done.b_ref = f32[20,8,256]{2,1,0:T(8,128)S(1)} collective-permute-done((f32[20,8,256]{2,1,0:T(8,128)S(1)}, f32[20,8,256]{2,1,0:T(8,128)S(1)}, u32[]{:S(2)}, u32[]{:S(2)}) %collective-permute-start) | collective-permute-done | bytes 163872 | tf_op jit(solution)/shard_map/ppermute | solution.py:487
  10.3 4.0 %collective-permute-start.3 = (f32[20,8,256]{2,1,0:T(8,128)S(1)}, f32[20,8,256]{2,1,0:T(8,128)S(1)}, u32[]{:S(2)}, u32[]{:S(2)}) collective-permute-start(f32[20,8,256]{2,1,0:T(8,128)S(1)} %join.1.a_ref), channel_id=1, source_target_pairs={{0,6},{2,4},{4,2},{6,0},{1,7},{3,5},{5,3},{7,1},{8,14},{10,12},{12... | collective-permute-start | bytes 491528 | tf_op jit(solution)/shard_map/ppermute | solution.py:489
  14.2 0.0 collective-permute-start.2
  14.3 0.7 %collective-permute-start.1 = (f32[20,8,256]{2,1,0:T(8,128)S(1)}, f32[20,8,256]{2,1,0:T(8,128)S(1)}, u32[]{:S(2)}, u32[]{:S(2)}) collective-permute-start(f32[20,8,256]{2,1,0:T(8,128)S(1)} %join.1.a_ref), channel_id=1, source_target_pairs={{0,2},{2,0},{4,6},{6,4},{1,3},{3,1},{5,7},{7,5},{8,10},{10,8},{12,... | collective-permute-start | bytes 491528 | tf_op jit(solution)/shard_map/ppermute | solution.py:489
  14.9 0.0 copy-done.5
  14.9 0.0 copy-done.4
  14.9 0.0 copy-done.1
  14.9 0.0 copy-done.2
  14.9 0.0 copy-done
  14.9 5.3 %diag.1 = (f32[6,128,2048]{2,1,0:T(8,128)S(1)}, bf16[128,2048]{1,0:T(8,128)(2,1)S(1)}, bf16[128,2048]{1,0:T(8,128)(2,1)S(1)}, bf16[16,2048]{1,0:T(8,128)(2,1)S(1...) custom-call(s32[1]{0:T(128)S(6)} %copy.15.live_ref, f32[8192,128]{1,0:T(8,128)S(1)} %bitcast.12, ...), custom_call_target="tpu_custom_call" | custom-call | flops 200000000 | bytes 12000000 | tf_op jit(solution)/shard_map/diag/pallas_call | solution.py:490
  20.3 1.0 %collective-permute-done.3.d_ref = f32[20,8,256]{2,1,0:T(8,128)S(1)} collective-permute-done((f32[20,8,256]{2,1,0:T(8,128)S(1)}, f32[20,8,256]{2,1,0:T(8,128)S(1)}, u32[]{:S(2)}, u32[]{:S(2)}) %collective-permute-start.3) | collective-permute-done | bytes 163872 | tf_op jit(solution)/shard_map/ppermute | solution.py:489
  21.3 0.0 collective-permute-done.2.c_ref
  21.3 1.1 %collective-permute-done.1.b_ref = f32[20,8,256]{2,1,0:T(8,128)S(1)} collective-permute-done((f32[20,8,256]{2,1,0:T(8,128)S(1)}, f32[20,8,256]{2,1,0:T(8,128)S(1)}, u32[]{:S(2)}, u32[]{:S(2)}) %collective-permute-start.1) | collective-permute-done | bytes 163872 | tf_op jit(solution)/shard_map/ppermute | solution.py:489
  22.4 0.1 solve.1.mine_ref
  22.5 1.3 %collective-permute-start.4 = (f32[5,8,256]{2,1,0:T(8,128)S(1)}, f32[5,8,256]{2,1,0:T(8,128)S(1)}, u32[]{:S(2)}, u32[]{:S(2)}) collective-permute-start(f32[5,8,256]{2,1,0:T(8,128)S(1)} %solve.1.mine_ref), channel_id=1, source_target_pairs={{0,1},{1,0},{2,3},{3,2},{4,5},{5,4},{6,7},{7,6},{8,9},{9,8},{10,11... | collective-permute-start | bytes 122888 | tf_op jit(solution)/shard_map/ppermute | solution.py:529
  23.8 0.9 %collective-permute-done.4.other_ref = f32[5,8,256]{2,1,0:T(8,128)S(1)} collective-permute-done((f32[5,8,256]{2,1,0:T(8,128)S(1)}, f32[5,8,256]{2,1,0:T(8,128)S(1)}, u32[]{:S(2)}, u32[]{:S(2)}) %collective-permute-start.4) | collective-permute-done | bytes 40992 | tf_op jit(solution)/shard_map/ppermute | solution.py:529
  24.7 0.0 copy-done.3
  24.7 4.6 %apply.1 = (f32[640,128]{1,0:T(8,128)S(1)}, f32[5,4096]{1,0:T(8,128)}) custom-call(f32[6,128,2048]{2,1,0:T(8,128)S(1)} %get-tuple-element.22.all_src_ref, f32[6,128,2048]{2,1,0:T(8,128)S(1)} %get-tuple-element.26.all_extra_ref, bf16[256,2048]{1,0:T(8,128)(2,1)S(1)} %get-tuple-element.27.src_low_ref, bf16[128,2048]{1,0:T(8,128)(2,1)S(1)} %get-tuple-element.28.seg_low_ref, ...), custom_call_target="tpu_custom_call" | custom-call | tf_op jit(solution)/shard_map/apply/pallas_call | solution.py:530
  29.3 20.5 %all_to_all.5 = f32[128,1,640]{2,1,0:T(1,128)S(1)} all-to-all(f32[128,1,640]{2,1,0:T(1,128)S(1)} %bitcast.15), channel_id=1, replica_groups=mesh['sky'=16,'tm'=4,'fov'=2] {'sky','tm','fov'}, dimensions={0} | all-to-all | bytes 655360 | tf_op jit(solution)/shard_map/all_to_all | solution.py:551
  49.8 0.1 attitude.1
  49.9 1.2 %collective-permute-start.5 = (f32[4,128]{1,0:T(4,128)S(1)}, f32[4,128]{1,0:T(4,128)S(1)}, u32[]{:S(2)}, u32[]{:S(2)}) collective-permute-start(f32[4,128]{1,0:T(4,128)S(1)} %attitude.1), channel_id=1, source_target_pairs={{0,1},{1,0},{2,3},{3,2},{4,5},{5,4},{6,7},{7,6},{8,9},{9,8},{10,11... | collective-permute-start | bytes 6152 | tf_op jit(solution)/shard_map/ppermute | solution.py:562
  51.1 1.4 %calibration.1 = f32[32,128]{1,0:T(8,128)} custom-call(f32[640,128]{1,0:T(8,128)S(1)} %bitcast.14), custom_call_target="tpu_custom_call" | custom-call | flops 100000000 | bytes 400000 | tf_op jit(solution)/shard_map/calibration/pallas_call | solution.py:563
  52.5 0.0 collective-permute-done.5
  52.5 0.6 %add.3 = f32[4,128]{1,0:T(4,128)} add(f32[4,128]{1,0:T(4,128)S(1)} %attitude.1, f32[4,128]{1,0:T(4,128)S(1)} %collective-permute-done.5) | non-fusion elementwise | flops 512 | bytes 6144 | tf_op jit(solution)/shard_map/add | solution.py:572
  (1 shorter events, 0.0 us)
Async XLA Ops:
  0.6 14.3 %copy-start.5 = (s32[2048]{0:T(1024)S(1)}, s32[2048]{0:T(1024)}, u32[]{:S(2)}) copy-start(s32[2048]{0:T(1024)} %param.16) | copy-start | bytes 24580
  0.6 14.3 %copy-start.4 = (s32[2048]{0:T(1024)S(1)}, s32[2048]{0:T(1024)}, u32[]{:S(2)}) copy-start(s32[2048]{0:T(1024)} %param.15) | copy-start | bytes 24580
  0.7 14.3 %copy-start.1 = (f32[2048,128]{1,0:T(8,128)S(1)}, f32[2048,128]{1,0:T(8,128)}, u32[]{:S(2)}) copy-start(f32[2048,128]{1,0:T(8,128)} %pha_ref.1) | copy-start | bytes 3145732
  0.7 14.3 %copy-start.2 = (f32[2048,128]{1,0:T(8,128)S(1)}, f32[2048,128]{1,0:T(8,128)}, u32[]{:S(2)}) copy-start(f32[2048,128]{1,0:T(8,128)} %cal_ref.1) | copy-start | bytes 3145732
  0.7 14.3 %copy-start = (f32[2048,4,128]{2,1,0:T(4,128)S(1)}, f32[2048,4,128]{2,1,0:T(4,128)}, u32[]{:S(2)}) copy-start(f32[2048,4,128]{2,1,0:T(4,128)} %param.10) | copy-start | bytes 12582916
  1.5 23.2 %copy-start.3 = (s32[2048]{0:T(1024)S(1)}, s32[2048]{0:T(1024)}, u32[]{:S(2)}) copy-start(s32[2048]{0:T(1024)} %param.14) | copy-start | bytes 24580
  7.8 2.5 %collective-permute-start = (f32[20,8,256]{2,1,0:T(8,128)S(1)}, f32[20,8,256]{2,1,0:T(8,128)S(1)}, u32[]{:S(2)}, u32[]{:S(2)}) collective-permute-start(f32[20,8,256]{2,1,0:T(8,128)S(1)} %get-tuple-element.24), channel_id=1, source_target_pairs={{0,1},{1,0},{2,3},{3,2},{4,5},{5,4},{6,7},{7,6},{8,9},{9,8},{10,11... | collective-permute-start | bytes 491528 | tf_op jit(solution)/shard_map/ppermute | solution.py:487
  10.3 11.0 %collective-permute-start.3 = (f32[20,8,256]{2,1,0:T(8,128)S(1)}, f32[20,8,256]{2,1,0:T(8,128)S(1)}, u32[]{:S(2)}, u32[]{:S(2)}) collective-permute-start(f32[20,8,256]{2,1,0:T(8,128)S(1)} %join.1.a_ref), channel_id=1, source_target_pairs={{0,6},{2,4},{4,2},{6,0},{1,7},{3,5},{5,3},{7,1},{8,14},{10,12},{12... | collective-permute-start | bytes 491528 | tf_op jit(solution)/shard_map/ppermute | solution.py:489
  14.2 7.0 %collective-permute-start.2 = (f32[20,8,256]{2,1,0:T(8,128)S(1)}, f32[20,8,256]{2,1,0:T(8,128)S(1)}, u32[]{:S(2)}, u32[]{:S(2)}) collective-permute-start(f32[20,8,256]{2,1,0:T(8,128)S(1)} %join.1.a_ref), channel_id=1, source_target_pairs={{0,4},{2,6},{4,0},{6,2},{1,5},{3,7},{5,1},{7,3},{8,12},{10,14},{12... | collective-permute-start | bytes 491528 | tf_op jit(solution)/shard_map/ppermute | solution.py:489
  14.3 8.1 %collective-permute-start.1 = (f32[20,8,256]{2,1,0:T(8,128)S(1)}, f32[20,8,256]{2,1,0:T(8,128)S(1)}, u32[]{:S(2)}, u32[]{:S(2)}) collective-permute-start(f32[20,8,256]{2,1,0:T(8,128)S(1)} %join.1.a_ref), channel_id=1, source_target_pairs={{0,2},{2,0},{4,6},{6,4},{1,3},{3,1},{5,7},{7,5},{8,10},{10,8},{12,... | collective-permute-start | bytes 491528 | tf_op jit(solution)/shard_map/ppermute | solution.py:489
  22.5 2.2 %collective-permute-start.4 = (f32[5,8,256]{2,1,0:T(8,128)S(1)}, f32[5,8,256]{2,1,0:T(8,128)S(1)}, u32[]{:S(2)}, u32[]{:S(2)}) collective-permute-start(f32[5,8,256]{2,1,0:T(8,128)S(1)} %solve.1.mine_ref), channel_id=1, source_target_pairs={{0,1},{1,0},{2,3},{3,2},{4,5},{5,4},{6,7},{7,6},{8,9},{9,8},{10,11... | collective-permute-start | bytes 122888 | tf_op jit(solution)/shard_map/ppermute | solution.py:529
  49.9 2.6 %collective-permute-start.5 = (f32[4,128]{1,0:T(4,128)S(1)}, f32[4,128]{1,0:T(4,128)S(1)}, u32[]{:S(2)}, u32[]{:S(2)}) collective-permute-start(f32[4,128]{1,0:T(4,128)S(1)} %attitude.1), channel_id=1, source_target_pairs={{0,1},{1,0},{2,3},{3,2},{4,5},{5,4},{6,7},{7,6},{8,9},{9,8},{10,11... | collective-permute-start | bytes 6152 | tf_op jit(solution)/shard_map/ppermute | solution.py:562

commit v7 on v5

--- a/solution.py
+++ b/solution.py
@@ -7,9 +7,9 @@
 
 BLK = 2048
 CUT = 256
-WIDE = 512
+WIDE = 1024
 WIDE_STEPS = BLK // WIDE
-LONG = 1024
+LONG = 2048
 LONG_STEPS = BLK // LONG
 OBS = 128
 CAP = 32

time: 53.4 us -> 52.6 us (0.985)
  Pallas kernels: 18.1 us -> 16.7 us
  waiting for transfers between devices: 4.02 us -> 4.64 us
    pallas_call x1, Pallas kernels: 5.33 us -> 4.71 us  [shards(): pl.pallas_call(diag_kernel, grid=(WIDE_STEPS,), in_specs=[SMEM, pl.BlockS...]
    ppermute x3, waiting for transfers between devices: 2.12 us -> 2.74 us  [shards(): lax.ppermute(half, 'tm', [(i, i ^ d) for i in range(4)])]
    pallas_call x1, Pallas kernels: 6.21 us -> 5.66 us  [shards(): pl.pallas_call(normals_kernel, grid=(WIDE_STEPS,), in_specs=[SMEM, pl.Blo...]
  transfers between devices with their start and end apart: 6 -> 6, of which waited for: 4 -> 4; matrix products, arithmetic and copies ran while one was open for 0% -> 0% of each run, Pallas kernels for 13% -> 12%
where the time goes in v7:
time: 52.6 us; the launch traced here: 52.5 us
  blocking collectives  20.5 us (39%)
  Pallas kernels  16.7 us (32%)
  starting transfers between devices  8.57 us (16%)
  waiting for transfers between devices  4.64 us (9%)
  between operations  1.52 us (3%)
  other arithmetic  0.58 us (1%)
    all_to_all x1, blocking collectives, shards(): lax.all_to_all(outgoing.reshape(128, 1, PIECES * 128), ALL, split_axis=0,...  20.5 us
    pallas_call x1, Pallas kernels, shards(): pl.pallas_call(normals_kernel, grid=(WIDE_STEPS,), in_specs=[SMEM, pl.Blo...  5.66 us
    pallas_call x1, Pallas kernels, shards(): pl.pallas_call(diag_kernel, grid=(WIDE_STEPS,), in_specs=[SMEM, pl.BlockS...  4.71 us
    pallas_call x1, Pallas kernels, shards(): pl.pallas_call(apply_kernel, grid=(LONG_STEPS,), in_specs=[VMEM] * 7 + [L...  4.63 us
    ppermute x3, starting transfers between devices, shards(): lax.ppermute(half, 'tm', [(i, i ^ d) for i in range(4)])  4.62 us
    ppermute x3, waiting for transfers between devices, shards(): lax.ppermute(half, 'tm', [(i, i ^ d) for i in range(4)])  2.74 us
    ppermute x1, starting transfers between devices, shards(): lax.ppermute(send, 'fov', [(0, 1), (1, 0)])  1.46 us
    pallas_call x1, Pallas kernels, shards(): pl.pallas_call(calibration_kernel, in_specs=[VMEM], out_specs=VMEM, out_s...  1.43 us
  transfers between devices with their start and end apart: 6, of which 4 were waited for; matrix products, arithmetic and copies ran while one was open for 0% of the time, Pallas kernels for 12%

profile of v7, /device:TPU:1, one launch (start us, length us, event | category | flops | bytes accessed | tf_op | source)
XLA Modules:
  0.0 52.5 jit_solution(10441578726433807304)
XLA Ops:
  0.6 0.0 copy-start.5
  0.6 0.0 copy-start.4
  0.7 0.0 copy-start.1
  0.7 0.0 copy-start.2
  0.7 0.0 copy-start
  1.5 0.0 copy-start.3
  1.5 5.7 %normals.1 = (f32[20,8,256]{2,1,0:T(8,128)S(1)}, f32[20,8,256]{2,1,0:T(8,128)S(1)}, f32[6,128,2048]{2,1,0:T(8,128)S(1)}, bf16[256,2048]{1,0:T(8,128)(2,1)S(1)}) custom-call(s32[1]{0:T(128)S(6)} %copy.15.live_ref, f32[5,2048,128]{2,1,0:T(8,128)} %bitcast.20, f32[2048,128]{1,0:T(8,128)} %res_ref.1, s32[2,1,1024]{2,1,0:T(1,128)} %bitcast.16), custom_call_target="tpu_custom_call" | custom-call | tf_op jit(solution)/shard_map/normals/pallas_call | solution.py:454
  7.2 1.5 %collective-permute-start = (f32[20,8,256]{2,1,0:T(8,128)S(1)}, f32[20,8,256]{2,1,0:T(8,128)S(1)}, u32[]{:S(2)}, u32[]{:S(2)}) collective-permute-start(f32[20,8,256]{2,1,0:T(8,128)S(1)} %get-tuple-element.24), channel_id=1, source_target_pairs={{0,1},{1,0},{2,3},{3,2},{4,5},{5,4},{6,7},{7,6},{8,9},{9,8},{10,11... | collective-permute-start | bytes 491528 | tf_op jit(solution)/shard_map/ppermute | solution.py:481
  8.6 1.0 %collective-permute-done.b_ref = f32[20,8,256]{2,1,0:T(8,128)S(1)} collective-permute-done((f32[20,8,256]{2,1,0:T(8,128)S(1)}, f32[20,8,256]{2,1,0:T(8,128)S(1)}, u32[]{:S(2)}, u32[]{:S(2)}) %collective-permute-start) | collective-permute-done | bytes 163872 | tf_op jit(solution)/shard_map/ppermute | solution.py:481
  9.7 4.0 %collective-permute-start.3 = (f32[20,8,256]{2,1,0:T(8,128)S(1)}, f32[20,8,256]{2,1,0:T(8,128)S(1)}, u32[]{:S(2)}, u32[]{:S(2)}) collective-permute-start(f32[20,8,256]{2,1,0:T(8,128)S(1)} %join.1.a_ref), channel_id=1, source_target_pairs={{0,6},{2,4},{4,2},{6,0},{1,7},{3,5},{5,3},{7,1},{8,14},{10,12},{12... | collective-permute-start | bytes 491528 | tf_op jit(solution)/shard_map/ppermute | solution.py:483
  13.6 0.0 collective-permute-start.2
  13.6 0.7 %collective-permute-start.1 = (f32[20,8,256]{2,1,0:T(8,128)S(1)}, f32[20,8,256]{2,1,0:T(8,128)S(1)}, u32[]{:S(2)}, u32[]{:S(2)}) collective-permute-start(f32[20,8,256]{2,1,0:T(8,128)S(1)} %join.1.a_ref), channel_id=1, source_target_pairs={{0,2},{2,0},{4,6},{6,4},{1,3},{3,1},{5,7},{7,5},{8,10},{10,8},{12,... | collective-permute-start | bytes 491528 | tf_op jit(solution)/shard_map/ppermute | solution.py:483
  14.3 0.0 copy-done.5
  14.3 0.0 copy-done.4
  14.3 0.0 copy-done.1
  14.3 0.0 copy-done.2
  14.3 0.0 copy-done
  14.3 4.7 %diag.1 = (f32[6,128,2048]{2,1,0:T(8,128)S(1)}, bf16[128,2048]{1,0:T(8,128)(2,1)S(1)}, bf16[128,2048]{1,0:T(8,128)(2,1)S(1)}, bf16[16,2048]{1,0:T(8,128)(2,1)S(1...) custom-call(s32[1]{0:T(128)S(6)} %copy.15.live_ref, f32[8192,128]{1,0:T(8,128)S(1)} %bitcast.12, ...), custom_call_target="tpu_custom_call" | custom-call | flops 200000000 | bytes 12000000 | tf_op jit(solution)/shard_map/diag/pallas_call | solution.py:484
  19.0 1.6 %collective-permute-done.3.d_ref = f32[20,8,256]{2,1,0:T(8,128)S(1)} collective-permute-done((f32[20,8,256]{2,1,0:T(8,128)S(1)}, f32[20,8,256]{2,1,0:T(8,128)S(1)}, u32[]{:S(2)}, u32[]{:S(2)}) %collective-permute-start.3) | collective-permute-done | bytes 163872 | tf_op jit(solution)/shard_map/ppermute | solution.py:483
  20.7 0.0 collective-permute-done.2.c_ref
  20.7 1.1 %collective-permute-done.1.b_ref = f32[20,8,256]{2,1,0:T(8,128)S(1)} collective-permute-done((f32[20,8,256]{2,1,0:T(8,128)S(1)}, f32[20,8,256]{2,1,0:T(8,128)S(1)}, u32[]{:S(2)}, u32[]{:S(2)}) %collective-permute-start.1) | collective-permute-done | bytes 163872 | tf_op jit(solution)/shard_map/ppermute | solution.py:483
  21.8 0.1 solve.1.mine_ref
  21.9 1.3 %collective-permute-start.4 = (f32[5,8,256]{2,1,0:T(8,128)S(1)}, f32[5,8,256]{2,1,0:T(8,128)S(1)}, u32[]{:S(2)}, u32[]{:S(2)}) collective-permute-start(f32[5,8,256]{2,1,0:T(8,128)S(1)} %solve.1.mine_ref), channel_id=1, source_target_pairs={{0,1},{1,0},{2,3},{3,2},{4,5},{5,4},{6,7},{7,6},{8,9},{9,8},{10,11... | collective-permute-start | bytes 122888 | tf_op jit(solution)/shard_map/ppermute | solution.py:523
  23.2 0.9 %collective-permute-done.4.other_ref = f32[5,8,256]{2,1,0:T(8,128)S(1)} collective-permute-done((f32[5,8,256]{2,1,0:T(8,128)S(1)}, f32[5,8,256]{2,1,0:T(8,128)S(1)}, u32[]{:S(2)}, u32[]{:S(2)}) %collective-permute-start.4) | collective-permute-done | bytes 40992 | tf_op jit(solution)/shard_map/ppermute | solution.py:523
  24.1 0.0 copy-done.3
  24.1 4.6 %apply.1 = (f32[640,128]{1,0:T(8,128)S(1)}, f32[5,4096]{1,0:T(8,128)}) custom-call(f32[6,128,2048]{2,1,0:T(8,128)S(1)} %get-tuple-element.22.all_src_ref, f32[6,128,2048]{2,1,0:T(8,128)S(1)} %get-tuple-element.26.all_extra_ref, bf16[256,2048]{1,0:T(8,128)(2,1)S(1)} %get-tuple-element.27.src_low_ref, bf16[128,2048]{1,0:T(8,128)(2,1)S(1)} %get-tuple-element.28.seg_low_ref, ...), custom_call_target="tpu_custom_call" | custom-call | tf_op jit(solution)/shard_map/apply/pallas_call | solution.py:524
  28.7 20.5 %all_to_all.5 = f32[128,1,640]{2,1,0:T(1,128)S(1)} all-to-all(f32[128,1,640]{2,1,0:T(1,128)S(1)} %bitcast.15), channel_id=1, replica_groups=mesh['sky'=16,'tm'=4,'fov'=2] {'sky','tm','fov'}, dimensions={0} | all-to-all | bytes 655360 | tf_op jit(solution)/shard_map/all_to_all | solution.py:545
  49.2 0.1 attitude.1
  49.3 1.2 %collective-permute-start.5 = (f32[4,128]{1,0:T(4,128)S(1)}, f32[4,128]{1,0:T(4,128)S(1)}, u32[]{:S(2)}, u32[]{:S(2)}) collective-permute-start(f32[4,128]{1,0:T(4,128)S(1)} %attitude.1), channel_id=1, source_target_pairs={{0,1},{1,0},{2,3},{3,2},{4,5},{5,4},{6,7},{7,6},{8,9},{9,8},{10,11... | collective-permute-start | bytes 6152 | tf_op jit(solution)/shard_map/ppermute | solution.py:556
  50.5 1.4 %calibration.1 = f32[32,128]{1,0:T(8,128)} custom-call(f32[640,128]{1,0:T(8,128)S(1)} %bitcast.14), custom_call_target="tpu_custom_call" | custom-call | flops 100000000 | bytes 400000 | tf_op jit(solution)/shard_map/calibration/pallas_call | solution.py:557
  51.9 0.0 collective-permute-done.5
  51.9 0.6 %add.3 = f32[4,128]{1,0:T(4,128)} add(f32[4,128]{1,0:T(4,128)S(1)} %attitude.1, f32[4,128]{1,0:T(4,128)S(1)} %collective-permute-done.5) | non-fusion elementwise | flops 512 | bytes 6144 | tf_op jit(solution)/shard_map/add | solution.py:566
  (1 shorter events, 0.0 us)
Async XLA Ops:
  0.6 13.7 %copy-start.5 = (s32[2048]{0:T(1024)S(1)}, s32[2048]{0:T(1024)}, u32[]{:S(2)}) copy-start(s32[2048]{0:T(1024)} %param.16) | copy-start | bytes 24580
  0.6 13.7 %copy-start.4 = (s32[2048]{0:T(1024)S(1)}, s32[2048]{0:T(1024)}, u32[]{:S(2)}) copy-start(s32[2048]{0:T(1024)} %param.15) | copy-start | bytes 24580
  0.7 13.6 %copy-start.1 = (f32[2048,128]{1,0:T(8,128)S(1)}, f32[2048,128]{1,0:T(8,128)}, u32[]{:S(2)}) copy-start(f32[2048,128]{1,0:T(8,128)} %pha_ref.1) | copy-start | bytes 3145732
  0.7 13.6 %copy-start.2 = (f32[2048,128]{1,0:T(8,128)S(1)}, f32[2048,128]{1,0:T(8,128)}, u32[]{:S(2)}) copy-start(f32[2048,128]{1,0:T(8,128)} %cal_ref.1) | copy-start | bytes 3145732
  0.7 13.6 %copy-start = (f32[2048,4,128]{2,1,0:T(4,128)S(1)}, f32[2048,4,128]{2,1,0:T(4,128)}, u32[]{:S(2)}) copy-start(f32[2048,4,128]{2,1,0:T(4,128)} %param.10) | copy-start | bytes 12582916
  1.5 22.6 %copy-start.3 = (s32[2048]{0:T(1024)S(1)}, s32[2048]{0:T(1024)}, u32[]{:S(2)}) copy-start(s32[2048]{0:T(1024)} %param.14) | copy-start | bytes 24580
  7.2 2.5 %collective-permute-start = (f32[20,8,256]{2,1,0:T(8,128)S(1)}, f32[20,8,256]{2,1,0:T(8,128)S(1)}, u32[]{:S(2)}, u32[]{:S(2)}) collective-permute-start(f32[20,8,256]{2,1,0:T(8,128)S(1)} %get-tuple-element.24), channel_id=1, source_target_pairs={{0,1},{1,0},{2,3},{3,2},{4,5},{5,4},{6,7},{7,6},{8,9},{9,8},{10,11... | collective-permute-start | bytes 491528 | tf_op jit(solution)/shard_map/ppermute | solution.py:481
  9.7 11.0 %collective-permute-start.3 = (f32[20,8,256]{2,1,0:T(8,128)S(1)}, f32[20,8,256]{2,1,0:T(8,128)S(1)}, u32[]{:S(2)}, u32[]{:S(2)}) collective-permute-start(f32[20,8,256]{2,1,0:T(8,128)S(1)} %join.1.a_ref), channel_id=1, source_target_pairs={{0,6},{2,4},{4,2},{6,0},{1,7},{3,5},{5,3},{7,1},{8,14},{10,12},{12... | collective-permute-start | bytes 491528 | tf_op jit(solution)/shard_map/ppermute | solution.py:483
  13.6 7.0 %collective-permute-start.2 = (f32[20,8,256]{2,1,0:T(8,128)S(1)}, f32[20,8,256]{2,1,0:T(8,128)S(1)}, u32[]{:S(2)}, u32[]{:S(2)}) collective-permute-start(f32[20,8,256]{2,1,0:T(8,128)S(1)} %join.1.a_ref), channel_id=1, source_target_pairs={{0,4},{2,6},{4,0},{6,2},{1,5},{3,7},{5,1},{7,3},{8,12},{10,14},{12... | collective-permute-start | bytes 491528 | tf_op jit(solution)/shard_map/ppermute | solution.py:483
  13.6 8.1 %collective-permute-start.1 = (f32[20,8,256]{2,1,0:T(8,128)S(1)}, f32[20,8,256]{2,1,0:T(8,128)S(1)}, u32[]{:S(2)}, u32[]{:S(2)}) collective-permute-start(f32[20,8,256]{2,1,0:T(8,128)S(1)} %join.1.a_ref), channel_id=1, source_target_pairs={{0,2},{2,0},{4,6},{6,4},{1,3},{3,1},{5,7},{7,5},{8,10},{10,8},{12,... | collective-permute-start | bytes 491528 | tf_op jit(solution)/shard_map/ppermute | solution.py:483
  21.9 2.2 %collective-permute-start.4 = (f32[5,8,256]{2,1,0:T(8,128)S(1)}, f32[5,8,256]{2,1,0:T(8,128)S(1)}, u32[]{:S(2)}, u32[]{:S(2)}) collective-permute-start(f32[5,8,256]{2,1,0:T(8,128)S(1)} %solve.1.mine_ref), channel_id=1, source_target_pairs={{0,1},{1,0},{2,3},{3,2},{4,5},{5,4},{6,7},{7,6},{8,9},{9,8},{10,11... | collective-permute-start | bytes 122888 | tf_op jit(solution)/shard_map/ppermute | solution.py:523
  49.3 2.6 %collective-permute-start.5 = (f32[4,128]{1,0:T(4,128)S(1)}, f32[4,128]{1,0:T(4,128)S(1)}, u32[]{:S(2)}, u32[]{:S(2)}) collective-permute-start(f32[4,128]{1,0:T(4,128)S(1)} %attitude.1), channel_id=1, source_target_pairs={{0,1},{1,0},{2,3},{3,2},{4,5},{5,4},{6,7},{7,6},{8,9},{9,8},{10,11... | collective-permute-start | bytes 6152 | tf_op jit(solution)/shard_map/ppermute | solution.py:556
